TPU v7x, 512 devices: a whole 4x4x16 slice. The times are simulated.
512 devices in a mesh: rep: 32 (over z, core), exp: 16 (over y, x).
Axes of the slice: x: 4, y: 4, z: 16, core: 2. Of those that a mesh axis runs over, the one named last changes fastest.
Arguments:
- tokens: bfloat16 [65536, 4096], P(('rep', 'exp')), may hold values from -6 to 6
- grad_out: bfloat16 [65536, 4096], P(('rep', 'exp')), may hold values from -6 to 6
- gates: float32 [65536, 2], P(('rep', 'exp')), may hold values from 0.1 to 0.9
- expert_ids: int32 [65536, 2], P(('rep', 'exp')), may hold values from 0 to 15, all different within a row; in each aligned block of 128 rows (0 to 127, 128 to 255, ...) at most 20 rows name the same one
- w_all: bfloat16 [16, 4096, 384], P('exp', 'rep'), may hold values from -0.09375 to 0.09375
- touched: int32 [32, 16, 32], P('rep', 'exp'), may hold values 0 or 1
Outputs:
- token_grad: bfloat16 [65536, 4096], P(('rep', 'exp'))
- weight_grad: float32 [16, 4096, 384], P('exp', 'rep')
Inputs may be any that keep to these rules, and one draw needn't show every extreme that they name: `expert_ids`: each token names two different experts. Among the tokens of one device no expert is named more than 20 times, a bound that some block reaches.
All inputs are finite; a program needn't handle non-finite values. No bound on the sum of `touched` on one device may be relied on, other than what follows from the above.
Results may differ from a plain program's by a relative error of at most 0.017.
Values may be sent and summed in bfloat16 or wider, within the bound.
No kernel may reach another device: no remote copies, remote signals or barrier semaphores. Data moves between devices by JAX's collectives and lax.ppermute only.
A program may use at most 64 MiB of HBM per device.

v0:
```python
import functools

import jax
import jax.numpy as jnp
from jax import lax
from jax.experimental import pallas as pl
from jax.experimental.pallas import tpu as pltpu
from jax.sharding import PartitionSpec as P


BF16 = jnp.bfloat16
F32 = jnp.float32
TOK, WIDTH, EXPERTS, CAP, HID = 128, 4096, 16, 20, 128
HALF = WIDTH // 2
ROWS = 2 * EXPERTS * CAP
STEPS = 4
COLS = HALF // STEPS
BLOCKS = WIDTH // 128


def half_of_row(shape, axis):
    row = lax.broadcasted_iota(jnp.int32, shape, axis)
    group = (row * 1639) >> 16
    rest = row - group * (2 * CAP)
    upper = rest >= CAP
    return upper, group * CAP + jnp.where(upper, rest - CAP, rest)


def targets(ids):
    expert = lax.broadcasted_iota(jnp.int32, (EXPERTS, TOK), 0)
    first = (jnp.broadcast_to(ids[0:1, :], (EXPERTS, TOK)) == expert).astype(F32)
    second = (jnp.broadcast_to(ids[1:2, :], (EXPERTS, TOK)) == expert).astype(F32)
    earlier = lax.broadcasted_iota(jnp.int32, (TOK, TOK), 0) < lax.broadcasted_iota(
        jnp.int32, (TOK, TOK), 1
    )
    before = jnp.dot(
        (first + second).astype(BF16),
        earlier.astype(F32).astype(BF16),
        preferred_element_type=F32,
    )
    rank0 = jnp.sum(first * before, 0, keepdims=True).astype(jnp.int32)
    rank1 = jnp.sum(second * before, 0, keepdims=True).astype(jnp.int32)
    return ids[0:1, :] * CAP + rank0, ids[1:2, :] * CAP + rank1


def hits(ids):
    target0, target1 = targets(ids)
    upper, slot = half_of_row((ROWS, TOK), 0)
    hit0 = slot == jnp.broadcast_to(target0, (ROWS, TOK))
    hit1 = slot == jnp.broadcast_to(target1, (ROWS, TOK))
    return hit0, hit1, upper


def placement(hit0, hit1, upper):
    hit = jnp.where(hit0 | hit1, 1.0, 0.0)
    return jnp.concatenate([jnp.where(upper, 0.0, hit), jnp.where(upper, hit, 0.0)], 1)


def place_kernel(
    ids_ref, gates_ref, x_low_ref, x_high_ref, dy_low_ref, dy_high_ref, out_ref, place, gate
):
    step = pl.program_id(0)

    @pl.when(step == 0)
    def _():
        place[...] = placement(*hits(ids_ref[...])).astype(BF16)

    @pl.when(step < STEPS)
    def _():
        both = jnp.concatenate([x_low_ref[...], x_high_ref[...]], 0)
        out_ref[...] = jnp.dot(place[...], both, preferred_element_type=F32).astype(BF16)

    @pl.when(step == STEPS)
    def _():
        hit0, hit1, _ = hits(ids_ref[...])
        gates = gates_ref[...]
        weight = jnp.where(hit0, jnp.broadcast_to(gates[0:1, :], (ROWS, TOK)), 0.0) + jnp.where(
            hit1, jnp.broadcast_to(gates[1:2, :], (ROWS, TOK)), 0.0
        )
        gate[...] = jnp.broadcast_to(jnp.sum(weight, 1, keepdims=True), (ROWS, 128))

    @pl.when(step >= STEPS)
    def _():
        both = jnp.concatenate([dy_low_ref[...], dy_high_ref[...]], 0)
        picked = jnp.dot(place[...], both, preferred_element_type=F32)
        scale = gate[...]
        for i in range(COLS // 128):
            part = picked[:, i * 128 : i * 128 + 128] * scale
            out_ref[:, i * 128 : i * 128 + 128] = part.astype(BF16)


def back_kernel(ids_ref, back_ref):
    back_ref[...] = placement(*hits(ids_ref[...])).T.astype(BF16)


def join_halves(acc, width):
    upper, _ = half_of_row((ROWS, width), 0)
    own = jnp.where(upper, acc[:, width:], acc[:, :width])
    other = jnp.where(upper, pltpu.roll(own, CAP, 0), pltpu.roll(own, ROWS - CAP, 0))
    return own + other


def stack_rows(table_ref, weights, step, h, start, stop):
    first = 4 * step + BLOCKS // 2 * h
    return jnp.concatenate([weights[table_ref[first + j], :, start:stop] for j in range(4)], 0)


def piece_copies(pieces, weights, sems):
    copies, at = [], 0
    for i, piece in enumerate(pieces):
        span = piece.shape[0]
        copies.append(pltpu.make_async_copy(piece, weights.at[pl.ds(at, span)], sems.at[i]))
        at += span
    return copies


def column_copy(recv_ref, slots, sems, i):
    at = pl.ds(pl.multiple_of(i * COLS, COLS), COLS)
    return pltpu.make_async_copy(recv_ref.at[:, at], slots.at[:, at], sems.at[i])


def expert_kernel(table_ref, info_ref, recv_ref, *refs):
    gathered, both_ref, pieces = refs[:5], refs[5], refs[6:11]
    slots, weights, turned_ref, gate_up, down, sems, w_sems = refs[11:]
    step = pl.program_id(0)

    @pl.when(step == 0)
    def _():
        copies = piece_copies(gathered, weights, w_sems)
        for copy in copies:
            copy.start()
        for i in range(2 * STEPS):
            column_copy(recv_ref, slots, sems, i).start()
        gate_up[...] = jnp.zeros_like(gate_up)
        down[...] = jnp.zeros_like(down)
        for copy in copies:
            copy.wait()

    @pl.when(step < 2 * STEPS)
    def _():
        column_copy(recv_ref, slots, sems, step).wait()

    @pl.when(step < STEPS)
    def _():
        x = slots[:, pl.ds(pl.multiple_of(step * COLS, COLS), COLS)]
        for h in range(2):
            gate_up[:, 2 * HID * h : 2 * HID * (h + 1)] += jnp.dot(
                x,
                stack_rows(table_ref, weights, step, h, 0, 2 * HID),
                preferred_element_type=F32,
            )

    @pl.when((step >= STEPS) & (step < 2 * STEPS))
    def _():
        dy = slots[:, pl.ds(pl.multiple_of(step * COLS, COLS), COLS)]
        w_down = [
            stack_rows(table_ref, weights, step - STEPS, h, 2 * HID, 3 * HID) for h in range(2)
        ]
        down[...] += jnp.dot(dy, jnp.concatenate(w_down, 1), preferred_element_type=F32)

    @pl.when(step == 2 * STEPS - 1)
    def _():
        joined = join_halves(gate_up[...], 2 * HID)
        hid_grad = join_halves(down[...], HID)
        gate_pre = joined[:, :HID]
        up_pre = joined[:, HID:]
        sigmoid_g = jax.nn.sigmoid(gate_pre)
        silu_val = gate_pre * sigmoid_g
        silu_slope = sigmoid_g * (1.0 + gate_pre * (1.0 - sigmoid_g))
        gate_grad = hid_grad * up_pre * silu_slope
        up_grad = hid_grad * silu_val
        hidden = silu_val * up_pre
        both_ref[:, :HID] = gate_grad.astype(BF16)
        both_ref[:, HID:] = up_grad.astype(BF16)
        upper, _ = half_of_row((HID, ROWS), 1)
        for i, value in enumerate((gate_grad, up_grad, hidden)):
            turned = value.T
            turned_ref[i * HID : (i + 1) * HID, :] = jnp.where(upper, 0.0, turned).astype(BF16)
            turned_ref[(i + 3) * HID : (i + 4) * HID, :] = jnp.where(upper, turned, 0.0).astype(
                BF16
            )

    @pl.when(step >= 2 * STEPS)
    def _():
        weight_grad(info_ref, step - 2 * STEPS, slots, turned_ref, pieces)


def weight_grad(info_ref, step, slots, turned_ref, pieces):
    at = pl.multiple_of(step * COLS, COLS)
    x = slots[:, pl.ds(at, COLS)]
    dy = slots[:, pl.ds(pl.multiple_of(at + HALF, COLS), COLS)]
    spans = tuple(zip(pieces, (0, 7, 15, 17, 24), (7, 15, 17, 24, 32)))
    for h in range(2):
        base = 3 * HID * h
        proj = jnp.dot(turned_ref[base : base + 2 * HID, :], x, preferred_element_type=F32)
        down = jnp.dot(
            turned_ref[base + 2 * HID : base + 3 * HID, :], dy, preferred_element_type=F32
        )
        for i in range(COLS // 128):
            block = step * (COLS // 128) + i + h * (BLOCKS // 2)
            keep = info_ref[block].astype(F32)
            place = info_ref[BLOCKS + block]
            top = (proj[:, i * 128 : i * 128 + 128] * keep).astype(BF16)
            bottom = (down[:, i * 128 : i * 128 + 128] * keep).astype(BF16)

            def put(ref, first):
                ref[place - first, : 2 * HID, :] = top
                ref[place - first, 2 * HID :, :] = bottom

            for ref, first, last in spans:
                pl.when((place >= first) & (place < last))(functools.partial(put, ref, first))


def slot_grad_kernel(table_ref, both_ref, *refs):
    gathered, (out_ref, weights, w_sems) = refs[:5], refs[5:]
    step = pl.program_id(0)

    @pl.when(step == 0)
    def _():
        copies = piece_copies(gathered, weights, w_sems)
        for copy in copies:
            copy.start()
        for copy in copies:
            copy.wait()

    both = both_ref[...]
    upper, _ = half_of_row((ROWS, 2 * HID), 0)
    zero = jnp.zeros_like(both)
    total = None
    for h in range(2):
        own = jnp.where(upper, both, zero) if h else jnp.where(upper, zero, both)
        part = lax.dot_general(
            own,
            stack_rows(table_ref, weights, step, h, 0, 2 * HID),
            (((1,), (1,)), ((), ())),
            preferred_element_type=F32,
        )
        total = part if total is None else total + part
    out_ref[...] = total.astype(BF16)


def combine_kernel(back_ref, slots_ref, out_ref):
    step = pl.program_id(0)
    total = jnp.dot(back_ref[...], slots_ref[...], preferred_element_type=F32).astype(BF16)
    at = pl.multiple_of(step * COLS, COLS)
    out_ref[:, pl.ds(at, COLS)] = total[:TOK, :]
    out_ref[:, pl.ds(pl.multiple_of(at + HALF, COLS), COLS)] = total[TOK:, :]


def whole(shape):
    return pl.BlockSpec(shape, lambda i, *_: (0,) * len(shape))


def columns(rows, at=lambda i: i):
    return pl.BlockSpec((rows, COLS), lambda i, *_: (0, at(i)))


def call(kernel, steps, ins, outs, shapes, flops, nbytes, scratch=(), prefetch=0):
    return pl.pallas_call(
        kernel,
        grid_spec=pltpu.PrefetchScalarGridSpec(
            num_scalar_prefetch=prefetch,
            grid=(steps,),
            in_specs=ins,
            out_specs=outs,
            scratch_shapes=list(scratch),
        ),
        out_shape=shapes,
        compiler_params=pltpu.CompilerParams(dimension_semantics=("arbitrary",)),
        cost_estimate=pl.CostEstimate(flops=flops, bytes_accessed=nbytes, transcendentals=0),
    )


def sds(shape, dtype):
    return jax.ShapeDtypeStruct(shape, dtype)


def exchange(rows):
    return lax.all_to_all(
        rows.reshape(EXPERTS, 2 * CAP, -1), "exp", split_axis=0, concat_axis=0, tiled=True
    ).reshape(rows.shape)


def hop(value, distance):
    reps = lax.axis_size("rep")
    turn = [
        (i, (i + 2 * distance) % reps if i % 2 == 0 else (i - 2 * distance) % reps)
        for i in range(reps)
    ]
    return lax.ppermute(value, "rep", turn)


def swap(value):
    return lax.ppermute(value, "rep", [(i, i ^ 1) for i in range(lax.axis_size("rep"))])


def places(rep, sign):
    block = jnp.arange(BLOCKS, dtype=jnp.int32)
    core = rep & 1
    kind = block & 1
    ahead = (sign * ((block >> 1) - (rep >> 1))) & 15
    carrier = jnp.where(ahead == 8, kind, (ahead > 8).astype(jnp.int32))
    carrier = jnp.where(ahead == 0, core, carrier)
    distance = jnp.where(ahead > 8, 16 - ahead, ahead)
    odd = (distance & 1) == 1
    step = jnp.where(odd, distance, distance - 1)
    second = (kind != carrier).astype(jnp.int32)
    pair = 2 * ((step & 2) + ((step >> 2) & 1)) + second
    return distance == 0, odd, pair, second, carrier == core


def gathered_places(rep):
    here, odd, pair, second, local = places(rep, -1)
    at = jnp.where(here, second, jnp.where(odd, 2, 10) + pair)
    return jnp.where(local, at, at + 16)


def scattered_places(rep):
    here, odd, pair, second, local = places(rep, 1)
    at = jnp.where(here, 15 + second, jnp.where(odd, 7, 0) + pair)
    return jnp.where(local, at, at + 17)


def gather_weights(own):
    near = jnp.stack([own, swap(own)])
    one = hop(near, 1)
    five = hop(one, 4)
    three_seven = hop(jnp.concatenate([one, five]), 2)
    odd = jnp.concatenate([one, five, three_seven])
    even = hop(odd, 1)
    return near, odd, even, swap(odd), swap(even)


def scatter_sum(even, odd, give_odd):
    def add(*parts):
        return functools.reduce(jnp.add, [part.astype(F32) for part in parts])

    one = hop(even, 1)
    got = swap(give_odd)
    last = lax.pad(one, jnp.zeros((), BF16), ((-4, 1, 0), (0, 0, 0), (0, 0, 0)))
    second = add(odd[4:], got[4:], last).astype(BF16)
    two = hop(second, 2)
    four = hop(add(odd[2:4], got[2:4], one[2:4], two[2:]).astype(BF16), 4)
    return hop(add(odd[:2], got[:2], one[:2], two[:2], four).astype(BF16), 1)


def per_device(tokens, grad_out, gates, expert_ids, w_all, touched):
    rep = lax.axis_index("rep")
    ids = expert_ids.T
    mbytes = 1 << 20
    early = lambda i: jnp.minimum(i, STEPS - 1)
    late = lambda i: jnp.maximum(i - STEPS, 0)
    sent = call(
        place_kernel,
        2 * STEPS,
        [
            whole((2, TOK)),
            whole((2, TOK)),
            columns(TOK, early),
            columns(TOK, lambda i: early(i) + STEPS),
            columns(TOK, late),
            columns(TOK, lambda i: late(i) + STEPS),
        ],
        columns(ROWS),
        sds((ROWS, WIDTH), BF16),
        4 * ROWS * 256 * HALF,
        8 * mbytes,
        [pltpu.VMEM((ROWS, 2 * TOK), BF16), pltpu.VMEM((ROWS, 128), F32)],
    )(ids, gates.T, tokens, tokens, grad_out, grad_out)
    received = exchange(sent)
    back = call(
        back_kernel,
        1,
        [whole((2, TOK))],
        whole((2 * TOK, ROWS)),
        sds((2 * TOK, ROWS), BF16),
        0,
        mbytes,
    )(ids)
    gathered = gather_weights(w_all[0])
    in_place = [pl.BlockSpec(memory_space=pl.ANY)]
    weights = [
        pltpu.VMEM((sum(piece.shape[0] for piece in gathered), 128, 3 * HID), BF16),
        pltpu.SemaphoreType.DMA((len(gathered),)),
    ]
    table = gathered_places(rep)
    info = jnp.concatenate([touched.reshape(-1), scattered_places(rep)])
    shares = [(n, 3 * HID, 128) for n in (7, 8, 2, 7, 8)]
    both_grad, even, odd, here, give_even, give_odd = call(
        expert_kernel,
        3 * STEPS,
        in_place * 6,
        [whole((ROWS, 2 * HID))] + [whole(share) for share in shares],
        [sds((ROWS, 2 * HID), BF16)] + [sds(share, BF16) for share in shares],
        2 * ROWS * HALF * 12 * HID,
        16 * mbytes,
        [
            pltpu.VMEM((ROWS, WIDTH), BF16),
            weights[0],
            pltpu.VMEM((6 * HID, ROWS), BF16),
            pltpu.VMEM((ROWS, 4 * HID), F32),
            pltpu.VMEM((ROWS, 2 * HID), F32),
            pltpu.SemaphoreType.DMA((2 * STEPS,)),
            weights[1],
        ],
        2,
    )(table, info, received, *gathered)
    paired = (even.astype(F32) + swap(give_even).astype(F32)).astype(BF16)
    paired, both_grad, give_odd = lax.optimization_barrier((paired, both_grad, give_odd))
    final = scatter_sum(paired, odd, give_odd)
    slot_grad = call(
        slot_grad_kernel,
        STEPS,
        [whole((ROWS, 2 * HID))] + in_place * 5,
        columns(ROWS),
        sds((ROWS, HALF), BF16),
        2 * ROWS * HALF * 4 * HID,
        6 * mbytes,
        weights,
        1,
    )(table, both_grad, *gathered)
    returned = exchange(slot_grad)
    token_grad = call(
        combine_kernel,
        STEPS,
        [whole((2 * TOK, ROWS)), columns(ROWS)],
        whole((TOK, WIDTH)),
        sds((TOK, WIDTH), BF16),
        2 * ROWS * 256 * HALF,
        4 * mbytes,
    )(back, returned)
    final, token_grad = lax.optimization_barrier((final, token_grad))
    total = here.astype(F32) + final.astype(F32)
    owned = total[:1] + swap(total[1:].astype(BF16)).astype(F32)
    return (token_grad, jnp.swapaxes(owned, 1, 2))


def solution(mesh):
    in_specs = (
        P(("rep", "exp"), None),
        P(("rep", "exp"), None),
        P(("rep", "exp"), None),
        P(("rep", "exp"), None),
        P("exp", "rep", None),
        P("rep", "exp", None),
    )
    out_specs = (P(("rep", "exp"), None), P("exp", "rep", None))

    return jax.shard_map(
        per_device, mesh=mesh, in_specs=in_specs, out_specs=out_specs, check_vma=False
    )
```

profile of v0, /device:TPU:1, one launch (start us, length us, event | category | flops | bytes accessed | tf_op | source)
XLA Modules:
  0.0 201.6 jit_solution(7220016490057642285)
XLA Ops:
  0.6 8.2 %shard_map.77 = bf16[640,4096]{1,0:T(8,128)(2,1)} custom-call(s32[2,128]{1,0:T(2,128)} %bitcast.16, f32[2,128]{1,0:T(2,128)} %bitcast.18, bf16[128,4096]{1,0:T(8,128)(2,1)} %x_high_ref.1, bf16[128,4096]{1,0:T(8,128)(2,1)} %x_high_ref.1, bf16[128,4096]{1,0:T(8,128)(2,1)} %dy_high_ref.1, bf16[128,4096]{1,0:T(8,128)(2,1)} %dy_high_ref.1), custom_call_target="tpu_custom_call" | custom-call | flops 1342177280 | bytes 8388608 | tf_op jit(solution)/shard_map/pallas_call | solution.py:353
  8.8 7.7 %all-to-all-start = ((bf16[16,40,4096]{2,1,0:T(8,128)(2,1)}), bf16[16,40,4096]{2,1,0:T(8,128)(2,1)}, u32[]{:S(2)}, u32[]{:S(2)}) async-start(bf16[16,40,4096]{2,1,0:T(8,128)(2,1)} %bitcast.11), calls=%async_computation | async-start | bytes 10485760 | tf_op jit(solution)/shard_map/all_to_all | solution.py:279
  16.5 0.0 copy-start.8
  16.6 5.7 %collective-permute-start = (bf16[128,384]{1,0:T(8,128)(2,1)S(1)}, bf16[128,384]{1,0:T(8,128)(2,1)S(1)}, u32[]{:S(2)}, u32[]{:S(2)}) collective-permute-start(bf16[128,384]{1,0:T(8,128)(2,1)S(1)} %bitcast.14), channel_id=1, source_target_pairs={{0,16},{16,0},{32,48},{48,32},{64,80},{80,64},{96,112},{112,96},{1... | collective-permute-start | bytes 294920 | tf_op jit(solution)/shard_map/ppermute | solution.py:294
  22.3 0.9 collective-permute-done
  23.3 0.0 copy-start.2
  23.3 8.3 %collective-permute-start.1 = (bf16[2,128,384]{2,1,0:T(8,128)(2,1)S(1)}, bf16[2,128,384]{2,1,0:T(8,128)(2,1)S(1)}, u32[]{:S(2)}, u32[]{:S(2)}) collective-permute-start(bf16[2,128,384]{2,1,0:T(8,128)(2,1)S(1)} %pad_maximum_fusion.1.refs_0_), channel_id=1, source_target_pairs={{0,32},{16,496},{32,64},{48,16},{64,96},{80,48},{96,128},{112,80},... | collective-permute-start | bytes 589832 | tf_op jit(solution)/shard_map/ppermute | solution.py:290
  31.5 2.6 %collective-permute-done.1 = bf16[2,128,384]{2,1,0:T(8,128)(2,1)S(1)} collective-permute-done((bf16[2,128,384]{2,1,0:T(8,128)(2,1)S(1)}, bf16[2,128,384]{2,1,0:T(8,128)(2,1)S(1)}, u32[]{:S(2)}, u32[]{:S(2)}) %collective-permute-start.1) | collective-permute-done | bytes 196640 | tf_op jit(solution)/shard_map/ppermute | solution.py:290
  34.1 5.5 %collective-permute-start.2 = (bf16[2,128,384]{2,1,0:T(8,128)(2,1)S(1)}, bf16[2,128,384]{2,1,0:T(8,128)(2,1)S(1)}, u32[]{:S(2)}, u32[]{:S(2)}) collective-permute-start(bf16[2,128,384]{2,1,0:T(8,128)(2,1)S(1)} %collective-permute-done.1), channel_id=1, source_target_pairs={{0,128},{16,400},{32,160},{48,432},{64,192},{80,464},{96,224},{112... | collective-permute-start | bytes 589832 | tf_op jit(solution)/shard_map/ppermute | solution.py:290
  39.7 6.8 %collective-permute-done.2 = bf16[2,128,384]{2,1,0:T(8,128)(2,1)S(1)} collective-permute-done((bf16[2,128,384]{2,1,0:T(8,128)(2,1)S(1)}, bf16[2,128,384]{2,1,0:T(8,128)(2,1)S(1)}, u32[]{:S(2)}, u32[]{:S(2)}) %collective-permute-start.2) | collective-permute-done | bytes 196640 | tf_op jit(solution)/shard_map/ppermute | solution.py:290
  46.5 7.8 %collective-permute-start.3 = (bf16[4,128,384]{2,1,0:T(8,128)(2,1)S(1)}, bf16[4,128,384]{2,1,0:T(8,128)(2,1)S(1)}, u32[]{:S(2)}, u32[]{:S(2)}) collective-permute-start(bf16[4,128,384]{2,1,0:T(8,128)(2,1)S(1)} %pad_maximum_fusion), channel_id=1, source_target_pairs={{0,64},{16,464},{32,96},{48,496},{64,128},{80,16},{96,160},{112,48... | collective-permute-start | bytes 1179656 | tf_op jit(solution)/shard_map/ppermute | solution.py:290
  54.4 8.7 %collective-permute-done.3 = bf16[4,128,384]{2,1,0:T(8,128)(2,1)S(1)} collective-permute-done((bf16[4,128,384]{2,1,0:T(8,128)(2,1)S(1)}, bf16[4,128,384]{2,1,0:T(8,128)(2,1)S(1)}, u32[]{:S(2)}, u32[]{:S(2)}) %collective-permute-start.3) | collective-permute-done | bytes 393248 | tf_op jit(solution)/shard_map/ppermute | solution.py:290
  63.0 0.1 constant_dynamic-update-slice_fusion.refs_1_
  63.1 0.0 copy-start.1
  63.1 2.0 %collective-permute-start.4 = (bf16[8,128,384]{2,1,0:T(8,128)(2,1)S(1)}, bf16[8,128,384]{2,1,0:T(8,128)(2,1)S(1)}, u32[]{:S(2)}, u32[]{:S(2)}) collective-permute-start(bf16[8,128,384]{2,1,0:T(8,128)(2,1)S(1)} %constant_dynamic-update-slice_fusion.refs_1_), channel_id=1, source_target_pairs={{0,32},{16,496},{32,64},{48,16},{64,96},{80,48},{96,128},{112,80},... | collective-permute-start | bytes 2359304 | tf_op jit(solution)/shard_map/ppermute | solution.py:290
  65.1 4.9 %collective-permute-start.5 = (bf16[8,128,384]{2,1,0:T(8,128)(2,1)S(1)}, bf16[8,128,384]{2,1,0:T(8,128)(2,1)S(1)}, u32[]{:S(2)}, u32[]{:S(2)}) collective-permute-start(bf16[8,128,384]{2,1,0:T(8,128)(2,1)S(1)} %constant_dynamic-update-slice_fusion.refs_1_), channel_id=1, source_target_pairs={{0,16},{16,0},{32,48},{48,32},{64,80},{80,64},{96,112},{112,96},{1... | collective-permute-start | bytes 2359304 | tf_op jit(solution)/shard_map/ppermute | solution.py:294
  70.0 6.2 %collective-permute-done.4.refs_2_ = bf16[8,128,384]{2,1,0:T(8,128)(2,1)S(1)} collective-permute-done((bf16[8,128,384]{2,1,0:T(8,128)(2,1)S(1)}, bf16[8,128,384]{2,1,0:T(8,128)(2,1)S(1)}, u32[]{:S(2)}, u32[]{:S(2)}) %collective-permute-start.4) | collective-permute-done | bytes 786464 | tf_op jit(solution)/shard_map/ppermute | solution.py:290
  76.2 7.0 %collective-permute-start.6 = (bf16[8,128,384]{2,1,0:T(8,128)(2,1)S(1)}, bf16[8,128,384]{2,1,0:T(8,128)(2,1)S(1)}, u32[]{:S(2)}, u32[]{:S(2)}) collective-permute-start(bf16[8,128,384]{2,1,0:T(8,128)(2,1)S(1)} %collective-permute-done.4.refs_2_), channel_id=1, source_target_pairs={{0,16},{16,0},{32,48},{48,32},{64,80},{80,64},{96,112},{112,96},{1... | collective-permute-start | bytes 2359304 | tf_op jit(solution)/shard_map/ppermute | solution.py:294
  83.2 0.6 compare_select_fusion.7.table_ref
  83.8 0.6 pad_add_fusion.info_ref
  84.4 0.0 collective-permute-done.5.refs_3_
  84.4 0.7 collective-permute-done.6.refs_4_
  85.1 1.1 all-to-all-done
  86.2 15.3 %shard_map.78 = (bf16[640,256]{1,0:T(8,128)(2,1)}, bf16[7,384,128]{2,1,0:T(8,128)(2,1)}, bf16[8,384,128]{2,1,0:T(8,128)(2,1)}, bf16[2,384,128]{2,1,0:T(8,128)(2,...) custom-call(s32[32]{0:T(128)} %compare_select_fusion.7.table_ref, s32[64]{0:T(128)} %pad_add_fusion.info_ref, ...), custom_call_target="tpu_custom_call" | custom-call | flops 4026531840 | bytes 16777216 | tf_op jit(solution)/shard_map/pallas_call | solution.py:389
  101.5 6.8 %collective-permute-start.7 = (bf16[7,384,128]{2,1,0:T(8,128)(2,1)}, bf16[7,384,128]{2,1,0:T(8,128)(2,1)S(1)}, u32[]{:S(2)}, u32[]{:S(2)}) collective-permute-start(bf16[7,384,128]{2,1,0:T(8,128)(2,1)} %get-tuple-element.15), channel_id=1, source_target_pairs={{0,16},{16,0},{32,48},{48,32},{64,80},{80,64},{96,112},{112,96},{1... | collective-permute-start | bytes 2064392 | tf_op jit(solution)/shard_map/ppermute | solution.py:294
  108.3 2.0 collective-permute-done.7
  110.3 2.1 %add_convert_fusion = bf16[7,384,128]{2,1,0:T(8,128)(2,1)} fusion(bf16[7,384,128]{2,1,0:T(8,128)(2,1)S(1)} %collective-permute-done.7, bf16[7,384,128]{2,1,0:T(8,128)(2,1)} %get-tuple-element.14), kind=kLoop, calls=%fused_computation | loop fusion | flops 1376256 | bytes 2064384 | tf_op jit(solution)/shard_map/convert_element_type | solution.py:408
  112.4 7.1 %shard_map.80 = bf16[640,2048]{1,0:T(8,128)(2,1)} custom-call(s32[32]{0:T(128)} %compare_select_fusion.7.table_ref, bf16[640,256]{1,0:T(8,128)(2,1)} %get-tuple-element.20.both_ref, bf16[2,128,384]{2,1,0:T(8,128)(2,1)} %copy-done.2, bf16[8,128,384]{2,1,0:T(8,128)(2,1)} %copy-done.1, bf16[8,128,384]{2,1,0:T(8,128)(2,1)} %copy-done.3, ...), custom_call_target="tpu_custom_call" | custom-call | flops 1342177280 | bytes 6291456 | tf_op jit(solution)/shard_map/pallas_call | solution.py:411
  119.5 4.5 %all-to-all-start.1 = ((bf16[16,40,2048]{2,1,0:T(8,128)(2,1)}), bf16[16,40,2048]{2,1,0:T(8,128)(2,1)S(1)}, u32[]{:S(2)}, u32[]{:S(2)}) async-start(bf16[16,40,2048]{2,1,0:T(8,128)(2,1)} %bitcast.12), calls=%async_computation.1 | async-start | bytes 5242880 | tf_op jit(solution)/shard_map/all_to_all | solution.py:279
  124.0 2.6 %collective-permute-start.8 = (bf16[8,384,128]{2,1,0:T(8,128)(2,1)}, bf16[8,384,128]{2,1,0:T(8,128)(2,1)S(1)}, u32[]{:S(2)}, u32[]{:S(2)}) collective-permute-start(bf16[8,384,128]{2,1,0:T(8,128)(2,1)} %get-tuple-element.18), channel_id=1, source_target_pairs={{0,16},{16,0},{32,48},{48,32},{64,80},{80,64},{96,112},{112,96},{1... | collective-permute-start | bytes 2359304 | tf_op jit(solution)/shard_map/ppermute | solution.py:294
  126.6 16.5 %collective-permute-start.9 = (bf16[7,384,128]{2,1,0:T(8,128)(2,1)}, bf16[7,384,128]{2,1,0:T(8,128)(2,1)S(1)}, u32[]{:S(2)}, u32[]{:S(2)}) collective-permute-start(bf16[7,384,128]{2,1,0:T(8,128)(2,1)} %add_convert_fusion), channel_id=1, source_target_pairs={{0,32},{16,496},{32,64},{48,16},{64,96},{80,48},{96,128},{112,80},... | collective-permute-start | bytes 2064392 | tf_op jit(solution)/shard_map/ppermute | solution.py:290
  143.1 8.2 %collective-permute-done.9 = bf16[7,384,128]{2,1,0:T(8,128)(2,1)S(1)} collective-permute-done((bf16[7,384,128]{2,1,0:T(8,128)(2,1)}, bf16[7,384,128]{2,1,0:T(8,128)(2,1)S(1)}, u32[]{:S(2)}, u32[]{:S(2)}) %collective-permute-start.9) | collective-permute-done | bytes 688160 | tf_op jit(solution)/shard_map/ppermute | solution.py:290
  151.3 0.0 collective-permute-done.8
  151.3 0.1 add_convert_fusion.1
  151.4 4.5 %collective-permute-start.10 = (bf16[4,384,128]{2,1,0:T(8,128)(2,1)S(1)}, bf16[4,384,128]{2,1,0:T(8,128)(2,1)S(1)}, u32[]{:S(2)}, u32[]{:S(2)}) collective-permute-start(bf16[4,384,128]{2,1,0:T(8,128)(2,1)S(1)} %add_convert_fusion.1), channel_id=1, source_target_pairs={{0,64},{16,464},{32,96},{48,496},{64,128},{80,16},{96,160},{112,48... | collective-permute-start | bytes 1179656 | tf_op jit(solution)/shard_map/ppermute | solution.py:290
  155.9 7.8 %collective-permute-done.10 = bf16[4,384,128]{2,1,0:T(8,128)(2,1)S(1)} collective-permute-done((bf16[4,384,128]{2,1,0:T(8,128)(2,1)S(1)}, bf16[4,384,128]{2,1,0:T(8,128)(2,1)S(1)}, u32[]{:S(2)}, u32[]{:S(2)}) %collective-permute-start.10) | collective-permute-done | bytes 393248 | tf_op jit(solution)/shard_map/ppermute | solution.py:290
  163.7 0.1 add_convert_fusion.3
  163.8 6.5 %collective-permute-start.11 = (bf16[2,384,128]{2,1,0:T(8,128)(2,1)S(1)}, bf16[2,384,128]{2,1,0:T(8,128)(2,1)S(1)}, u32[]{:S(2)}, u32[]{:S(2)}) collective-permute-start(bf16[2,384,128]{2,1,0:T(8,128)(2,1)S(1)} %add_convert_fusion.3), channel_id=1, source_target_pairs={{0,128},{16,400},{32,160},{48,432},{64,192},{80,464},{96,224},{112... | collective-permute-start | bytes 589832 | tf_op jit(solution)/shard_map/ppermute | solution.py:290
  170.3 4.7 %collective-permute-done.11 = bf16[2,384,128]{2,1,0:T(8,128)(2,1)S(1)} collective-permute-done((bf16[2,384,128]{2,1,0:T(8,128)(2,1)S(1)}, bf16[2,384,128]{2,1,0:T(8,128)(2,1)S(1)}, u32[]{:S(2)}, u32[]{:S(2)}) %collective-permute-start.11) | collective-permute-done | bytes 196640 | tf_op jit(solution)/shard_map/ppermute | solution.py:290
  175.0 0.8 add_convert_fusion.2
  175.8 9.1 %collective-permute-start.12 = (bf16[2,384,128]{2,1,0:T(8,128)(2,1)}, bf16[2,384,128]{2,1,0:T(8,128)(2,1)S(1)}, u32[]{:S(2)}, u32[]{:S(2)}) collective-permute-start(bf16[2,384,128]{2,1,0:T(8,128)(2,1)} %add_convert_fusion.2), channel_id=1, source_target_pairs={{0,32},{16,496},{32,64},{48,16},{64,96},{80,48},{96,128},{112,80},... | collective-permute-start | bytes 589832 | tf_op jit(solution)/shard_map/ppermute | solution.py:290
  184.9 1.8 shard_map.79.back_ref
  186.7 1.5 copy-done
  188.2 4.4 %shard_map.81 = bf16[128,4096]{1,0:T(8,128)(2,1)} custom-call(bf16[256,640]{1,0:T(8,128)(2,1)} %shard_map.79.back_ref, bf16[640,2048]{1,0:T(8,128)(2,1)} %bitcast.13), custom_call_target="tpu_custom_call" | custom-call | flops 671088640 | bytes 4194304 | tf_op jit(solution)/shard_map/pallas_call | solution.py:423
  192.6 1.0 convert_add_fusion
  193.6 6.2 %collective-permute-start.13 = (bf16[1,384,128]{2,1,0:T(8,128)(2,1)S(1)}, bf16[1,384,128]{2,1,0:T(8,128)(2,1)S(1)}, u32[]{:S(2)}, u32[]{:S(2)}) collective-permute-start(bf16[1,384,128]{2,1,0:T(8,128)(2,1)S(1)} %slice.73), channel_id=1, source_target_pairs={{0,16},{16,0},{32,48},{48,32},{64,80},{80,64},{96,112},{112,96},{1... | collective-permute-start | bytes 294920 | tf_op jit(solution)/shard_map/ppermute | solution.py:294
  199.8 0.9 collective-permute-done.13
  200.8 0.8 copy.8
  (23 shorter events, 0.2 us)
Async XLA Ops:
  8.8 7.7 %copy-start.7 = (bf16[1,128,384]{2,1,0:T(8,128)(2,1)S(1)}, bf16[1,128,384]{2,1,0:T(8,128)(2,1)}, u32[]{:S(2)}) copy-start(bf16[1,128,384]{2,1,0:T(8,128)(2,1)} %param.10) | copy-start | bytes 294916
  8.8 77.4 %all-to-all-start = ((bf16[16,40,4096]{2,1,0:T(8,128)(2,1)}), bf16[16,40,4096]{2,1,0:T(8,128)(2,1)}, u32[]{:S(2)}, u32[]{:S(2)}) async-start(bf16[16,40,4096]{2,1,0:T(8,128)(2,1)} %bitcast.11), calls=%async_computation | async-start | bytes 10485760 | tf_op jit(solution)/shard_map/all_to_all | solution.py:279
  16.5 67.2 %copy-start.8 = (s32[1,1,32]{2,1,0:T(1,128)S(1)}, s32[1,1,32]{2,1,0:T(1,128)}, u32[]{:S(2)}) copy-start(s32[1,1,32]{2,1,0:T(1,128)} %param.11) | copy-start | bytes 388
  16.6 6.7 %collective-permute-start = (bf16[128,384]{1,0:T(8,128)(2,1)S(1)}, bf16[128,384]{1,0:T(8,128)(2,1)S(1)}, u32[]{:S(2)}, u32[]{:S(2)}) collective-permute-start(bf16[128,384]{1,0:T(8,128)(2,1)S(1)} %bitcast.14), channel_id=1, source_target_pairs={{0,16},{16,0},{32,48},{48,32},{64,80},{80,64},{96,112},{112,96},{1... | collective-permute-start | bytes 294920 | tf_op jit(solution)/shard_map/ppermute | solution.py:294
  23.3 62.9 %copy-start.2 = (bf16[2,128,384]{2,1,0:T(8,128)(2,1)}, bf16[2,128,384]{2,1,0:T(8,128)(2,1)S(1)}, u32[]{:S(2)}) copy-start(bf16[2,128,384]{2,1,0:T(8,128)(2,1)S(1)} %pad_maximum_fusion.1.refs_0_) | copy-start | bytes 589828
  23.3 10.9 %collective-permute-start.1 = (bf16[2,128,384]{2,1,0:T(8,128)(2,1)S(1)}, bf16[2,128,384]{2,1,0:T(8,128)(2,1)S(1)}, u32[]{:S(2)}, u32[]{:S(2)}) collective-permute-start(bf16[2,128,384]{2,1,0:T(8,128)(2,1)S(1)} %pad_maximum_fusion.1.refs_0_), channel_id=1, source_target_pairs={{0,32},{16,496},{32,64},{48,16},{64,96},{80,48},{96,128},{112,80},... | collective-permute-start | bytes 589832 | tf_op jit(solution)/shard_map/ppermute | solution.py:290
  34.1 12.3 %collective-permute-start.2 = (bf16[2,128,384]{2,1,0:T(8,128)(2,1)S(1)}, bf16[2,128,384]{2,1,0:T(8,128)(2,1)S(1)}, u32[]{:S(2)}, u32[]{:S(2)}) collective-permute-start(bf16[2,128,384]{2,1,0:T(8,128)(2,1)S(1)} %collective-permute-done.1), channel_id=1, source_target_pairs={{0,128},{16,400},{32,160},{48,432},{64,192},{80,464},{96,224},{112... | collective-permute-start | bytes 589832 | tf_op jit(solution)/shard_map/ppermute | solution.py:290
  46.5 16.5 %collective-permute-start.3 = (bf16[4,128,384]{2,1,0:T(8,128)(2,1)S(1)}, bf16[4,128,384]{2,1,0:T(8,128)(2,1)S(1)}, u32[]{:S(2)}, u32[]{:S(2)}) collective-permute-start(bf16[4,128,384]{2,1,0:T(8,128)(2,1)S(1)} %pad_maximum_fusion), channel_id=1, source_target_pairs={{0,64},{16,464},{32,96},{48,496},{64,128},{80,16},{96,160},{112,48... | collective-permute-start | bytes 1179656 | tf_op jit(solution)/shard_map/ppermute | solution.py:290
  63.1 23.1 %copy-start.1 = (bf16[8,128,384]{2,1,0:T(8,128)(2,1)}, bf16[8,128,384]{2,1,0:T(8,128)(2,1)S(1)}, u32[]{:S(2)}) copy-start(bf16[8,128,384]{2,1,0:T(8,128)(2,1)S(1)} %constant_dynamic-update-slice_fusion.refs_1_) | copy-start | bytes 2359300
  63.1 13.1 %collective-permute-start.4 = (bf16[8,128,384]{2,1,0:T(8,128)(2,1)S(1)}, bf16[8,128,384]{2,1,0:T(8,128)(2,1)S(1)}, u32[]{:S(2)}, u32[]{:S(2)}) collective-permute-start(bf16[8,128,384]{2,1,0:T(8,128)(2,1)S(1)} %constant_dynamic-update-slice_fusion.refs_1_), channel_id=1, source_target_pairs={{0,32},{16,496},{32,64},{48,16},{64,96},{80,48},{96,128},{112,80},... | collective-permute-start | bytes 2359304 | tf_op jit(solution)/shard_map/ppermute | solution.py:290
  65.1 19.2 %collective-permute-start.5 = (bf16[8,128,384]{2,1,0:T(8,128)(2,1)S(1)}, bf16[8,128,384]{2,1,0:T(8,128)(2,1)S(1)}, u32[]{:S(2)}, u32[]{:S(2)}) collective-permute-start(bf16[8,128,384]{2,1,0:T(8,128)(2,1)S(1)} %constant_dynamic-update-slice_fusion.refs_1_), channel_id=1, source_target_pairs={{0,16},{16,0},{32,48},{48,32},{64,80},{80,64},{96,112},{112,96},{1... | collective-permute-start | bytes 2359304 | tf_op jit(solution)/shard_map/ppermute | solution.py:294
  76.2 9.9 %copy-start.3 = (bf16[8,128,384]{2,1,0:T(8,128)(2,1)}, bf16[8,128,384]{2,1,0:T(8,128)(2,1)S(1)}, u32[]{:S(2)}) copy-start(bf16[8,128,384]{2,1,0:T(8,128)(2,1)S(1)} %collective-permute-done.4.refs_2_) | copy-start | bytes 2359300
  76.2 8.9 %collective-permute-start.6 = (bf16[8,128,384]{2,1,0:T(8,128)(2,1)S(1)}, bf16[8,128,384]{2,1,0:T(8,128)(2,1)S(1)}, u32[]{:S(2)}, u32[]{:S(2)}) collective-permute-start(bf16[8,128,384]{2,1,0:T(8,128)(2,1)S(1)} %collective-permute-done.4.refs_2_), channel_id=1, source_target_pairs={{0,16},{16,0},{32,48},{48,32},{64,80},{80,64},{96,112},{112,96},{1... | collective-permute-start | bytes 2359304 | tf_op jit(solution)/shard_map/ppermute | solution.py:294
  84.4 1.8 copy-start.4
  85.1 1.1 copy-start.5
  101.5 8.8 %collective-permute-start.7 = (bf16[7,384,128]{2,1,0:T(8,128)(2,1)}, bf16[7,384,128]{2,1,0:T(8,128)(2,1)S(1)}, u32[]{:S(2)}, u32[]{:S(2)}) collective-permute-start(bf16[7,384,128]{2,1,0:T(8,128)(2,1)} %get-tuple-element.15), channel_id=1, source_target_pairs={{0,16},{16,0},{32,48},{48,32},{64,80},{80,64},{96,112},{112,96},{1... | collective-permute-start | bytes 2064392 | tf_op jit(solution)/shard_map/ppermute | solution.py:294
  119.5 31.7 %copy-start.6 = (bf16[8,384,128]{2,1,0:T(8,128)(2,1)S(1)}, bf16[8,384,128]{2,1,0:T(8,128)(2,1)}, u32[]{:S(2)}) copy-start(bf16[8,384,128]{2,1,0:T(8,128)(2,1)} %get-tuple-element.13) | copy-start | bytes 2359300
  119.5 67.1 %all-to-all-start.1 = ((bf16[16,40,2048]{2,1,0:T(8,128)(2,1)}), bf16[16,40,2048]{2,1,0:T(8,128)(2,1)S(1)}, u32[]{:S(2)}, u32[]{:S(2)}) async-start(bf16[16,40,2048]{2,1,0:T(8,128)(2,1)} %bitcast.12), calls=%async_computation.1 | async-start | bytes 5242880 | tf_op jit(solution)/shard_map/all_to_all | solution.py:279
  124.0 27.3 %collective-permute-start.8 = (bf16[8,384,128]{2,1,0:T(8,128)(2,1)}, bf16[8,384,128]{2,1,0:T(8,128)(2,1)S(1)}, u32[]{:S(2)}, u32[]{:S(2)}) collective-permute-start(bf16[8,384,128]{2,1,0:T(8,128)(2,1)} %get-tuple-element.18), channel_id=1, source_target_pairs={{0,16},{16,0},{32,48},{48,32},{64,80},{80,64},{96,112},{112,96},{1... | collective-permute-start | bytes 2359304 | tf_op jit(solution)/shard_map/ppermute | solution.py:294
  126.6 24.7 %collective-permute-start.9 = (bf16[7,384,128]{2,1,0:T(8,128)(2,1)}, bf16[7,384,128]{2,1,0:T(8,128)(2,1)S(1)}, u32[]{:S(2)}, u32[]{:S(2)}) collective-permute-start(bf16[7,384,128]{2,1,0:T(8,128)(2,1)} %add_convert_fusion), channel_id=1, source_target_pairs={{0,32},{16,496},{32,64},{48,16},{64,96},{80,48},{96,128},{112,80},... | collective-permute-start | bytes 2064392 | tf_op jit(solution)/shard_map/ppermute | solution.py:290
  151.4 12.3 %collective-permute-start.10 = (bf16[4,384,128]{2,1,0:T(8,128)(2,1)S(1)}, bf16[4,384,128]{2,1,0:T(8,128)(2,1)S(1)}, u32[]{:S(2)}, u32[]{:S(2)}) collective-permute-start(bf16[4,384,128]{2,1,0:T(8,128)(2,1)S(1)} %add_convert_fusion.1), channel_id=1, source_target_pairs={{0,64},{16,464},{32,96},{48,496},{64,128},{80,16},{96,160},{112,48... | collective-permute-start | bytes 1179656 | tf_op jit(solution)/shard_map/ppermute | solution.py:290
  163.8 11.2 %collective-permute-start.11 = (bf16[2,384,128]{2,1,0:T(8,128)(2,1)S(1)}, bf16[2,384,128]{2,1,0:T(8,128)(2,1)S(1)}, u32[]{:S(2)}, u32[]{:S(2)}) collective-permute-start(bf16[2,384,128]{2,1,0:T(8,128)(2,1)S(1)} %add_convert_fusion.3), channel_id=1, source_target_pairs={{0,128},{16,400},{32,160},{48,432},{64,192},{80,464},{96,224},{112... | collective-permute-start | bytes 589832 | tf_op jit(solution)/shard_map/ppermute | solution.py:290
  175.8 16.8 %collective-permute-start.12 = (bf16[2,384,128]{2,1,0:T(8,128)(2,1)}, bf16[2,384,128]{2,1,0:T(8,128)(2,1)S(1)}, u32[]{:S(2)}, u32[]{:S(2)}) collective-permute-start(bf16[2,384,128]{2,1,0:T(8,128)(2,1)} %add_convert_fusion.2), channel_id=1, source_target_pairs={{0,32},{16,496},{32,64},{48,16},{64,96},{80,48},{96,128},{112,80},... | collective-permute-start | bytes 589832 | tf_op jit(solution)/shard_map/ppermute | solution.py:290
  186.7 1.5 copy-start
  193.6 7.2 %collective-permute-start.13 = (bf16[1,384,128]{2,1,0:T(8,128)(2,1)S(1)}, bf16[1,384,128]{2,1,0:T(8,128)(2,1)S(1)}, u32[]{:S(2)}, u32[]{:S(2)}) collective-permute-start(bf16[1,384,128]{2,1,0:T(8,128)(2,1)S(1)} %slice.73), channel_id=1, source_target_pairs={{0,16},{16,0},{32,48},{48,32},{64,80},{80,64},{96,112},{112,96},{1... | collective-permute-start | bytes 294920 | tf_op jit(solution)/shard_map/ppermute | solution.py:294
where the time goes:
time: 203 us; the launch traced here: 202 us
  starting transfers between devices  106 us (52%)
  waiting for transfers between devices  50.5 us (25%)
  Pallas kernels  36.8 us (18%)
  other arithmetic  5.42 us (3%)
  local copies, waits for them, and re-layouts  2.49 us (1%)
    ppermute x8, starting transfers between devices, hop(): return lax.ppermute(value, 'rep', turn)  60.1 us
    ppermute x8, waiting for transfers between devices, hop(): return lax.ppermute(value, 'rep', turn)  44.9 us
    ppermute x6, starting transfers between devices, swap(): lax.ppermute(value, 'rep', [(i, i ^ 1) for i in range(lax.axis_size('rep'...  33.2 us
    pallas_call x1, Pallas kernels, per_device(): call(expert_kernel, 3 * STEPS, in_place * 6, [whole((ROWS, 2 * HID))] + [...  15.3 us
    all_to_all x2, starting transfers between devices, exchange(): lax.all_to_all(rows.reshape(EXPERTS, 2 * CAP, -1), 'exp', split_axis=0, c...  12.2 us
    pallas_call x1, Pallas kernels, per_device(): call(place_kernel, 2 * STEPS, [whole((2, TOK)), whole((2, TOK)), columns(...  8.17 us
    pallas_call x1, Pallas kernels, per_device(): call(slot_grad_kernel, STEPS, [whole((ROWS, 2 * HID))] + in_place * 5, co...  7.1 us
    ppermute x6, waiting for transfers between devices, swap(): lax.ppermute(value, 'rep', [(i, i ^ 1) for i in range(lax.axis_size('rep'...  4.52 us
  transfers between devices with their start and end apart: 16, of which 12 were waited for; matrix products, arithmetic and copies ran while one was open for 1% of the time, Pallas kernels for 3%

commit v1 on v0

--- a/solution.py
+++ b/solution.py
@@ -120,8 +120,8 @@
 
 
 def expert_kernel(table_ref, info_ref, recv_ref, *refs):
-    gathered, both_ref, pieces = refs[:5], refs[5], refs[6:11]
-    slots, weights, turned_ref, gate_up, down, sems, w_sems = refs[11:]
+    gathered, both_ref, pieces = refs[:5], refs[5], refs[6:10]
+    slots, weights, turned_ref, gate_up, down, sems, w_sems = refs[10:]
     step = pl.program_id(0)
 
     @pl.when(step == 0)
@@ -189,7 +189,7 @@
     at = pl.multiple_of(step * COLS, COLS)
     x = slots[:, pl.ds(at, COLS)]
     dy = slots[:, pl.ds(pl.multiple_of(at + HALF, COLS), COLS)]
-    spans = tuple(zip(pieces, (0, 7, 15, 17, 24), (7, 15, 17, 24, 32)))
+    spans = tuple(zip(pieces, (0, 8, 16, 24), (8, 16, 24, 32)))
     for h in range(2):
         base = 3 * HID * h
         proj = jnp.dot(turned_ref[base : base + 2 * HID, :], x, preferred_element_type=F32)
@@ -294,31 +294,35 @@
     return lax.ppermute(value, "rep", [(i, i ^ 1) for i in range(lax.axis_size("rep"))])
 
 
-def places(rep, sign):
+def gathered_places(rep):
     block = jnp.arange(BLOCKS, dtype=jnp.int32)
     core = rep & 1
     kind = block & 1
-    ahead = (sign * ((block >> 1) - (rep >> 1))) & 15
-    carrier = jnp.where(ahead == 8, kind, (ahead > 8).astype(jnp.int32))
-    carrier = jnp.where(ahead == 0, core, carrier)
-    distance = jnp.where(ahead > 8, 16 - ahead, ahead)
+    behind = ((rep >> 1) - (block >> 1)) & 15
+    carrier = jnp.where(behind == 8, kind, (behind > 8).astype(jnp.int32))
+    carrier = jnp.where(behind == 0, core, carrier)
+    distance = jnp.where(behind > 8, 16 - behind, behind)
     odd = (distance & 1) == 1
     step = jnp.where(odd, distance, distance - 1)
     second = (kind != carrier).astype(jnp.int32)
     pair = 2 * ((step & 2) + ((step >> 2) & 1)) + second
-    return distance == 0, odd, pair, second, carrier == core
-
-
-def gathered_places(rep):
-    here, odd, pair, second, local = places(rep, -1)
-    at = jnp.where(here, second, jnp.where(odd, 2, 10) + pair)
-    return jnp.where(local, at, at + 16)
+    at = jnp.where(behind == 0, second, jnp.where(odd, 2, 10) + pair)
+    return jnp.where(carrier == core, at, at + 16)
 
 
 def scattered_places(rep):
-    here, odd, pair, second, local = places(rep, 1)
-    at = jnp.where(here, 15 + second, jnp.where(odd, 7, 0) + pair)
-    return jnp.where(local, at, at + 17)
+    block = jnp.arange(BLOCKS, dtype=jnp.int32)
+    ahead = ((block >> 1) - (rep >> 1)) & 15
+    index = ahead >> 2
+    rest = ahead & 3
+    at = jnp.where(rest == 1, index, jnp.where(rest == 2, 8 + index, 12 + index))
+    at = jnp.where(rest == 3, 4 + ((index + 1) & 3), at)
+    return jnp.where((block & 1) == (rep & 1), at, at + 16)
+
+
+def shift(value, distance):
+    reps = lax.axis_size("rep")
+    return lax.ppermute(value, "rep", [(i, (i + 2 * distance) % reps) for i in range(reps)])
 
 
 def gather_weights(own):
@@ -331,17 +335,8 @@
     return near, odd, even, swap(odd), swap(even)
 
 
-def scatter_sum(even, odd, give_odd):
-    def add(*parts):
-        return functools.reduce(jnp.add, [part.astype(F32) for part in parts])
-
-    one = hop(even, 1)
-    got = swap(give_odd)
-    last = lax.pad(one, jnp.zeros((), BF16), ((-4, 1, 0), (0, 0, 0), (0, 0, 0)))
-    second = add(odd[4:], got[4:], last).astype(BF16)
-    two = hop(second, 2)
-    four = hop(add(odd[2:4], got[2:4], one[2:4], two[2:]).astype(BF16), 4)
-    return hop(add(odd[:2], got[:2], one[:2], two[:2], four).astype(BF16), 1)
+def add(*parts):
+    return functools.reduce(jnp.add, [part.astype(F32) for part in parts])
 
 
 def per_device(tokens, grad_out, gates, expert_ids, w_all, touched):
@@ -385,8 +380,8 @@
     ]
     table = gathered_places(rep)
     info = jnp.concatenate([touched.reshape(-1), scattered_places(rep)])
-    shares = [(n, 3 * HID, 128) for n in (7, 8, 2, 7, 8)]
-    both_grad, even, odd, here, give_even, give_odd = call(
+    shares = [(8, 3 * HID, 128)] * 4
+    both_grad, sides, rest, give_sides, give_rest = call(
         expert_kernel,
         3 * STEPS,
         in_place * 6,
@@ -405,9 +400,25 @@
         ],
         2,
     )(table, info, received, *gathered)
-    paired = (even.astype(F32) + swap(give_even).astype(F32)).astype(BF16)
-    paired, both_grad, give_odd = lax.optimization_barrier((paired, both_grad, give_odd))
-    final = scatter_sum(paired, odd, give_odd)
+    got = swap(give_sides)
+    above = add(sides[:4], got[:4]).astype(BF16)
+    below = add(sides[4:], got[4:]).astype(BF16)
+    above, below, both_grad, give_rest = lax.optimization_barrier(
+        (above, below, both_grad, give_rest)
+    )
+    from_below = shift(above, 1)
+    from_above = shift(below, -1)
+    got = swap(give_rest)
+    two_above = add(rest[:2], got[:2]).astype(BF16)
+    two_below = add(rest[2:4], got[2:4]).astype(BF16)
+    two_below, two_above = shift(two_above, 2), shift(two_below, -2)
+    near = [add(rest[4 + i], got[4 + i], from_below[i], from_above[i]) for i in range(4)]
+    far = [
+        shift((near[1] + two_below[1].astype(F32)).astype(BF16), 4),
+        shift(near[2].astype(BF16), 8),
+        shift((near[3] + two_above[0].astype(F32)).astype(BF16), -4),
+    ]
+    near = add(near[0], two_below[0], two_above[1])
     slot_grad = call(
         slot_grad_kernel,
         STEPS,
@@ -429,10 +440,8 @@
         2 * ROWS * 256 * HALF,
         4 * mbytes,
     )(back, returned)
-    final, token_grad = lax.optimization_barrier((final, token_grad))
-    total = here.astype(F32) + final.astype(F32)
-    owned = total[:1] + swap(total[1:].astype(BF16)).astype(F32)
-    return (token_grad, jnp.swapaxes(owned, 1, 2))
+    far, token_grad = lax.optimization_barrier((far, token_grad))
+    return (token_grad, add(near, *far).T[None])
 
 
 def solution(mesh):

time: 203 us -> 200 us (0.985)
  the two profiles are of different devices: /device:TPU:1 before, /device:TPU:2 now
where the time goes in v1:
time: 200 us; the launch traced here: 199 us
  starting transfers between devices  81.6 us (41%)
  waiting for transfers between devices  72 us (36%)
  Pallas kernels  36.6 us (18%)
  other arithmetic  5.76 us (3%)
  local copies, waits for them, and re-layouts  2.48 us (1%)
    ppermute x4, waiting for transfers between devices, hop(): return lax.ppermute(value, 'rep', turn)  46.6 us
    ppermute x7, starting transfers between devices, shift(): lax.ppermute(value, 'rep', [(i, (i + 2 * distance) % reps) for i in range...  43.5 us
    all_to_all x2, starting transfers between devices, exchange(): lax.all_to_all(rows.reshape(EXPERTS, 2 * CAP, -1), 'exp', split_axis=0, c...  19.5 us
    ppermute x7, waiting for transfers between devices, shift(): lax.ppermute(value, 'rep', [(i, (i + 2 * distance) % reps) for i in range...  19.4 us
    pallas_call x1, Pallas kernels, per_device(): call(expert_kernel, 3 * STEPS, in_place * 6, [whole((ROWS, 2 * HID))] + [...  15.1 us
    ppermute x5, starting transfers between devices, swap(): lax.ppermute(value, 'rep', [(i, i ^ 1) for i in range(lax.axis_size('rep'...  9.58 us
    ppermute x4, starting transfers between devices, hop(): return lax.ppermute(value, 'rep', turn)  9.04 us
    pallas_call x1, Pallas kernels, per_device(): call(place_kernel, 2 * STEPS, [whole((2, TOK)), whole((2, TOK)), columns(...  8.08 us
  transfers between devices with their start and end apart: 18, of which 11 were waited for; matrix products, arithmetic and copies ran while one was open for 1% of the time, Pallas kernels for 3%

profile of v1, /device:TPU:2, one launch (start us, length us, event | category | flops | bytes accessed | tf_op | source)
XLA Modules:
  0.0 199.4 jit_solution(17117839895625919412)
XLA Ops:
  0.6 8.1 %shard_map.77 = bf16[640,4096]{1,0:T(8,128)(2,1)} custom-call(s32[2,128]{1,0:T(2,128)} %bitcast.32, f32[2,128]{1,0:T(2,128)} %bitcast.34, bf16[128,4096]{1,0:T(8,128)(2,1)} %x_high_ref.1, bf16[128,4096]{1,0:T(8,128)(2,1)} %x_high_ref.1, bf16[128,4096]{1,0:T(8,128)(2,1)} %dy_high_ref.1, bf16[128,4096]{1,0:T(8,128)(2,1)} %dy_high_ref.1), custom_call_target="tpu_custom_call" | custom-call | flops 1342177280 | bytes 8388608 | tf_op jit(solution)/shard_map/pallas_call | solution.py:348
  8.7 10.4 %all-to-all-start = ((bf16[16,40,4096]{2,1,0:T(8,128)(2,1)}), bf16[16,40,4096]{2,1,0:T(8,128)(2,1)}, u32[]{:S(2)}, u32[]{:S(2)}) async-start(bf16[16,40,4096]{2,1,0:T(8,128)(2,1)} %bitcast.27), calls=%async_computation | async-start | bytes 10485760 | tf_op jit(solution)/shard_map/all_to_all | solution.py:279
  19.1 1.9 collective-permute-start
  21.0 1.3 collective-permute-done
  22.3 0.0 copy-start.2
  22.3 1.9 collective-permute-start.1
  24.2 10.4 %collective-permute-done.1 = bf16[2,128,384]{2,1,0:T(8,128)(2,1)S(1)} collective-permute-done((bf16[2,128,384]{2,1,0:T(8,128)(2,1)S(1)}, bf16[2,128,384]{2,1,0:T(8,128)(2,1)S(1)}, u32[]{:S(2)}, u32[]{:S(2)}) %collective-permute-start.1) | collective-permute-done | bytes 196640 | tf_op jit(solution)/shard_map/ppermute | solution.py:290
  34.6 2.8 %collective-permute-start.2 = (bf16[2,128,384]{2,1,0:T(8,128)(2,1)S(1)}, bf16[2,128,384]{2,1,0:T(8,128)(2,1)S(1)}, u32[]{:S(2)}, u32[]{:S(2)}) collective-permute-start(bf16[2,128,384]{2,1,0:T(8,128)(2,1)S(1)} %collective-permute-done.1), channel_id=1, source_target_pairs={{0,128},{16,400},{32,160},{48,432},{64,192},{80,464},{96,224},{112... | collective-permute-start | bytes 589832 | tf_op jit(solution)/shard_map/ppermute | solution.py:290
  37.4 11.4 %collective-permute-done.2 = bf16[2,128,384]{2,1,0:T(8,128)(2,1)S(1)} collective-permute-done((bf16[2,128,384]{2,1,0:T(8,128)(2,1)S(1)}, bf16[2,128,384]{2,1,0:T(8,128)(2,1)S(1)}, u32[]{:S(2)}, u32[]{:S(2)}) %collective-permute-start.2) | collective-permute-done | bytes 196640 | tf_op jit(solution)/shard_map/ppermute | solution.py:290
  48.9 2.4 %collective-permute-start.3 = (bf16[4,128,384]{2,1,0:T(8,128)(2,1)S(1)}, bf16[4,128,384]{2,1,0:T(8,128)(2,1)S(1)}, u32[]{:S(2)}, u32[]{:S(2)}) collective-permute-start(bf16[4,128,384]{2,1,0:T(8,128)(2,1)S(1)} %pad_maximum_fusion), channel_id=1, source_target_pairs={{0,64},{16,464},{32,96},{48,496},{64,128},{80,16},{96,160},{112,48... | collective-permute-start | bytes 1179656 | tf_op jit(solution)/shard_map/ppermute | solution.py:290
  51.4 13.6 %collective-permute-done.3 = bf16[4,128,384]{2,1,0:T(8,128)(2,1)S(1)} collective-permute-done((bf16[4,128,384]{2,1,0:T(8,128)(2,1)S(1)}, bf16[4,128,384]{2,1,0:T(8,128)(2,1)S(1)}, u32[]{:S(2)}, u32[]{:S(2)}) %collective-permute-start.3) | collective-permute-done | bytes 393248 | tf_op jit(solution)/shard_map/ppermute | solution.py:290
  64.9 0.1 constant_dynamic-update-slice_fusion.refs_1_
  65.0 0.0 copy-start.1
  65.0 1.9 collective-permute-start.4
  66.9 1.9 collective-permute-start.5
  68.9 11.2 %collective-permute-done.4.refs_2_ = bf16[8,128,384]{2,1,0:T(8,128)(2,1)S(1)} collective-permute-done((bf16[8,128,384]{2,1,0:T(8,128)(2,1)S(1)}, bf16[8,128,384]{2,1,0:T(8,128)(2,1)S(1)}, u32[]{:S(2)}, u32[]{:S(2)}) %collective-permute-start.4) | collective-permute-done | bytes 786464 | tf_op jit(solution)/shard_map/ppermute | solution.py:290
  80.1 1.9 collective-permute-start.6
  82.0 0.5 compare_select_fusion.5.table_ref
  82.6 0.6 pad_add_fusion.info_ref
  83.2 1.1 collective-permute-done.6.refs_4_
  84.3 1.2 all-to-all-done
  85.5 15.1 %shard_map.78 = (bf16[640,256]{1,0:T(8,128)(2,1)}, bf16[8,384,128]{2,1,0:T(8,128)(2,1)}, bf16[8,384,128]{2,1,0:T(8,128)(2,1)}, bf16[8,384,128]{2,1,0:T(8,128)(2,1)}, bf16[8,384,128]{2,1,0:T(8,128)(2,1)}) custom-call(s32[32]{0:T(128)} %compare_select_fusion.5.table_ref, s32[64]{0:T(128)} %pad_add_fusion.info_ref, bf16[640,4096]{1,0:T(8,128)(2,1)} %bitcast.4.recv_ref, ...), custom_call_target="tpu_custom_call" | custom-call | flops 4026531840 | bytes 16777216 | tf_op jit(solution)/shard_map/pallas_call | solution.py:384
  100.6 1.9 collective-permute-start.7
  102.6 2.5 %collective-permute-done.7 = bf16[8,384,128]{2,1,0:T(8,128)(2,1)S(1)} collective-permute-done((bf16[8,384,128]{2,1,0:T(8,128)(2,1)}, bf16[8,384,128]{2,1,0:T(8,128)(2,1)S(1)}, u32[]{:S(2)}, u32[]{:S(2)}) %collective-permute-start.7) | collective-permute-done | bytes 786464 | tf_op jit(solution)/shard_map/ppermute | solution.py:294
  105.0 2.2 %add_convert_fusion = (bf16[4,384,128]{2,1,0:T(8,128)(2,1)}, bf16[4,384,128]{2,1,0:T(8,128)(2,1)}) fusion(bf16[8,384,128]{2,1,0:T(8,128)(2,1)S(1)} %collective-permute-done.7, bf16[8,384,128]{2,1,0:T(8,128)(2,1)} %get-tuple-element.16), kind=kLoop, calls=%fused_computation | loop fusion | flops 1572864 | bytes 2359296 | tf_op jit(solution)/shard_map/convert_element_type | solution.py:405
  107.3 7.2 %shard_map.80 = bf16[640,2048]{1,0:T(8,128)(2,1)} custom-call(s32[32]{0:T(128)} %compare_select_fusion.5.table_ref, bf16[640,256]{1,0:T(8,128)(2,1)} %get-tuple-element.23.both_ref, bf16[2,128,384]{2,1,0:T(8,128)(2,1)} %copy-done.2, bf16[8,128,384]{2,1,0:T(8,128)(2,1)} %copy-done.1, bf16[8,128,384]{2,1,0:T(8,128)(2,1)} %copy-done.3, ...), custom_call_target="tpu_custom_call" | custom-call | flops 1342177280 | bytes 6291456 | tf_op jit(solution)/shard_map/pallas_call | solution.py:422
  114.5 9.1 %all-to-all-start.1 = ((bf16[16,40,2048]{2,1,0:T(8,128)(2,1)}), bf16[16,40,2048]{2,1,0:T(8,128)(2,1)S(1)}, u32[]{:S(2)}, u32[]{:S(2)}) async-start(bf16[16,40,2048]{2,1,0:T(8,128)(2,1)} %bitcast.28), calls=%async_computation.1 | async-start | bytes 5242880 | tf_op jit(solution)/shard_map/all_to_all | solution.py:279
  123.6 1.9 collective-permute-start.8
  125.6 16.7 %collective-permute-start.10 = (bf16[4,384,128]{2,1,0:T(8,128)(2,1)}, bf16[4,384,128]{2,1,0:T(8,128)(2,1)S(1)}, u32[]{:S(2)}, u32[]{:S(2)}) collective-permute-start(bf16[4,384,128]{2,1,0:T(8,128)(2,1)} %get-tuple-element.22), channel_id=1, source_target_pairs={{0,480},{16,496},{32,0},{48,16},{64,32},{80,48},{96,64},{112,80},{... | collective-permute-start | bytes 1179656 | tf_op jit(solution)/shard_map/ppermute | solution.py:325
  142.2 1.9 collective-permute-start.9
  144.2 0.0 collective-permute-done.8
  144.2 0.1 add_convert_fusion.2
  144.3 4.4 %collective-permute-start.14 = (bf16[2,384,128]{2,1,0:T(8,128)(2,1)S(1)}, bf16[2,384,128]{2,1,0:T(8,128)(2,1)S(1)}, u32[]{:S(2)}, u32[]{:S(2)}) collective-permute-start(bf16[2,384,128]{2,1,0:T(8,128)(2,1)S(1)} %get-tuple-element.33), channel_id=1, source_target_pairs={{0,448},{16,464},{32,480},{48,496},{64,0},{80,16},{96,32},{112,48}... | collective-permute-start | bytes 589832 | tf_op jit(solution)/shard_map/ppermute | solution.py:325
  148.7 2.4 %collective-permute-start.11 = (bf16[2,384,128]{2,1,0:T(8,128)(2,1)S(1)}, bf16[2,384,128]{2,1,0:T(8,128)(2,1)S(1)}, u32[]{:S(2)}, u32[]{:S(2)}) collective-permute-start(bf16[2,384,128]{2,1,0:T(8,128)(2,1)S(1)} %get-tuple-element.34), channel_id=1, source_target_pairs={{0,64},{16,80},{32,96},{48,112},{64,128},{80,144},{96,160},{112,17... | collective-permute-start | bytes 589832 | tf_op jit(solution)/shard_map/ppermute | solution.py:325
  151.1 2.1 %collective-permute-done.10 = bf16[4,384,128]{2,1,0:T(8,128)(2,1)S(1)} collective-permute-done((bf16[4,384,128]{2,1,0:T(8,128)(2,1)}, bf16[4,384,128]{2,1,0:T(8,128)(2,1)S(1)}, u32[]{:S(2)}, u32[]{:S(2)}) %collective-permute-start.10) | collective-permute-done | bytes 393248 | tf_op jit(solution)/shard_map/ppermute | solution.py:325
  153.2 8.6 %collective-permute-done.9 = bf16[4,384,128]{2,1,0:T(8,128)(2,1)S(1)} collective-permute-done((bf16[4,384,128]{2,1,0:T(8,128)(2,1)}, bf16[4,384,128]{2,1,0:T(8,128)(2,1)S(1)}, u32[]{:S(2)}, u32[]{:S(2)}) %collective-permute-start.9) | collective-permute-done | bytes 393248 | tf_op jit(solution)/shard_map/ppermute | solution.py:325
  161.8 0.0 collective-permute-done.14
  161.8 0.9 fusion.5
  162.7 1.9 collective-permute-start.12
  164.7 10.8 %collective-permute-start.13 = (bf16[384,128]{1,0:T(8,128)(2,1)}, bf16[384,128]{1,0:T(8,128)(2,1)}, u32[]{:S(2)}, u32[]{:S(2)}) collective-permute-start(bf16[384,128]{1,0:T(8,128)(2,1)} %get-tuple-element.31), channel_id=1, source_target_pairs={{0,256},{16,272},{32,288},{48,304},{64,320},{80,336},{96,352},{112... | collective-permute-start | bytes 294920 | tf_op jit(solution)/shard_map/ppermute | solution.py:325
  175.5 5.4 %collective-permute-start.15 = (bf16[384,128]{1,0:T(8,128)(2,1)}, bf16[384,128]{1,0:T(8,128)(2,1)}, u32[]{:S(2)}, u32[]{:S(2)}) collective-permute-start(bf16[384,128]{1,0:T(8,128)(2,1)} %get-tuple-element.30), channel_id=1, source_target_pairs={{0,384},{16,400},{32,416},{48,432},{64,448},{80,464},{96,480},{112... | collective-permute-start | bytes 294920 | tf_op jit(solution)/shard_map/ppermute | solution.py:325
  180.9 1.8 shard_map.79.back_ref
  182.7 0.0 all-to-all-done.1
  182.7 1.5 copy-done
  184.2 4.4 %shard_map.81 = bf16[128,4096]{1,0:T(8,128)(2,1)} custom-call(bf16[256,640]{1,0:T(8,128)(2,1)} %shard_map.79.back_ref, bf16[640,2048]{1,0:T(8,128)(2,1)} %bitcast.29), custom_call_target="tpu_custom_call" | custom-call | flops 671088640 | bytes 4194304 | tf_op jit(solution)/shard_map/pallas_call | solution.py:434
  188.6 8.7 %collective-permute-done.15 = bf16[384,128]{1,0:T(8,128)(2,1)} collective-permute-done((bf16[384,128]{1,0:T(8,128)(2,1)}, bf16[384,128]{1,0:T(8,128)(2,1)}, u32[]{:S(2)}, u32[]{:S(2)}) %collective-permute-start.15) | collective-permute-done | bytes 98336 | tf_op jit(solution)/shard_map/ppermute | solution.py:325
  197.3 1.3 fusion.2
  198.6 0.8 copy.8
  (34 shorter events, 0.2 us)
Async XLA Ops:
  8.7 10.4 %copy-start.12 = (bf16[1,128,384]{2,1,0:T(8,128)(2,1)S(1)}, bf16[1,128,384]{2,1,0:T(8,128)(2,1)}, u32[]{:S(2)}) copy-start(bf16[1,128,384]{2,1,0:T(8,128)(2,1)} %param.10) | copy-start | bytes 294916
  8.7 73.9 %copy-start.13 = (s32[1,1,32]{2,1,0:T(1,128)S(1)}, s32[1,1,32]{2,1,0:T(1,128)}, u32[]{:S(2)}) copy-start(s32[1,1,32]{2,1,0:T(1,128)} %param.11) | copy-start | bytes 388
  8.7 76.8 %all-to-all-start = ((bf16[16,40,4096]{2,1,0:T(8,128)(2,1)}), bf16[16,40,4096]{2,1,0:T(8,128)(2,1)}, u32[]{:S(2)}, u32[]{:S(2)}) async-start(bf16[16,40,4096]{2,1,0:T(8,128)(2,1)} %bitcast.27), calls=%async_computation | async-start | bytes 10485760 | tf_op jit(solution)/shard_map/all_to_all | solution.py:279
  19.1 3.2 %collective-permute-start = (bf16[128,384]{1,0:T(8,128)(2,1)S(1)}, bf16[128,384]{1,0:T(8,128)(2,1)S(1)}, u32[]{:S(2)}, u32[]{:S(2)}) collective-permute-start(bf16[128,384]{1,0:T(8,128)(2,1)S(1)} %bitcast.30), channel_id=1, source_target_pairs={{0,16},{16,0},{32,48},{48,32},{64,80},{80,64},{96,112},{112,96},{1... | collective-permute-start | bytes 294920 | tf_op jit(solution)/shard_map/ppermute | solution.py:294
  22.3 63.2 %copy-start.2 = (bf16[2,128,384]{2,1,0:T(8,128)(2,1)}, bf16[2,128,384]{2,1,0:T(8,128)(2,1)S(1)}, u32[]{:S(2)}) copy-start(bf16[2,128,384]{2,1,0:T(8,128)(2,1)S(1)} %pad_maximum_fusion.1.refs_0_) | copy-start | bytes 589828
  22.3 12.3 %collective-permute-start.1 = (bf16[2,128,384]{2,1,0:T(8,128)(2,1)S(1)}, bf16[2,128,384]{2,1,0:T(8,128)(2,1)S(1)}, u32[]{:S(2)}, u32[]{:S(2)}) collective-permute-start(bf16[2,128,384]{2,1,0:T(8,128)(2,1)S(1)} %pad_maximum_fusion.1.refs_0_), channel_id=1, source_target_pairs={{0,32},{16,496},{32,64},{48,16},{64,96},{80,48},{96,128},{112,80},... | collective-permute-start | bytes 589832 | tf_op jit(solution)/shard_map/ppermute | solution.py:290
  34.6 14.2 %collective-permute-start.2 = (bf16[2,128,384]{2,1,0:T(8,128)(2,1)S(1)}, bf16[2,128,384]{2,1,0:T(8,128)(2,1)S(1)}, u32[]{:S(2)}, u32[]{:S(2)}) collective-permute-start(bf16[2,128,384]{2,1,0:T(8,128)(2,1)S(1)} %collective-permute-done.1), channel_id=1, source_target_pairs={{0,128},{16,400},{32,160},{48,432},{64,192},{80,464},{96,224},{112... | collective-permute-start | bytes 589832 | tf_op jit(solution)/shard_map/ppermute | solution.py:290
  48.9 16.0 %collective-permute-start.3 = (bf16[4,128,384]{2,1,0:T(8,128)(2,1)S(1)}, bf16[4,128,384]{2,1,0:T(8,128)(2,1)S(1)}, u32[]{:S(2)}, u32[]{:S(2)}) collective-permute-start(bf16[4,128,384]{2,1,0:T(8,128)(2,1)S(1)} %pad_maximum_fusion), channel_id=1, source_target_pairs={{0,64},{16,464},{32,96},{48,496},{64,128},{80,16},{96,160},{112,48... | collective-permute-start | bytes 1179656 | tf_op jit(solution)/shard_map/ppermute | solution.py:290
  65.0 20.5 %copy-start.1 = (bf16[8,128,384]{2,1,0:T(8,128)(2,1)}, bf16[8,128,384]{2,1,0:T(8,128)(2,1)S(1)}, u32[]{:S(2)}) copy-start(bf16[8,128,384]{2,1,0:T(8,128)(2,1)S(1)} %constant_dynamic-update-slice_fusion.refs_1_) | copy-start | bytes 2359300
  65.0 15.1 %collective-permute-start.4 = (bf16[8,128,384]{2,1,0:T(8,128)(2,1)S(1)}, bf16[8,128,384]{2,1,0:T(8,128)(2,1)S(1)}, u32[]{:S(2)}, u32[]{:S(2)}) collective-permute-start(bf16[8,128,384]{2,1,0:T(8,128)(2,1)S(1)} %constant_dynamic-update-slice_fusion.refs_1_), channel_id=1, source_target_pairs={{0,32},{16,496},{32,64},{48,16},{64,96},{80,48},{96,128},{112,80},... | collective-permute-start | bytes 2359304 | tf_op jit(solution)/shard_map/ppermute | solution.py:290
  66.9 16.2 %collective-permute-start.5 = (bf16[8,128,384]{2,1,0:T(8,128)(2,1)S(1)}, bf16[8,128,384]{2,1,0:T(8,128)(2,1)S(1)}, u32[]{:S(2)}, u32[]{:S(2)}) collective-permute-start(bf16[8,128,384]{2,1,0:T(8,128)(2,1)S(1)} %constant_dynamic-update-slice_fusion.refs_1_), channel_id=1, source_target_pairs={{0,16},{16,0},{32,48},{48,32},{64,80},{80,64},{96,112},{112,96},{1... | collective-permute-start | bytes 2359304 | tf_op jit(solution)/shard_map/ppermute | solution.py:294
  80.1 5.4 %copy-start.3 = (bf16[8,128,384]{2,1,0:T(8,128)(2,1)}, bf16[8,128,384]{2,1,0:T(8,128)(2,1)S(1)}, u32[]{:S(2)}) copy-start(bf16[8,128,384]{2,1,0:T(8,128)(2,1)S(1)} %collective-permute-done.4.refs_2_) | copy-start | bytes 2359300
  80.1 4.2 %collective-permute-start.6 = (bf16[8,128,384]{2,1,0:T(8,128)(2,1)S(1)}, bf16[8,128,384]{2,1,0:T(8,128)(2,1)S(1)}, u32[]{:S(2)}, u32[]{:S(2)}) collective-permute-start(bf16[8,128,384]{2,1,0:T(8,128)(2,1)S(1)} %collective-permute-done.4.refs_2_), channel_id=1, source_target_pairs={{0,16},{16,0},{32,48},{48,32},{64,80},{80,64},{96,112},{112,96},{1... | collective-permute-start | bytes 2359304 | tf_op jit(solution)/shard_map/ppermute | solution.py:294
  83.2 2.3 %copy-start.4 = (bf16[8,128,384]{2,1,0:T(8,128)(2,1)}, bf16[8,128,384]{2,1,0:T(8,128)(2,1)S(1)}, u32[]{:S(2)}) copy-start(bf16[8,128,384]{2,1,0:T(8,128)(2,1)S(1)} %collective-permute-done.5.refs_3_) | copy-start | bytes 2359300
  84.3 1.3 copy-start.5
  100.6 4.4 %collective-permute-start.7 = (bf16[8,384,128]{2,1,0:T(8,128)(2,1)}, bf16[8,384,128]{2,1,0:T(8,128)(2,1)S(1)}, u32[]{:S(2)}, u32[]{:S(2)}) collective-permute-start(bf16[8,384,128]{2,1,0:T(8,128)(2,1)} %get-tuple-element.17), channel_id=1, source_target_pairs={{0,16},{16,0},{32,48},{48,32},{64,80},{80,64},{96,112},{112,96},{1... | collective-permute-start | bytes 2359304 | tf_op jit(solution)/shard_map/ppermute | solution.py:294
  107.3 36.9 %copy-start.6 = (bf16[8,384,128]{2,1,0:T(8,128)(2,1)S(1)}, bf16[8,384,128]{2,1,0:T(8,128)(2,1)}, u32[]{:S(2)}) copy-start(bf16[8,384,128]{2,1,0:T(8,128)(2,1)} %get-tuple-element.15) | copy-start | bytes 2359300
  114.5 68.2 %all-to-all-start.1 = ((bf16[16,40,2048]{2,1,0:T(8,128)(2,1)}), bf16[16,40,2048]{2,1,0:T(8,128)(2,1)S(1)}, u32[]{:S(2)}, u32[]{:S(2)}) async-start(bf16[16,40,2048]{2,1,0:T(8,128)(2,1)} %bitcast.28), calls=%async_computation.1 | async-start | bytes 5242880 | tf_op jit(solution)/shard_map/all_to_all | solution.py:279
  123.6 20.5 %collective-permute-start.8 = (bf16[8,384,128]{2,1,0:T(8,128)(2,1)}, bf16[8,384,128]{2,1,0:T(8,128)(2,1)S(1)}, u32[]{:S(2)}, u32[]{:S(2)}) collective-permute-start(bf16[8,384,128]{2,1,0:T(8,128)(2,1)} %get-tuple-element.20), channel_id=1, source_target_pairs={{0,16},{16,0},{32,48},{48,32},{64,80},{80,64},{96,112},{112,96},{1... | collective-permute-start | bytes 2359304 | tf_op jit(solution)/shard_map/ppermute | solution.py:294
  125.6 27.6 %collective-permute-start.10 = (bf16[4,384,128]{2,1,0:T(8,128)(2,1)}, bf16[4,384,128]{2,1,0:T(8,128)(2,1)S(1)}, u32[]{:S(2)}, u32[]{:S(2)}) collective-permute-start(bf16[4,384,128]{2,1,0:T(8,128)(2,1)} %get-tuple-element.22), channel_id=1, source_target_pairs={{0,480},{16,496},{32,0},{48,16},{64,32},{80,48},{96,64},{112,80},{... | collective-permute-start | bytes 1179656 | tf_op jit(solution)/shard_map/ppermute | solution.py:325
  142.2 19.5 %collective-permute-start.9 = (bf16[4,384,128]{2,1,0:T(8,128)(2,1)}, bf16[4,384,128]{2,1,0:T(8,128)(2,1)S(1)}, u32[]{:S(2)}, u32[]{:S(2)}) collective-permute-start(bf16[4,384,128]{2,1,0:T(8,128)(2,1)} %get-tuple-element.21), channel_id=1, source_target_pairs={{0,32},{16,48},{32,64},{48,80},{64,96},{80,112},{96,128},{112,144}... | collective-permute-start | bytes 1179656 | tf_op jit(solution)/shard_map/ppermute | solution.py:325
  144.2 17.6 %copy-start.7 = (bf16[8,384,128]{2,1,0:T(8,128)(2,1)}, bf16[8,384,128]{2,1,0:T(8,128)(2,1)S(1)}, u32[]{:S(2)}) copy-start(bf16[8,384,128]{2,1,0:T(8,128)(2,1)S(1)} %collective-permute-done.8) | copy-start | bytes 2359300
  144.3 17.4 %collective-permute-start.14 = (bf16[2,384,128]{2,1,0:T(8,128)(2,1)S(1)}, bf16[2,384,128]{2,1,0:T(8,128)(2,1)S(1)}, u32[]{:S(2)}, u32[]{:S(2)}) collective-permute-start(bf16[2,384,128]{2,1,0:T(8,128)(2,1)S(1)} %get-tuple-element.33), channel_id=1, source_target_pairs={{0,448},{16,464},{32,480},{48,496},{64,0},{80,16},{96,32},{112,48}... | collective-permute-start | bytes 589832 | tf_op jit(solution)/shard_map/ppermute | solution.py:325
  148.7 13.1 %collective-permute-start.11 = (bf16[2,384,128]{2,1,0:T(8,128)(2,1)S(1)}, bf16[2,384,128]{2,1,0:T(8,128)(2,1)S(1)}, u32[]{:S(2)}, u32[]{:S(2)}) collective-permute-start(bf16[2,384,128]{2,1,0:T(8,128)(2,1)S(1)} %get-tuple-element.34), channel_id=1, source_target_pairs={{0,64},{16,80},{32,96},{48,112},{64,128},{80,144},{96,160},{112,17... | collective-permute-start | bytes 589832 | tf_op jit(solution)/shard_map/ppermute | solution.py:325
  153.1 9.6 %copy-start.8 = (bf16[4,384,128]{2,1,0:T(8,128)(2,1)}, bf16[4,384,128]{2,1,0:T(8,128)(2,1)S(1)}, u32[]{:S(2)}) copy-start(bf16[4,384,128]{2,1,0:T(8,128)(2,1)S(1)} %collective-permute-done.10) | copy-start | bytes 1179652
  161.8 1.0 copy-start.9
  161.8 2.9 %copy-start.10 = (bf16[2,384,128]{2,1,0:T(8,128)(2,1)}, bf16[2,384,128]{2,1,0:T(8,128)(2,1)S(1)}, u32[]{:S(2)}) copy-start(bf16[2,384,128]{2,1,0:T(8,128)(2,1)S(1)} %collective-permute-done.14) | copy-start | bytes 589828
  161.8 2.9 %copy-start.11 = (bf16[2,384,128]{2,1,0:T(8,128)(2,1)}, bf16[2,384,128]{2,1,0:T(8,128)(2,1)S(1)}, u32[]{:S(2)}) copy-start(bf16[2,384,128]{2,1,0:T(8,128)(2,1)S(1)} %collective-permute-done.11) | copy-start | bytes 589828
  162.7 25.9 %collective-permute-start.12 = (bf16[384,128]{1,0:T(8,128)(2,1)}, bf16[384,128]{1,0:T(8,128)(2,1)S(1)}, u32[]{:S(2)}, u32[]{:S(2)}) collective-permute-start(bf16[384,128]{1,0:T(8,128)(2,1)} %get-tuple-element.32), channel_id=1, source_target_pairs={{0,128},{16,144},{32,160},{48,176},{64,192},{80,208},{96,224},{112... | collective-permute-start | bytes 294920 | tf_op jit(solution)/shard_map/ppermute | solution.py:325
  164.7 23.9 %collective-permute-start.13 = (bf16[384,128]{1,0:T(8,128)(2,1)}, bf16[384,128]{1,0:T(8,128)(2,1)}, u32[]{:S(2)}, u32[]{:S(2)}) collective-permute-start(bf16[384,128]{1,0:T(8,128)(2,1)} %get-tuple-element.31), channel_id=1, source_target_pairs={{0,256},{16,272},{32,288},{48,304},{64,320},{80,336},{96,352},{112... | collective-permute-start | bytes 294920 | tf_op jit(solution)/shard_map/ppermute | solution.py:325
  175.5 21.8 %collective-permute-start.15 = (bf16[384,128]{1,0:T(8,128)(2,1)}, bf16[384,128]{1,0:T(8,128)(2,1)}, u32[]{:S(2)}, u32[]{:S(2)}) collective-permute-start(bf16[384,128]{1,0:T(8,128)(2,1)} %get-tuple-element.30), channel_id=1, source_target_pairs={{0,384},{16,400},{32,416},{48,432},{64,448},{80,464},{96,480},{112... | collective-permute-start | bytes 294920 | tf_op jit(solution)/shard_map/ppermute | solution.py:325
  182.7 1.5 copy-start

commit v2 on v0

--- a/solution.py
+++ b/solution.py
@@ -13,7 +13,7 @@
 TOK, WIDTH, EXPERTS, CAP, HID = 128, 4096, 16, 20, 128
 HALF = WIDTH // 2
 ROWS = 2 * EXPERTS * CAP
-STEPS = 4
+STEPS = 1
 COLS = HALF // STEPS
 BLOCKS = WIDTH // 128
 
@@ -101,8 +101,11 @@
 
 
 def stack_rows(table_ref, weights, step, h, start, stop):
-    first = 4 * step + BLOCKS // 2 * h
-    return jnp.concatenate([weights[table_ref[first + j], :, start:stop] for j in range(4)], 0)
+    count = COLS // 128
+    first = count * step + BLOCKS // 2 * h
+    return jnp.concatenate(
+        [weights[table_ref[first + j], :, start:stop] for j in range(count)], 0
+    )
 
 
 def piece_copies(pieces, weights, sems):
@@ -406,7 +409,7 @@
         2,
     )(table, info, received, *gathered)
     paired = (even.astype(F32) + swap(give_even).astype(F32)).astype(BF16)
-    paired, both_grad, give_odd = lax.optimization_barrier((paired, both_grad, give_odd))
+    paired, both_grad = lax.optimization_barrier((paired, both_grad))
     final = scatter_sum(paired, odd, give_odd)
     slot_grad = call(
         slot_grad_kernel,

time: 203 us -> 196 us (0.966)
  Pallas kernels: 36.8 us -> 30.3 us
    pallas_call x1, Pallas kernels: 15.3 us -> 12.5 us  [per_device(): call(expert_kernel, 3 * STEPS, in_place * 6, [whole((ROWS, 2 * HID))] + [...]
    pallas_call x1, Pallas kernels: 8.17 us -> 5.56 us  [per_device(): call(place_kernel, 2 * STEPS, [whole((2, TOK)), whole((2, TOK)), columns(...]
where the time goes in v2:
time: 196 us; the launch traced here: 195 us
  starting transfers between devices  105 us (54%)
  waiting for transfers between devices  50.6 us (26%)
  Pallas kernels  30.3 us (15%)
  other arithmetic  5.42 us (3%)
  local copies, waits for them, and re-layouts  2.49 us (1%)
    ppermute x8, starting transfers between devices, hop(): return lax.ppermute(value, 'rep', turn)  59.9 us
    ppermute x8, waiting for transfers between devices, hop(): return lax.ppermute(value, 'rep', turn)  45.1 us
    ppermute x6, starting transfers between devices, swap(): lax.ppermute(value, 'rep', [(i, i ^ 1) for i in range(lax.axis_size('rep'...  33.2 us
    pallas_call x1, Pallas kernels, per_device(): call(expert_kernel, 3 * STEPS, in_place * 6, [whole((ROWS, 2 * HID))] + [...  12.5 us
    all_to_all x2, starting transfers between devices, exchange(): lax.all_to_all(rows.reshape(EXPERTS, 2 * CAP, -1), 'exp', split_axis=0, c...  12.3 us
    pallas_call x1, Pallas kernels, per_device(): call(slot_grad_kernel, STEPS, [whole((ROWS, 2 * HID))] + in_place * 5, co...  6.71 us
    pallas_call x1, Pallas kernels, per_device(): call(place_kernel, 2 * STEPS, [whole((2, TOK)), whole((2, TOK)), columns(...  5.56 us
    ppermute x6, waiting for transfers between devices, swap(): lax.ppermute(value, 'rep', [(i, i ^ 1) for i in range(lax.axis_size('rep'...  4.33 us
  transfers between devices with their start and end apart: 16, of which 12 were waited for; matrix products, arithmetic and copies ran while one was open for 1% of the time, Pallas kernels for 3%

profile of v2, /device:TPU:1, one launch (start us, length us, event | category | flops | bytes accessed | tf_op | source)
XLA Modules:
  0.0 195.1 jit_solution(14201900120290875301)
XLA Ops:
  0.6 5.6 %shard_map.77 = bf16[640,4096]{1,0:T(8,128)(2,1)} custom-call(s32[2,128]{1,0:T(2,128)} %bitcast.16, f32[2,128]{1,0:T(2,128)} %bitcast.18, bf16[128,4096]{1,0:T(8,128)(2,1)} %x_high_ref.1, bf16[128,4096]{1,0:T(8,128)(2,1)} %x_high_ref.1, bf16[128,4096]{1,0:T(8,128)(2,1)} %dy_high_ref.1, bf16[128,4096]{1,0:T(8,128)(2,1)} %dy_high_ref.1), custom_call_target="tpu_custom_call" | custom-call | flops 1342177280 | bytes 8388608 | tf_op jit(solution)/shard_map/pallas_call | solution.py:356
  6.2 7.8 %all-to-all-start = ((bf16[16,40,4096]{2,1,0:T(8,128)(2,1)}), bf16[16,40,4096]{2,1,0:T(8,128)(2,1)}, u32[]{:S(2)}, u32[]{:S(2)}) async-start(bf16[16,40,4096]{2,1,0:T(8,128)(2,1)} %bitcast.11), calls=%async_computation | async-start | bytes 10485760 | tf_op jit(solution)/shard_map/all_to_all | solution.py:282
  13.9 0.0 copy-start.8
  14.0 5.7 %collective-permute-start = (bf16[128,384]{1,0:T(8,128)(2,1)S(1)}, bf16[128,384]{1,0:T(8,128)(2,1)S(1)}, u32[]{:S(2)}, u32[]{:S(2)}) collective-permute-start(bf16[128,384]{1,0:T(8,128)(2,1)S(1)} %bitcast.14), channel_id=1, source_target_pairs={{0,16},{16,0},{32,48},{48,32},{64,80},{80,64},{96,112},{112,96},{1... | collective-permute-start | bytes 294920 | tf_op jit(solution)/shard_map/ppermute | solution.py:297
  19.7 0.9 collective-permute-done
  20.6 0.0 copy-start.2
  20.7 8.3 %collective-permute-start.1 = (bf16[2,128,384]{2,1,0:T(8,128)(2,1)S(1)}, bf16[2,128,384]{2,1,0:T(8,128)(2,1)S(1)}, u32[]{:S(2)}, u32[]{:S(2)}) collective-permute-start(bf16[2,128,384]{2,1,0:T(8,128)(2,1)S(1)} %pad_maximum_fusion.1.refs_0_), channel_id=1, source_target_pairs={{0,32},{16,496},{32,64},{48,16},{64,96},{80,48},{96,128},{112,80},... | collective-permute-start | bytes 589832 | tf_op jit(solution)/shard_map/ppermute | solution.py:293
  28.9 2.6 %collective-permute-done.1 = bf16[2,128,384]{2,1,0:T(8,128)(2,1)S(1)} collective-permute-done((bf16[2,128,384]{2,1,0:T(8,128)(2,1)S(1)}, bf16[2,128,384]{2,1,0:T(8,128)(2,1)S(1)}, u32[]{:S(2)}, u32[]{:S(2)}) %collective-permute-start.1) | collective-permute-done | bytes 196640 | tf_op jit(solution)/shard_map/ppermute | solution.py:293
  31.5 5.5 %collective-permute-start.2 = (bf16[2,128,384]{2,1,0:T(8,128)(2,1)S(1)}, bf16[2,128,384]{2,1,0:T(8,128)(2,1)S(1)}, u32[]{:S(2)}, u32[]{:S(2)}) collective-permute-start(bf16[2,128,384]{2,1,0:T(8,128)(2,1)S(1)} %collective-permute-done.1), channel_id=1, source_target_pairs={{0,128},{16,400},{32,160},{48,432},{64,192},{80,464},{96,224},{112... | collective-permute-start | bytes 589832 | tf_op jit(solution)/shard_map/ppermute | solution.py:293
  37.1 6.8 %collective-permute-done.2 = bf16[2,128,384]{2,1,0:T(8,128)(2,1)S(1)} collective-permute-done((bf16[2,128,384]{2,1,0:T(8,128)(2,1)S(1)}, bf16[2,128,384]{2,1,0:T(8,128)(2,1)S(1)}, u32[]{:S(2)}, u32[]{:S(2)}) %collective-permute-start.2) | collective-permute-done | bytes 196640 | tf_op jit(solution)/shard_map/ppermute | solution.py:293
  43.9 7.8 %collective-permute-start.3 = (bf16[4,128,384]{2,1,0:T(8,128)(2,1)S(1)}, bf16[4,128,384]{2,1,0:T(8,128)(2,1)S(1)}, u32[]{:S(2)}, u32[]{:S(2)}) collective-permute-start(bf16[4,128,384]{2,1,0:T(8,128)(2,1)S(1)} %pad_maximum_fusion), channel_id=1, source_target_pairs={{0,64},{16,464},{32,96},{48,496},{64,128},{80,16},{96,160},{112,48... | collective-permute-start | bytes 1179656 | tf_op jit(solution)/shard_map/ppermute | solution.py:293
  51.8 8.7 %collective-permute-done.3 = bf16[4,128,384]{2,1,0:T(8,128)(2,1)S(1)} collective-permute-done((bf16[4,128,384]{2,1,0:T(8,128)(2,1)S(1)}, bf16[4,128,384]{2,1,0:T(8,128)(2,1)S(1)}, u32[]{:S(2)}, u32[]{:S(2)}) %collective-permute-start.3) | collective-permute-done | bytes 393248 | tf_op jit(solution)/shard_map/ppermute | solution.py:293
  60.4 0.1 constant_dynamic-update-slice_fusion.refs_1_
  60.5 0.0 copy-start.1
  60.5 2.0 %collective-permute-start.4 = (bf16[8,128,384]{2,1,0:T(8,128)(2,1)S(1)}, bf16[8,128,384]{2,1,0:T(8,128)(2,1)S(1)}, u32[]{:S(2)}, u32[]{:S(2)}) collective-permute-start(bf16[8,128,384]{2,1,0:T(8,128)(2,1)S(1)} %constant_dynamic-update-slice_fusion.refs_1_), channel_id=1, source_target_pairs={{0,32},{16,496},{32,64},{48,16},{64,96},{80,48},{96,128},{112,80},... | collective-permute-start | bytes 2359304 | tf_op jit(solution)/shard_map/ppermute | solution.py:293
  62.5 4.9 %collective-permute-start.5 = (bf16[8,128,384]{2,1,0:T(8,128)(2,1)S(1)}, bf16[8,128,384]{2,1,0:T(8,128)(2,1)S(1)}, u32[]{:S(2)}, u32[]{:S(2)}) collective-permute-start(bf16[8,128,384]{2,1,0:T(8,128)(2,1)S(1)} %constant_dynamic-update-slice_fusion.refs_1_), channel_id=1, source_target_pairs={{0,16},{16,0},{32,48},{48,32},{64,80},{80,64},{96,112},{112,96},{1... | collective-permute-start | bytes 2359304 | tf_op jit(solution)/shard_map/ppermute | solution.py:297
  67.4 6.2 %collective-permute-done.4.refs_2_ = bf16[8,128,384]{2,1,0:T(8,128)(2,1)S(1)} collective-permute-done((bf16[8,128,384]{2,1,0:T(8,128)(2,1)S(1)}, bf16[8,128,384]{2,1,0:T(8,128)(2,1)S(1)}, u32[]{:S(2)}, u32[]{:S(2)}) %collective-permute-start.4) | collective-permute-done | bytes 786464 | tf_op jit(solution)/shard_map/ppermute | solution.py:293
  73.7 6.9 %collective-permute-start.6 = (bf16[8,128,384]{2,1,0:T(8,128)(2,1)S(1)}, bf16[8,128,384]{2,1,0:T(8,128)(2,1)S(1)}, u32[]{:S(2)}, u32[]{:S(2)}) collective-permute-start(bf16[8,128,384]{2,1,0:T(8,128)(2,1)S(1)} %collective-permute-done.4.refs_2_), channel_id=1, source_target_pairs={{0,16},{16,0},{32,48},{48,32},{64,80},{80,64},{96,112},{112,96},{1... | collective-permute-start | bytes 2359304 | tf_op jit(solution)/shard_map/ppermute | solution.py:297
  80.6 0.6 compare_select_fusion.7.table_ref
  81.2 0.6 pad_add_fusion.info_ref
  81.8 0.0 collective-permute-done.5.refs_3_
  81.8 0.7 collective-permute-done.6.refs_4_
  82.5 1.2 all-to-all-done
  83.7 12.5 %shard_map.78 = (bf16[640,256]{1,0:T(8,128)(2,1)}, bf16[7,384,128]{2,1,0:T(8,128)(2,1)}, bf16[8,384,128]{2,1,0:T(8,128)(2,1)}, bf16[2,384,128]{2,1,0:T(8,128)(2,...) custom-call(s32[32]{0:T(128)} %compare_select_fusion.7.table_ref, s32[64]{0:T(128)} %pad_add_fusion.info_ref, ...), custom_call_target="tpu_custom_call" | custom-call | flops 4026531840 | bytes 16777216 | tf_op jit(solution)/shard_map/pallas_call | solution.py:392
  96.2 6.9 %collective-permute-start.8 = (bf16[7,384,128]{2,1,0:T(8,128)(2,1)}, bf16[7,384,128]{2,1,0:T(8,128)(2,1)S(1)}, u32[]{:S(2)}, u32[]{:S(2)}) collective-permute-start(bf16[7,384,128]{2,1,0:T(8,128)(2,1)} %get-tuple-element.15), channel_id=1, source_target_pairs={{0,16},{16,0},{32,48},{48,32},{64,80},{80,64},{96,112},{112,96},{1... | collective-permute-start | bytes 2064392 | tf_op jit(solution)/shard_map/ppermute | solution.py:297
  103.1 1.8 collective-permute-done.8
  104.9 2.1 %add_convert_fusion = bf16[7,384,128]{2,1,0:T(8,128)(2,1)} fusion(bf16[7,384,128]{2,1,0:T(8,128)(2,1)S(1)} %collective-permute-done.8, bf16[7,384,128]{2,1,0:T(8,128)(2,1)} %get-tuple-element.14), kind=kLoop, calls=%fused_computation | loop fusion | flops 1376256 | bytes 2064384 | tf_op jit(solution)/shard_map/convert_element_type | solution.py:411
  107.0 6.7 %shard_map.80 = bf16[640,2048]{1,0:T(8,128)(2,1)} custom-call(s32[32]{0:T(128)} %compare_select_fusion.7.table_ref, bf16[640,256]{1,0:T(8,128)(2,1)} %get-tuple-element.18.both_ref, bf16[2,128,384]{2,1,0:T(8,128)(2,1)} %copy-done.2, bf16[8,128,384]{2,1,0:T(8,128)(2,1)} %copy-done.1, bf16[8,128,384]{2,1,0:T(8,128)(2,1)} %copy-done.3, ...), custom_call_target="tpu_custom_call" | custom-call | flops 1342177280 | bytes 6291456 | tf_op jit(solution)/shard_map/pallas_call | solution.py:414
  113.7 4.5 %all-to-all-start.1 = ((bf16[16,40,2048]{2,1,0:T(8,128)(2,1)}), bf16[16,40,2048]{2,1,0:T(8,128)(2,1)S(1)}, u32[]{:S(2)}, u32[]{:S(2)}) async-start(bf16[16,40,2048]{2,1,0:T(8,128)(2,1)} %bitcast.12), calls=%async_computation.1 | async-start | bytes 5242880 | tf_op jit(solution)/shard_map/all_to_all | solution.py:282
  118.3 2.6 %collective-permute-start.7 = (bf16[8,384,128]{2,1,0:T(8,128)(2,1)}, bf16[8,384,128]{2,1,0:T(8,128)(2,1)S(1)}, u32[]{:S(2)}, u32[]{:S(2)}) collective-permute-start(bf16[8,384,128]{2,1,0:T(8,128)(2,1)} %get-tuple-element.13), channel_id=1, source_target_pairs={{0,16},{16,0},{32,48},{48,32},{64,80},{80,64},{96,112},{112,96},{1... | collective-permute-start | bytes 2359304 | tf_op jit(solution)/shard_map/ppermute | solution.py:297
  120.8 16.4 %collective-permute-start.9 = (bf16[7,384,128]{2,1,0:T(8,128)(2,1)}, bf16[7,384,128]{2,1,0:T(8,128)(2,1)S(1)}, u32[]{:S(2)}, u32[]{:S(2)}) collective-permute-start(bf16[7,384,128]{2,1,0:T(8,128)(2,1)} %add_convert_fusion), channel_id=1, source_target_pairs={{0,32},{16,496},{32,64},{48,16},{64,96},{80,48},{96,128},{112,80},... | collective-permute-start | bytes 2064392 | tf_op jit(solution)/shard_map/ppermute | solution.py:293
  137.3 0.0 collective-permute-done.7
  137.3 8.2 %collective-permute-done.9 = bf16[7,384,128]{2,1,0:T(8,128)(2,1)S(1)} collective-permute-done((bf16[7,384,128]{2,1,0:T(8,128)(2,1)}, bf16[7,384,128]{2,1,0:T(8,128)(2,1)S(1)}, u32[]{:S(2)}, u32[]{:S(2)}) %collective-permute-start.9) | collective-permute-done | bytes 688160 | tf_op jit(solution)/shard_map/ppermute | solution.py:293
  145.4 0.1 add_convert_fusion.1
  145.6 4.4 %collective-permute-start.10 = (bf16[4,384,128]{2,1,0:T(8,128)(2,1)S(1)}, bf16[4,384,128]{2,1,0:T(8,128)(2,1)S(1)}, u32[]{:S(2)}, u32[]{:S(2)}) collective-permute-start(bf16[4,384,128]{2,1,0:T(8,128)(2,1)S(1)} %add_convert_fusion.1), channel_id=1, source_target_pairs={{0,64},{16,464},{32,96},{48,496},{64,128},{80,16},{96,160},{112,48... | collective-permute-start | bytes 1179656 | tf_op jit(solution)/shard_map/ppermute | solution.py:293
  150.0 7.8 %collective-permute-done.10 = bf16[4,384,128]{2,1,0:T(8,128)(2,1)S(1)} collective-permute-done((bf16[4,384,128]{2,1,0:T(8,128)(2,1)S(1)}, bf16[4,384,128]{2,1,0:T(8,128)(2,1)S(1)}, u32[]{:S(2)}, u32[]{:S(2)}) %collective-permute-start.10) | collective-permute-done | bytes 393248 | tf_op jit(solution)/shard_map/ppermute | solution.py:293
  157.9 0.1 add_convert_fusion.3
  158.0 6.4 %collective-permute-start.11 = (bf16[2,384,128]{2,1,0:T(8,128)(2,1)S(1)}, bf16[2,384,128]{2,1,0:T(8,128)(2,1)S(1)}, u32[]{:S(2)}, u32[]{:S(2)}) collective-permute-start(bf16[2,384,128]{2,1,0:T(8,128)(2,1)S(1)} %add_convert_fusion.3), channel_id=1, source_target_pairs={{0,128},{16,400},{32,160},{48,432},{64,192},{80,464},{96,224},{112... | collective-permute-start | bytes 589832 | tf_op jit(solution)/shard_map/ppermute | solution.py:293
  164.4 4.8 %collective-permute-done.11 = bf16[2,384,128]{2,1,0:T(8,128)(2,1)S(1)} collective-permute-done((bf16[2,384,128]{2,1,0:T(8,128)(2,1)S(1)}, bf16[2,384,128]{2,1,0:T(8,128)(2,1)S(1)}, u32[]{:S(2)}, u32[]{:S(2)}) %collective-permute-start.11) | collective-permute-done | bytes 196640 | tf_op jit(solution)/shard_map/ppermute | solution.py:293
  169.2 0.8 add_convert_fusion.2
  170.0 9.0 %collective-permute-start.12 = (bf16[2,384,128]{2,1,0:T(8,128)(2,1)}, bf16[2,384,128]{2,1,0:T(8,128)(2,1)S(1)}, u32[]{:S(2)}, u32[]{:S(2)}) collective-permute-start(bf16[2,384,128]{2,1,0:T(8,128)(2,1)} %add_convert_fusion.2), channel_id=1, source_target_pairs={{0,32},{16,496},{32,64},{48,16},{64,96},{80,48},{96,128},{112,80},... | collective-permute-start | bytes 589832 | tf_op jit(solution)/shard_map/ppermute | solution.py:293
  179.0 1.8 shard_map.79.back_ref
  180.8 1.5 copy-done
  182.3 3.8 %shard_map.81 = bf16[128,4096]{1,0:T(8,128)(2,1)} custom-call(bf16[256,640]{1,0:T(8,128)(2,1)} %shard_map.79.back_ref, bf16[640,2048]{1,0:T(8,128)(2,1)} %bitcast.13), custom_call_target="tpu_custom_call" | custom-call | flops 671088640 | bytes 4194304 | tf_op jit(solution)/shard_map/pallas_call | solution.py:426
  186.2 1.0 convert_add_fusion
  187.1 6.2 %collective-permute-start.13 = (bf16[1,384,128]{2,1,0:T(8,128)(2,1)S(1)}, bf16[1,384,128]{2,1,0:T(8,128)(2,1)S(1)}, u32[]{:S(2)}, u32[]{:S(2)}) collective-permute-start(bf16[1,384,128]{2,1,0:T(8,128)(2,1)S(1)} %slice.73), channel_id=1, source_target_pairs={{0,16},{16,0},{32,48},{48,32},{64,80},{80,64},{96,112},{112,96},{1... | collective-permute-start | bytes 294920 | tf_op jit(solution)/shard_map/ppermute | solution.py:297
  193.3 0.9 collective-permute-done.13
  194.3 0.8 copy.8
  (23 shorter events, 0.2 us)
Async XLA Ops:
  6.2 7.8 %copy-start.7 = (bf16[1,128,384]{2,1,0:T(8,128)(2,1)S(1)}, bf16[1,128,384]{2,1,0:T(8,128)(2,1)}, u32[]{:S(2)}) copy-start(bf16[1,128,384]{2,1,0:T(8,128)(2,1)} %param.10) | copy-start | bytes 294916
  6.2 77.5 %all-to-all-start = ((bf16[16,40,4096]{2,1,0:T(8,128)(2,1)}), bf16[16,40,4096]{2,1,0:T(8,128)(2,1)}, u32[]{:S(2)}, u32[]{:S(2)}) async-start(bf16[16,40,4096]{2,1,0:T(8,128)(2,1)} %bitcast.11), calls=%async_computation | async-start | bytes 10485760 | tf_op jit(solution)/shard_map/all_to_all | solution.py:282
  13.9 67.2 %copy-start.8 = (s32[1,1,32]{2,1,0:T(1,128)S(1)}, s32[1,1,32]{2,1,0:T(1,128)}, u32[]{:S(2)}) copy-start(s32[1,1,32]{2,1,0:T(1,128)} %param.11) | copy-start | bytes 388
  14.0 6.6 %collective-permute-start = (bf16[128,384]{1,0:T(8,128)(2,1)S(1)}, bf16[128,384]{1,0:T(8,128)(2,1)S(1)}, u32[]{:S(2)}, u32[]{:S(2)}) collective-permute-start(bf16[128,384]{1,0:T(8,128)(2,1)S(1)} %bitcast.14), channel_id=1, source_target_pairs={{0,16},{16,0},{32,48},{48,32},{64,80},{80,64},{96,112},{112,96},{1... | collective-permute-start | bytes 294920 | tf_op jit(solution)/shard_map/ppermute | solution.py:297
  20.6 63.0 %copy-start.2 = (bf16[2,128,384]{2,1,0:T(8,128)(2,1)}, bf16[2,128,384]{2,1,0:T(8,128)(2,1)S(1)}, u32[]{:S(2)}) copy-start(bf16[2,128,384]{2,1,0:T(8,128)(2,1)S(1)} %pad_maximum_fusion.1.refs_0_) | copy-start | bytes 589828
  20.7 10.9 %collective-permute-start.1 = (bf16[2,128,384]{2,1,0:T(8,128)(2,1)S(1)}, bf16[2,128,384]{2,1,0:T(8,128)(2,1)S(1)}, u32[]{:S(2)}, u32[]{:S(2)}) collective-permute-start(bf16[2,128,384]{2,1,0:T(8,128)(2,1)S(1)} %pad_maximum_fusion.1.refs_0_), channel_id=1, source_target_pairs={{0,32},{16,496},{32,64},{48,16},{64,96},{80,48},{96,128},{112,80},... | collective-permute-start | bytes 589832 | tf_op jit(solution)/shard_map/ppermute | solution.py:293
  31.5 12.3 %collective-permute-start.2 = (bf16[2,128,384]{2,1,0:T(8,128)(2,1)S(1)}, bf16[2,128,384]{2,1,0:T(8,128)(2,1)S(1)}, u32[]{:S(2)}, u32[]{:S(2)}) collective-permute-start(bf16[2,128,384]{2,1,0:T(8,128)(2,1)S(1)} %collective-permute-done.1), channel_id=1, source_target_pairs={{0,128},{16,400},{32,160},{48,432},{64,192},{80,464},{96,224},{112... | collective-permute-start | bytes 589832 | tf_op jit(solution)/shard_map/ppermute | solution.py:293
  43.9 16.6 %collective-permute-start.3 = (bf16[4,128,384]{2,1,0:T(8,128)(2,1)S(1)}, bf16[4,128,384]{2,1,0:T(8,128)(2,1)S(1)}, u32[]{:S(2)}, u32[]{:S(2)}) collective-permute-start(bf16[4,128,384]{2,1,0:T(8,128)(2,1)S(1)} %pad_maximum_fusion), channel_id=1, source_target_pairs={{0,64},{16,464},{32,96},{48,496},{64,128},{80,16},{96,160},{112,48... | collective-permute-start | bytes 1179656 | tf_op jit(solution)/shard_map/ppermute | solution.py:293
  60.5 23.2 %copy-start.1 = (bf16[8,128,384]{2,1,0:T(8,128)(2,1)}, bf16[8,128,384]{2,1,0:T(8,128)(2,1)S(1)}, u32[]{:S(2)}) copy-start(bf16[8,128,384]{2,1,0:T(8,128)(2,1)S(1)} %constant_dynamic-update-slice_fusion.refs_1_) | copy-start | bytes 2359300
  60.5 13.1 %collective-permute-start.4 = (bf16[8,128,384]{2,1,0:T(8,128)(2,1)S(1)}, bf16[8,128,384]{2,1,0:T(8,128)(2,1)S(1)}, u32[]{:S(2)}, u32[]{:S(2)}) collective-permute-start(bf16[8,128,384]{2,1,0:T(8,128)(2,1)S(1)} %constant_dynamic-update-slice_fusion.refs_1_), channel_id=1, source_target_pairs={{0,32},{16,496},{32,64},{48,16},{64,96},{80,48},{96,128},{112,80},... | collective-permute-start | bytes 2359304 | tf_op jit(solution)/shard_map/ppermute | solution.py:293
  62.5 19.2 %collective-permute-start.5 = (bf16[8,128,384]{2,1,0:T(8,128)(2,1)S(1)}, bf16[8,128,384]{2,1,0:T(8,128)(2,1)S(1)}, u32[]{:S(2)}, u32[]{:S(2)}) collective-permute-start(bf16[8,128,384]{2,1,0:T(8,128)(2,1)S(1)} %constant_dynamic-update-slice_fusion.refs_1_), channel_id=1, source_target_pairs={{0,16},{16,0},{32,48},{48,32},{64,80},{80,64},{96,112},{112,96},{1... | collective-permute-start | bytes 2359304 | tf_op jit(solution)/shard_map/ppermute | solution.py:297
  73.7 10.0 %copy-start.3 = (bf16[8,128,384]{2,1,0:T(8,128)(2,1)}, bf16[8,128,384]{2,1,0:T(8,128)(2,1)S(1)}, u32[]{:S(2)}) copy-start(bf16[8,128,384]{2,1,0:T(8,128)(2,1)S(1)} %collective-permute-done.4.refs_2_) | copy-start | bytes 2359300
  73.7 8.8 %collective-permute-start.6 = (bf16[8,128,384]{2,1,0:T(8,128)(2,1)S(1)}, bf16[8,128,384]{2,1,0:T(8,128)(2,1)S(1)}, u32[]{:S(2)}, u32[]{:S(2)}) collective-permute-start(bf16[8,128,384]{2,1,0:T(8,128)(2,1)S(1)} %collective-permute-done.4.refs_2_), channel_id=1, source_target_pairs={{0,16},{16,0},{32,48},{48,32},{64,80},{80,64},{96,112},{112,96},{1... | collective-permute-start | bytes 2359304 | tf_op jit(solution)/shard_map/ppermute | solution.py:297
  81.8 1.9 copy-start.4
  82.5 1.2 copy-start.5
  96.2 8.7 %collective-permute-start.8 = (bf16[7,384,128]{2,1,0:T(8,128)(2,1)}, bf16[7,384,128]{2,1,0:T(8,128)(2,1)S(1)}, u32[]{:S(2)}, u32[]{:S(2)}) collective-permute-start(bf16[7,384,128]{2,1,0:T(8,128)(2,1)} %get-tuple-element.15), channel_id=1, source_target_pairs={{0,16},{16,0},{32,48},{48,32},{64,80},{80,64},{96,112},{112,96},{1... | collective-permute-start | bytes 2064392 | tf_op jit(solution)/shard_map/ppermute | solution.py:297
  113.7 31.7 %copy-start.6 = (bf16[8,384,128]{2,1,0:T(8,128)(2,1)S(1)}, bf16[8,384,128]{2,1,0:T(8,128)(2,1)}, u32[]{:S(2)}) copy-start(bf16[8,384,128]{2,1,0:T(8,128)(2,1)} %get-tuple-element.12) | copy-start | bytes 2359300
  113.7 67.1 %all-to-all-start.1 = ((bf16[16,40,2048]{2,1,0:T(8,128)(2,1)}), bf16[16,40,2048]{2,1,0:T(8,128)(2,1)S(1)}, u32[]{:S(2)}, u32[]{:S(2)}) async-start(bf16[16,40,2048]{2,1,0:T(8,128)(2,1)} %bitcast.12), calls=%async_computation.1 | async-start | bytes 5242880 | tf_op jit(solution)/shard_map/all_to_all | solution.py:282
  118.3 19.0 %collective-permute-start.7 = (bf16[8,384,128]{2,1,0:T(8,128)(2,1)}, bf16[8,384,128]{2,1,0:T(8,128)(2,1)S(1)}, u32[]{:S(2)}, u32[]{:S(2)}) collective-permute-start(bf16[8,384,128]{2,1,0:T(8,128)(2,1)} %get-tuple-element.13), channel_id=1, source_target_pairs={{0,16},{16,0},{32,48},{48,32},{64,80},{80,64},{96,112},{112,96},{1... | collective-permute-start | bytes 2359304 | tf_op jit(solution)/shard_map/ppermute | solution.py:297
  120.8 24.6 %collective-permute-start.9 = (bf16[7,384,128]{2,1,0:T(8,128)(2,1)}, bf16[7,384,128]{2,1,0:T(8,128)(2,1)S(1)}, u32[]{:S(2)}, u32[]{:S(2)}) collective-permute-start(bf16[7,384,128]{2,1,0:T(8,128)(2,1)} %add_convert_fusion), channel_id=1, source_target_pairs={{0,32},{16,496},{32,64},{48,16},{64,96},{80,48},{96,128},{112,80},... | collective-permute-start | bytes 2064392 | tf_op jit(solution)/shard_map/ppermute | solution.py:293
  145.6 12.3 %collective-permute-start.10 = (bf16[4,384,128]{2,1,0:T(8,128)(2,1)S(1)}, bf16[4,384,128]{2,1,0:T(8,128)(2,1)S(1)}, u32[]{:S(2)}, u32[]{:S(2)}) collective-permute-start(bf16[4,384,128]{2,1,0:T(8,128)(2,1)S(1)} %add_convert_fusion.1), channel_id=1, source_target_pairs={{0,64},{16,464},{32,96},{48,496},{64,128},{80,16},{96,160},{112,48... | collective-permute-start | bytes 1179656 | tf_op jit(solution)/shard_map/ppermute | solution.py:293
  158.0 11.2 %collective-permute-start.11 = (bf16[2,384,128]{2,1,0:T(8,128)(2,1)S(1)}, bf16[2,384,128]{2,1,0:T(8,128)(2,1)S(1)}, u32[]{:S(2)}, u32[]{:S(2)}) collective-permute-start(bf16[2,384,128]{2,1,0:T(8,128)(2,1)S(1)} %add_convert_fusion.3), channel_id=1, source_target_pairs={{0,128},{16,400},{32,160},{48,432},{64,192},{80,464},{96,224},{112... | collective-permute-start | bytes 589832 | tf_op jit(solution)/shard_map/ppermute | solution.py:293
  170.0 16.1 %collective-permute-start.12 = (bf16[2,384,128]{2,1,0:T(8,128)(2,1)}, bf16[2,384,128]{2,1,0:T(8,128)(2,1)S(1)}, u32[]{:S(2)}, u32[]{:S(2)}) collective-permute-start(bf16[2,384,128]{2,1,0:T(8,128)(2,1)} %add_convert_fusion.2), channel_id=1, source_target_pairs={{0,32},{16,496},{32,64},{48,16},{64,96},{80,48},{96,128},{112,80},... | collective-permute-start | bytes 589832 | tf_op jit(solution)/shard_map/ppermute | solution.py:293
  180.8 1.5 copy-start
  187.1 7.1 %collective-permute-start.13 = (bf16[1,384,128]{2,1,0:T(8,128)(2,1)S(1)}, bf16[1,384,128]{2,1,0:T(8,128)(2,1)S(1)}, u32[]{:S(2)}, u32[]{:S(2)}) collective-permute-start(bf16[1,384,128]{2,1,0:T(8,128)(2,1)S(1)} %slice.73), channel_id=1, source_target_pairs={{0,16},{16,0},{32,48},{48,32},{64,80},{80,64},{96,112},{112,96},{1... | collective-permute-start | bytes 294920 | tf_op jit(solution)/shard_map/ppermute | solution.py:297

commit v3 on v2

--- a/solution.py
+++ b/solution.py
@@ -14,6 +14,7 @@
 HALF = WIDTH // 2
 ROWS = 2 * EXPERTS * CAP
 STEPS = 1
+PARTS = 2
 COLS = HALF // STEPS
 BLOCKS = WIDTH // 128
 
@@ -93,9 +94,9 @@
     back_ref[...] = placement(*hits(ids_ref[...])).T.astype(BF16)
 
 
-def join_halves(acc, width):
-    upper, _ = half_of_row((ROWS, width), 0)
-    own = jnp.where(upper, acc[:, width:], acc[:, :width])
+def join_halves(low, high):
+    upper, _ = half_of_row(low.shape, 0)
+    own = jnp.where(upper, high, low)
     other = jnp.where(upper, pltpu.roll(own, CAP, 0), pltpu.roll(own, ROWS - CAP, 0))
     return own + other
 
@@ -117,101 +118,80 @@
     return copies
 
 
-def column_copy(recv_ref, slots, sems, i):
-    at = pl.ds(pl.multiple_of(i * COLS, COLS), COLS)
-    return pltpu.make_async_copy(recv_ref.at[:, at], slots.at[:, at], sems.at[i])
-
-
 def expert_kernel(table_ref, info_ref, recv_ref, *refs):
     gathered, both_ref, pieces = refs[:5], refs[5], refs[6:11]
-    slots, weights, turned_ref, gate_up, down, sems, w_sems = refs[11:]
-    step = pl.program_id(0)
-
-    @pl.when(step == 0)
-    def _():
-        copies = piece_copies(gathered, weights, w_sems)
-        for copy in copies:
-            copy.start()
-        for i in range(2 * STEPS):
-            column_copy(recv_ref, slots, sems, i).start()
-        gate_up[...] = jnp.zeros_like(gate_up)
-        down[...] = jnp.zeros_like(down)
-        for copy in copies:
-            copy.wait()
-
-    @pl.when(step < 2 * STEPS)
-    def _():
-        column_copy(recv_ref, slots, sems, step).wait()
-
-    @pl.when(step < STEPS)
-    def _():
-        x = slots[:, pl.ds(pl.multiple_of(step * COLS, COLS), COLS)]
+    slots, weights, turned_ref, staged, sems, w_sems, out_sems = refs[11:]
+    w_copies = piece_copies(gathered, weights, w_sems)
+    for copy in w_copies:
+        copy.start()
+    halves = []
+    for i in range(2):
+        at = pl.ds(i * HALF, HALF)
+        halves.append(pltpu.make_async_copy(recv_ref.at[:, at], slots.at[:, at], sems.at[i]))
+        halves[-1].start()
+    for copy in w_copies:
+        copy.wait()
+    halves[0].wait()
+    x = slots[:, :HALF]
+    gate_up = [
+        jnp.dot(x, stack_rows(table_ref, weights, 0, h, 0, 2 * HID), preferred_element_type=F32)
+        for h in range(2)
+    ]
+    joined = join_halves(*gate_up)
+    gate_pre = joined[:, :HID]
+    up_pre = joined[:, HID:]
+    sigmoid_g = jax.nn.sigmoid(gate_pre)
+    silu_val = gate_pre * sigmoid_g
+    silu_slope = sigmoid_g * (1.0 + gate_pre * (1.0 - sigmoid_g))
+    hidden = silu_val * up_pre
+    halves[1].wait()
+    dy = slots[:, HALF:]
+    w_down = [stack_rows(table_ref, weights, 0, h, 2 * HID, 3 * HID) for h in range(2)]
+    down = jnp.dot(dy, jnp.concatenate(w_down, 1), preferred_element_type=F32)
+    hid_grad = join_halves(down[:, :HID], down[:, HID:])
+    gate_grad = hid_grad * up_pre * silu_slope
+    up_grad = hid_grad * silu_val
+    both_ref[:, :HID] = gate_grad.astype(BF16)
+    both_ref[:, HID:] = up_grad.astype(BF16)
+    upper, _ = half_of_row((HID, ROWS), 1)
+    for i, value in enumerate((gate_grad, up_grad, hidden)):
+        turned = value.T
+        turned_ref[i * HID : (i + 1) * HID, :] = jnp.where(upper, 0.0, turned).astype(BF16)
+        turned_ref[(i + 3) * HID : (i + 4) * HID, :] = jnp.where(upper, turned, 0.0).astype(BF16)
+    spans = tuple(zip(pieces, (0, 7, 15, 17, 24), (7, 15, 17, 24, 32)))
+    for part in range(PARTS):
+        columns_of = slice(part * HALF // PARTS, (part + 1) * HALF // PARTS)
         for h in range(2):
-            gate_up[:, 2 * HID * h : 2 * HID * (h + 1)] += jnp.dot(
-                x,
-                stack_rows(table_ref, weights, step, h, 0, 2 * HID),
+            base = 3 * HID * h
+            proj = jnp.dot(
+                turned_ref[base : base + 2 * HID, :],
+                slots[:, columns_of],
                 preferred_element_type=F32,
             )
-
-    @pl.when((step >= STEPS) & (step < 2 * STEPS))
-    def _():
-        dy = slots[:, pl.ds(pl.multiple_of(step * COLS, COLS), COLS)]
-        w_down = [
-            stack_rows(table_ref, weights, step - STEPS, h, 2 * HID, 3 * HID) for h in range(2)
-        ]
-        down[...] += jnp.dot(dy, jnp.concatenate(w_down, 1), preferred_element_type=F32)
-
-    @pl.when(step == 2 * STEPS - 1)
-    def _():
-        joined = join_halves(gate_up[...], 2 * HID)
-        hid_grad = join_halves(down[...], HID)
-        gate_pre = joined[:, :HID]
-        up_pre = joined[:, HID:]
-        sigmoid_g = jax.nn.sigmoid(gate_pre)
-        silu_val = gate_pre * sigmoid_g
-        silu_slope = sigmoid_g * (1.0 + gate_pre * (1.0 - sigmoid_g))
-        gate_grad = hid_grad * up_pre * silu_slope
-        up_grad = hid_grad * silu_val
-        hidden = silu_val * up_pre
-        both_ref[:, :HID] = gate_grad.astype(BF16)
-        both_ref[:, HID:] = up_grad.astype(BF16)
-        upper, _ = half_of_row((HID, ROWS), 1)
-        for i, value in enumerate((gate_grad, up_grad, hidden)):
-            turned = value.T
-            turned_ref[i * HID : (i + 1) * HID, :] = jnp.where(upper, 0.0, turned).astype(BF16)
-            turned_ref[(i + 3) * HID : (i + 4) * HID, :] = jnp.where(upper, turned, 0.0).astype(
-                BF16
+            down = jnp.dot(
+                turned_ref[base + 2 * HID : base + 3 * HID, :],
+                slots[:, HALF + columns_of.start : HALF + columns_of.stop],
+                preferred_element_type=F32,
             )
-
-    @pl.when(step >= 2 * STEPS)
-    def _():
-        weight_grad(info_ref, step - 2 * STEPS, slots, turned_ref, pieces)
-
-
-def weight_grad(info_ref, step, slots, turned_ref, pieces):
-    at = pl.multiple_of(step * COLS, COLS)
-    x = slots[:, pl.ds(at, COLS)]
-    dy = slots[:, pl.ds(pl.multiple_of(at + HALF, COLS), COLS)]
-    spans = tuple(zip(pieces, (0, 7, 15, 17, 24), (7, 15, 17, 24, 32)))
-    for h in range(2):
-        base = 3 * HID * h
-        proj = jnp.dot(turned_ref[base : base + 2 * HID, :], x, preferred_element_type=F32)
-        down = jnp.dot(
-            turned_ref[base + 2 * HID : base + 3 * HID, :], dy, preferred_element_type=F32
-        )
-        for i in range(COLS // 128):
-            block = step * (COLS // 128) + i + h * (BLOCKS // 2)
-            keep = info_ref[block].astype(F32)
-            place = info_ref[BLOCKS + block]
-            top = (proj[:, i * 128 : i * 128 + 128] * keep).astype(BF16)
-            bottom = (down[:, i * 128 : i * 128 + 128] * keep).astype(BF16)
-
-            def put(ref, first):
-                ref[place - first, : 2 * HID, :] = top
-                ref[place - first, 2 * HID :, :] = bottom
-
-            for ref, first, last in spans:
-                pl.when((place >= first) & (place < last))(functools.partial(put, ref, first))
+            for i in range(HALF // PARTS // 128):
+                block = columns_of.start // 128 + i + h * (BLOCKS // 2)
+                keep = info_ref[block].astype(F32)
+                place = info_ref[BLOCKS + block]
+                lanes = slice(i * 128, i * 128 + 128)
+                staged[block, : 2 * HID, :] = (proj[:, lanes] * keep).astype(BF16)
+                staged[block, 2 * HID :, :] = (down[:, lanes] * keep).astype(BF16)
+
+                def send(ref, first):
+                    pltpu.make_async_copy(
+                        staged.at[block], ref.at[place - first], out_sems.at[block]
+                    ).start()
+
+                for ref, first, last in spans:
+                    pl.when((place >= first) & (place < last))(
+                        functools.partial(send, ref, first)
+                    )
+    for block in range(BLOCKS):
+        pltpu.make_async_copy(staged.at[block], pieces[0].at[0], out_sems.at[block]).wait()
 
 
 def slot_grad_kernel(table_ref, both_ref, *refs):
@@ -334,17 +314,18 @@
     return near, odd, even, swap(odd), swap(even)
 
 
+def add(*parts):
+    return functools.reduce(jnp.add, [part.astype(F32) for part in parts])
+
+
 def scatter_sum(even, odd, give_odd):
-    def add(*parts):
-        return functools.reduce(jnp.add, [part.astype(F32) for part in parts])
-
     one = hop(even, 1)
     got = swap(give_odd)
     last = lax.pad(one, jnp.zeros((), BF16), ((-4, 1, 0), (0, 0, 0), (0, 0, 0)))
     second = add(odd[4:], got[4:], last).astype(BF16)
     two = hop(second, 2)
-    four = hop(add(odd[2:4], got[2:4], one[2:4], two[2:]).astype(BF16), 4)
-    return hop(add(odd[:2], got[:2], one[:2], two[:2], four).astype(BF16), 1)
+    five = hop(add(odd[2:4], got[2:4], one[2:4], two[2:]).astype(BF16), 5)
+    return five, hop(add(odd[:2], got[:2], one[:2], two[:2]).astype(BF16), 1)
 
 
 def per_device(tokens, grad_out, gates, expert_ids, w_all, touched):
@@ -391,9 +372,9 @@
     shares = [(n, 3 * HID, 128) for n in (7, 8, 2, 7, 8)]
     both_grad, even, odd, here, give_even, give_odd = call(
         expert_kernel,
-        3 * STEPS,
+        1,
         in_place * 6,
-        [whole((ROWS, 2 * HID))] + [whole(share) for share in shares],
+        [whole((ROWS, 2 * HID))] + in_place * 5,
         [sds((ROWS, 2 * HID), BF16)] + [sds(share, BF16) for share in shares],
         2 * ROWS * HALF * 12 * HID,
         16 * mbytes,
@@ -401,10 +382,10 @@
             pltpu.VMEM((ROWS, WIDTH), BF16),
             weights[0],
             pltpu.VMEM((6 * HID, ROWS), BF16),
-            pltpu.VMEM((ROWS, 4 * HID), F32),
-            pltpu.VMEM((ROWS, 2 * HID), F32),
-            pltpu.SemaphoreType.DMA((2 * STEPS,)),
+            pltpu.VMEM((BLOCKS, 3 * HID, 128), BF16),
+            pltpu.SemaphoreType.DMA((2,)),
             weights[1],
+            pltpu.SemaphoreType.DMA((BLOCKS,)),
         ],
         2,
     )(table, info, received, *gathered)
@@ -433,7 +414,7 @@
         4 * mbytes,
     )(back, returned)
     final, token_grad = lax.optimization_barrier((final, token_grad))
-    total = here.astype(F32) + final.astype(F32)
+    total = add(here, *final)
     owned = total[:1] + swap(total[1:].astype(BF16)).astype(F32)
     return (token_grad, jnp.swapaxes(owned, 1, 2))
 

time: 196 us -> 188 us (0.959)
  starting transfers between devices: 105 us -> 101 us
    ppermute x8, starting transfers between devices: 59.9 us -> 56.7 us  [hop(): return lax.ppermute(value, 'rep', turn)]
  transfers between devices with their start and end apart: 16 -> 16, of which waited for: 12 -> 13; matrix products, arithmetic and copies ran while one was open for 1% -> 1% of each run, Pallas kernels for 3% -> 3%
where the time goes in v3:
time: 188 us; the launch traced here: 187 us
  starting transfers between devices  101 us (54%)
  waiting for transfers between devices  48.9 us (26%)
  Pallas kernels  29.6 us (16%)
  other arithmetic  4.66 us (2%)
  local copies, waits for them, and re-layouts  2.5 us (1%)
    ppermute x8, starting transfers between devices, hop(): return lax.ppermute(value, 'rep', turn)  56.7 us
    ppermute x8, waiting for transfers between devices, hop(): return lax.ppermute(value, 'rep', turn)  43.3 us
    ppermute x6, starting transfers between devices, swap(): lax.ppermute(value, 'rep', [(i, i ^ 1) for i in range(lax.axis_size('rep'...  31.6 us
    all_to_all x2, starting transfers between devices, exchange(): lax.all_to_all(rows.reshape(EXPERTS, 2 * CAP, -1), 'exp', split_axis=0, c...  12.3 us
    pallas_call x1, Pallas kernels, per_device(): call(expert_kernel, 1, in_place * 6, [whole((ROWS, 2 * HID))] + in_place...  11.8 us
    pallas_call x1, Pallas kernels, per_device(): call(slot_grad_kernel, STEPS, [whole((ROWS, 2 * HID))] + in_place * 5, co...  6.72 us
    pallas_call x1, Pallas kernels, per_device(): call(place_kernel, 2 * STEPS, [whole((2, TOK)), whole((2, TOK)), columns(...  5.5 us
    ppermute x6, waiting for transfers between devices, swap(): lax.ppermute(value, 'rep', [(i, i ^ 1) for i in range(lax.axis_size('rep'...  4.4 us
  transfers between devices with their start and end apart: 16, of which 13 were waited for; matrix products, arithmetic and copies ran while one was open for 1% of the time, Pallas kernels for 3%

profile of v3, /device:TPU:1, one launch (start us, length us, event | category | flops | bytes accessed | tf_op | source)
XLA Modules:
  0.0 187.1 jit_solution(1155239073471016581)
XLA Ops:
  0.6 5.5 %shard_map.77 = bf16[640,4096]{1,0:T(8,128)(2,1)} custom-call(s32[2,128]{1,0:T(2,128)} %bitcast.16, f32[2,128]{1,0:T(2,128)} %bitcast.18, bf16[128,4096]{1,0:T(8,128)(2,1)} %x_high_ref.1, bf16[128,4096]{1,0:T(8,128)(2,1)} %x_high_ref.1, bf16[128,4096]{1,0:T(8,128)(2,1)} %dy_high_ref.1, bf16[128,4096]{1,0:T(8,128)(2,1)} %dy_high_ref.1), custom_call_target="tpu_custom_call" | custom-call | flops 1342177280 | bytes 8388608 | tf_op jit(solution)/shard_map/pallas_call | solution.py:337
  6.1 7.7 %all-to-all-start = ((bf16[16,40,4096]{2,1,0:T(8,128)(2,1)}), bf16[16,40,4096]{2,1,0:T(8,128)(2,1)}, u32[]{:S(2)}, u32[]{:S(2)}) async-start(bf16[16,40,4096]{2,1,0:T(8,128)(2,1)} %bitcast.11), calls=%async_computation | async-start | bytes 10485760 | tf_op jit(solution)/shard_map/all_to_all | solution.py:262
  13.9 0.0 copy-start.9
  13.9 5.7 %collective-permute-start = (bf16[128,384]{1,0:T(8,128)(2,1)S(1)}, bf16[128,384]{1,0:T(8,128)(2,1)S(1)}, u32[]{:S(2)}, u32[]{:S(2)}) collective-permute-start(bf16[128,384]{1,0:T(8,128)(2,1)S(1)} %bitcast.14), channel_id=1, source_target_pairs={{0,16},{16,0},{32,48},{48,32},{64,80},{80,64},{96,112},{112,96},{1... | collective-permute-start | bytes 294920 | tf_op jit(solution)/shard_map/ppermute | solution.py:277
  19.6 0.9 collective-permute-done
  20.6 0.0 copy-start.2
  20.6 8.3 %collective-permute-start.1 = (bf16[2,128,384]{2,1,0:T(8,128)(2,1)S(1)}, bf16[2,128,384]{2,1,0:T(8,128)(2,1)S(1)}, u32[]{:S(2)}, u32[]{:S(2)}) collective-permute-start(bf16[2,128,384]{2,1,0:T(8,128)(2,1)S(1)} %pad_maximum_fusion.1.refs_0_), channel_id=1, source_target_pairs={{0,32},{16,496},{32,64},{48,16},{64,96},{80,48},{96,128},{112,80},... | collective-permute-start | bytes 589832 | tf_op jit(solution)/shard_map/ppermute | solution.py:273
  28.9 2.6 %collective-permute-done.1 = bf16[2,128,384]{2,1,0:T(8,128)(2,1)S(1)} collective-permute-done((bf16[2,128,384]{2,1,0:T(8,128)(2,1)S(1)}, bf16[2,128,384]{2,1,0:T(8,128)(2,1)S(1)}, u32[]{:S(2)}, u32[]{:S(2)}) %collective-permute-start.1) | collective-permute-done | bytes 196640 | tf_op jit(solution)/shard_map/ppermute | solution.py:273
  31.5 5.5 %collective-permute-start.2 = (bf16[2,128,384]{2,1,0:T(8,128)(2,1)S(1)}, bf16[2,128,384]{2,1,0:T(8,128)(2,1)S(1)}, u32[]{:S(2)}, u32[]{:S(2)}) collective-permute-start(bf16[2,128,384]{2,1,0:T(8,128)(2,1)S(1)} %collective-permute-done.1), channel_id=1, source_target_pairs={{0,128},{16,400},{32,160},{48,432},{64,192},{80,464},{96,224},{112... | collective-permute-start | bytes 589832 | tf_op jit(solution)/shard_map/ppermute | solution.py:273
  37.0 6.8 %collective-permute-done.2 = bf16[2,128,384]{2,1,0:T(8,128)(2,1)S(1)} collective-permute-done((bf16[2,128,384]{2,1,0:T(8,128)(2,1)S(1)}, bf16[2,128,384]{2,1,0:T(8,128)(2,1)S(1)}, u32[]{:S(2)}, u32[]{:S(2)}) %collective-permute-start.2) | collective-permute-done | bytes 196640 | tf_op jit(solution)/shard_map/ppermute | solution.py:273
  43.8 7.8 %collective-permute-start.3 = (bf16[4,128,384]{2,1,0:T(8,128)(2,1)S(1)}, bf16[4,128,384]{2,1,0:T(8,128)(2,1)S(1)}, u32[]{:S(2)}, u32[]{:S(2)}) collective-permute-start(bf16[4,128,384]{2,1,0:T(8,128)(2,1)S(1)} %pad_maximum_fusion), channel_id=1, source_target_pairs={{0,64},{16,464},{32,96},{48,496},{64,128},{80,16},{96,160},{112,48... | collective-permute-start | bytes 1179656 | tf_op jit(solution)/shard_map/ppermute | solution.py:273
  51.7 8.7 %collective-permute-done.3 = bf16[4,128,384]{2,1,0:T(8,128)(2,1)S(1)} collective-permute-done((bf16[4,128,384]{2,1,0:T(8,128)(2,1)S(1)}, bf16[4,128,384]{2,1,0:T(8,128)(2,1)S(1)}, u32[]{:S(2)}, u32[]{:S(2)}) %collective-permute-start.3) | collective-permute-done | bytes 393248 | tf_op jit(solution)/shard_map/ppermute | solution.py:273
  60.4 0.1 constant_dynamic-update-slice_fusion.refs_1_
  60.5 0.0 copy-start.1
  60.5 2.0 %collective-permute-start.4 = (bf16[8,128,384]{2,1,0:T(8,128)(2,1)S(1)}, bf16[8,128,384]{2,1,0:T(8,128)(2,1)S(1)}, u32[]{:S(2)}, u32[]{:S(2)}) collective-permute-start(bf16[8,128,384]{2,1,0:T(8,128)(2,1)S(1)} %constant_dynamic-update-slice_fusion.refs_1_), channel_id=1, source_target_pairs={{0,32},{16,496},{32,64},{48,16},{64,96},{80,48},{96,128},{112,80},... | collective-permute-start | bytes 2359304 | tf_op jit(solution)/shard_map/ppermute | solution.py:273
  62.5 4.9 %collective-permute-start.5 = (bf16[8,128,384]{2,1,0:T(8,128)(2,1)S(1)}, bf16[8,128,384]{2,1,0:T(8,128)(2,1)S(1)}, u32[]{:S(2)}, u32[]{:S(2)}) collective-permute-start(bf16[8,128,384]{2,1,0:T(8,128)(2,1)S(1)} %constant_dynamic-update-slice_fusion.refs_1_), channel_id=1, source_target_pairs={{0,16},{16,0},{32,48},{48,32},{64,80},{80,64},{96,112},{112,96},{1... | collective-permute-start | bytes 2359304 | tf_op jit(solution)/shard_map/ppermute | solution.py:277
  67.4 6.2 %collective-permute-done.4.refs_2_ = bf16[8,128,384]{2,1,0:T(8,128)(2,1)S(1)} collective-permute-done((bf16[8,128,384]{2,1,0:T(8,128)(2,1)S(1)}, bf16[8,128,384]{2,1,0:T(8,128)(2,1)S(1)}, u32[]{:S(2)}, u32[]{:S(2)}) %collective-permute-start.4) | collective-permute-done | bytes 786464 | tf_op jit(solution)/shard_map/ppermute | solution.py:273
  73.6 6.9 %collective-permute-start.6 = (bf16[8,128,384]{2,1,0:T(8,128)(2,1)S(1)}, bf16[8,128,384]{2,1,0:T(8,128)(2,1)S(1)}, u32[]{:S(2)}, u32[]{:S(2)}) collective-permute-start(bf16[8,128,384]{2,1,0:T(8,128)(2,1)S(1)} %collective-permute-done.4.refs_2_), channel_id=1, source_target_pairs={{0,16},{16,0},{32,48},{48,32},{64,80},{80,64},{96,112},{112,96},{1... | collective-permute-start | bytes 2359304 | tf_op jit(solution)/shard_map/ppermute | solution.py:277
  80.5 0.6 compare_select_fusion.7.table_ref
  81.2 0.7 pad_add_fusion.info_ref
  81.8 0.0 collective-permute-done.5.refs_3_
  81.8 0.6 collective-permute-done.6.refs_4_
  82.4 1.2 all-to-all-done
  83.6 11.8 %shard_map.78 = (bf16[640,256]{1,0:T(8,128)(2,1)}, bf16[7,384,128]{2,1,0:T(8,128)(2,1)}, bf16[8,384,128]{2,1,0:T(8,128)(2,1)}, bf16[2,384,128]{2,1,0:T(8,128)(2,...) custom-call(s32[32]{0:T(128)} %compare_select_fusion.7.table_ref, s32[64]{0:T(128)} %pad_add_fusion.info_ref, ...), custom_call_target="tpu_custom_call" | custom-call | flops 4026531840 | bytes 16777216 | tf_op jit(solution)/shard_map/pallas_call | solution.py:373
  95.5 6.8 %collective-permute-start.8 = (bf16[7,384,128]{2,1,0:T(8,128)(2,1)}, bf16[7,384,128]{2,1,0:T(8,128)(2,1)S(1)}, u32[]{:S(2)}, u32[]{:S(2)}) collective-permute-start(bf16[7,384,128]{2,1,0:T(8,128)(2,1)} %get-tuple-element.16), channel_id=1, source_target_pairs={{0,16},{16,0},{32,48},{48,32},{64,80},{80,64},{96,112},{112,96},{1... | collective-permute-start | bytes 2064392 | tf_op jit(solution)/shard_map/ppermute | solution.py:277
  102.3 2.0 %collective-permute-done.8 = bf16[7,384,128]{2,1,0:T(8,128)(2,1)S(1)} collective-permute-done((bf16[7,384,128]{2,1,0:T(8,128)(2,1)}, bf16[7,384,128]{2,1,0:T(8,128)(2,1)S(1)}, u32[]{:S(2)}, u32[]{:S(2)}) %collective-permute-start.8) | collective-permute-done | bytes 688160 | tf_op jit(solution)/shard_map/ppermute | solution.py:277
  104.3 2.1 %add_convert_fusion = bf16[7,384,128]{2,1,0:T(8,128)(2,1)} fusion(bf16[7,384,128]{2,1,0:T(8,128)(2,1)S(1)} %collective-permute-done.8, bf16[7,384,128]{2,1,0:T(8,128)(2,1)} %get-tuple-element.15), kind=kLoop, calls=%fused_computation | loop fusion | flops 1376256 | bytes 2064384 | tf_op jit(solution)/shard_map/convert_element_type | solution.py:392
  106.4 6.7 %shard_map.80 = bf16[640,2048]{1,0:T(8,128)(2,1)} custom-call(s32[32]{0:T(128)} %compare_select_fusion.7.table_ref, bf16[640,256]{1,0:T(8,128)(2,1)} %get-tuple-element.19.both_ref, bf16[2,128,384]{2,1,0:T(8,128)(2,1)} %copy-done.2, bf16[8,128,384]{2,1,0:T(8,128)(2,1)} %copy-done.1, bf16[8,128,384]{2,1,0:T(8,128)(2,1)} %copy-done.3, ...), custom_call_target="tpu_custom_call" | custom-call | flops 1342177280 | bytes 6291456 | tf_op jit(solution)/shard_map/pallas_call | solution.py:395
  113.1 4.5 %all-to-all-start.1 = ((bf16[16,40,2048]{2,1,0:T(8,128)(2,1)}), bf16[16,40,2048]{2,1,0:T(8,128)(2,1)S(1)}, u32[]{:S(2)}, u32[]{:S(2)}) async-start(bf16[16,40,2048]{2,1,0:T(8,128)(2,1)} %bitcast.12), calls=%async_computation.1 | async-start | bytes 5242880 | tf_op jit(solution)/shard_map/all_to_all | solution.py:262
  117.7 2.6 %collective-permute-start.7 = (bf16[8,384,128]{2,1,0:T(8,128)(2,1)}, bf16[8,384,128]{2,1,0:T(8,128)(2,1)S(1)}, u32[]{:S(2)}, u32[]{:S(2)}) collective-permute-start(bf16[8,384,128]{2,1,0:T(8,128)(2,1)} %get-tuple-element.14), channel_id=1, source_target_pairs={{0,16},{16,0},{32,48},{48,32},{64,80},{80,64},{96,112},{112,96},{1... | collective-permute-start | bytes 2359304 | tf_op jit(solution)/shard_map/ppermute | solution.py:277
  120.2 16.4 %collective-permute-start.9 = (bf16[7,384,128]{2,1,0:T(8,128)(2,1)}, bf16[7,384,128]{2,1,0:T(8,128)(2,1)S(1)}, u32[]{:S(2)}, u32[]{:S(2)}) collective-permute-start(bf16[7,384,128]{2,1,0:T(8,128)(2,1)} %add_convert_fusion), channel_id=1, source_target_pairs={{0,32},{16,496},{32,64},{48,16},{64,96},{80,48},{96,128},{112,80},... | collective-permute-start | bytes 2064392 | tf_op jit(solution)/shard_map/ppermute | solution.py:273
  136.6 0.0 collective-permute-done.7
  136.6 8.2 %collective-permute-done.9 = bf16[7,384,128]{2,1,0:T(8,128)(2,1)S(1)} collective-permute-done((bf16[7,384,128]{2,1,0:T(8,128)(2,1)}, bf16[7,384,128]{2,1,0:T(8,128)(2,1)S(1)}, u32[]{:S(2)}, u32[]{:S(2)}) %collective-permute-start.9) | collective-permute-done | bytes 688160 | tf_op jit(solution)/shard_map/ppermute | solution.py:273
  144.8 0.1 add_convert_fusion.1
  144.9 4.4 %collective-permute-start.10 = (bf16[4,384,128]{2,1,0:T(8,128)(2,1)S(1)}, bf16[4,384,128]{2,1,0:T(8,128)(2,1)S(1)}, u32[]{:S(2)}, u32[]{:S(2)}) collective-permute-start(bf16[4,384,128]{2,1,0:T(8,128)(2,1)S(1)} %add_convert_fusion.1), channel_id=1, source_target_pairs={{0,64},{16,464},{32,96},{48,496},{64,128},{80,16},{96,160},{112,48... | collective-permute-start | bytes 1179656 | tf_op jit(solution)/shard_map/ppermute | solution.py:273
  149.4 7.8 %collective-permute-done.10 = bf16[4,384,128]{2,1,0:T(8,128)(2,1)S(1)} collective-permute-done((bf16[4,384,128]{2,1,0:T(8,128)(2,1)S(1)}, bf16[4,384,128]{2,1,0:T(8,128)(2,1)S(1)}, u32[]{:S(2)}, u32[]{:S(2)}) %collective-permute-start.10) | collective-permute-done | bytes 393248 | tf_op jit(solution)/shard_map/ppermute | solution.py:273
  157.2 1.0 add_convert_fusion.2
  158.2 10.3 %collective-permute-start.11 = (bf16[2,384,128]{2,1,0:T(8,128)(2,1)}, bf16[2,384,128]{2,1,0:T(8,128)(2,1)S(1)}, u32[]{:S(2)}, u32[]{:S(2)}) collective-permute-start(bf16[2,384,128]{2,1,0:T(8,128)(2,1)} %get-tuple-element.27), channel_id=1, source_target_pairs={{0,160},{16,368},{32,192},{48,400},{64,224},{80,432},{96,256},{112... | collective-permute-start | bytes 589832 | tf_op jit(solution)/shard_map/ppermute | solution.py:273
  168.5 1.9 %collective-permute-start.12 = (bf16[2,384,128]{2,1,0:T(8,128)(2,1)}, bf16[2,384,128]{2,1,0:T(8,128)(2,1)S(1)}, u32[]{:S(2)}, u32[]{:S(2)}) collective-permute-start(bf16[2,384,128]{2,1,0:T(8,128)(2,1)} %get-tuple-element.26), channel_id=1, source_target_pairs={{0,32},{16,496},{32,64},{48,16},{64,96},{80,48},{96,128},{112,80},... | collective-permute-start | bytes 589832 | tf_op jit(solution)/shard_map/ppermute | solution.py:273
  170.4 1.8 shard_map.79.back_ref
  172.2 1.5 copy-done
  173.7 3.8 %shard_map.81 = bf16[128,4096]{1,0:T(8,128)(2,1)} custom-call(bf16[256,640]{1,0:T(8,128)(2,1)} %shard_map.79.back_ref, bf16[640,2048]{1,0:T(8,128)(2,1)} %bitcast.13), custom_call_target="tpu_custom_call" | custom-call | flops 671088640 | bytes 4194304 | tf_op jit(solution)/shard_map/pallas_call | solution.py:407
  177.5 0.9 collective-permute-done.11
  178.4 2.1 %collective-permute-done.12 = bf16[2,384,128]{2,1,0:T(8,128)(2,1)S(1)} collective-permute-done((bf16[2,384,128]{2,1,0:T(8,128)(2,1)}, bf16[2,384,128]{2,1,0:T(8,128)(2,1)S(1)}, u32[]{:S(2)}, u32[]{:S(2)}) %collective-permute-start.12) | collective-permute-done | bytes 196640 | tf_op jit(solution)/shard_map/ppermute | solution.py:273
  180.5 0.1 convert_add_fusion
  180.6 4.8 %collective-permute-start.13 = (bf16[1,384,128]{2,1,0:T(8,128)(2,1)S(1)}, bf16[1,384,128]{2,1,0:T(8,128)(2,1)S(1)}, u32[]{:S(2)}, u32[]{:S(2)}) collective-permute-start(bf16[1,384,128]{2,1,0:T(8,128)(2,1)S(1)} %slice.73), channel_id=1, source_target_pairs={{0,16},{16,0},{32,48},{48,32},{64,80},{80,64},{96,112},{112,96},{1... | collective-permute-start | bytes 294920 | tf_op jit(solution)/shard_map/ppermute | solution.py:277
  185.4 0.9 collective-permute-done.13
  186.3 0.8 copy.8
  (24 shorter events, 0.2 us)
Async XLA Ops:
  6.1 7.8 %copy-start.8 = (bf16[1,128,384]{2,1,0:T(8,128)(2,1)S(1)}, bf16[1,128,384]{2,1,0:T(8,128)(2,1)}, u32[]{:S(2)}) copy-start(bf16[1,128,384]{2,1,0:T(8,128)(2,1)} %param.10) | copy-start | bytes 294916
  6.1 77.5 %all-to-all-start = ((bf16[16,40,4096]{2,1,0:T(8,128)(2,1)}), bf16[16,40,4096]{2,1,0:T(8,128)(2,1)}, u32[]{:S(2)}, u32[]{:S(2)}) async-start(bf16[16,40,4096]{2,1,0:T(8,128)(2,1)} %bitcast.11), calls=%async_computation | async-start | bytes 10485760 | tf_op jit(solution)/shard_map/all_to_all | solution.py:262
  13.9 67.3 %copy-start.9 = (s32[1,1,32]{2,1,0:T(1,128)S(1)}, s32[1,1,32]{2,1,0:T(1,128)}, u32[]{:S(2)}) copy-start(s32[1,1,32]{2,1,0:T(1,128)} %param.11) | copy-start | bytes 388
  13.9 6.6 %collective-permute-start = (bf16[128,384]{1,0:T(8,128)(2,1)S(1)}, bf16[128,384]{1,0:T(8,128)(2,1)S(1)}, u32[]{:S(2)}, u32[]{:S(2)}) collective-permute-start(bf16[128,384]{1,0:T(8,128)(2,1)S(1)} %bitcast.14), channel_id=1, source_target_pairs={{0,16},{16,0},{32,48},{48,32},{64,80},{80,64},{96,112},{112,96},{1... | collective-permute-start | bytes 294920 | tf_op jit(solution)/shard_map/ppermute | solution.py:277
  20.6 63.0 %copy-start.2 = (bf16[2,128,384]{2,1,0:T(8,128)(2,1)}, bf16[2,128,384]{2,1,0:T(8,128)(2,1)S(1)}, u32[]{:S(2)}) copy-start(bf16[2,128,384]{2,1,0:T(8,128)(2,1)S(1)} %pad_maximum_fusion.1.refs_0_) | copy-start | bytes 589828
  20.6 10.9 %collective-permute-start.1 = (bf16[2,128,384]{2,1,0:T(8,128)(2,1)S(1)}, bf16[2,128,384]{2,1,0:T(8,128)(2,1)S(1)}, u32[]{:S(2)}, u32[]{:S(2)}) collective-permute-start(bf16[2,128,384]{2,1,0:T(8,128)(2,1)S(1)} %pad_maximum_fusion.1.refs_0_), channel_id=1, source_target_pairs={{0,32},{16,496},{32,64},{48,16},{64,96},{80,48},{96,128},{112,80},... | collective-permute-start | bytes 589832 | tf_op jit(solution)/shard_map/ppermute | solution.py:273
  31.5 12.3 %collective-permute-start.2 = (bf16[2,128,384]{2,1,0:T(8,128)(2,1)S(1)}, bf16[2,128,384]{2,1,0:T(8,128)(2,1)S(1)}, u32[]{:S(2)}, u32[]{:S(2)}) collective-permute-start(bf16[2,128,384]{2,1,0:T(8,128)(2,1)S(1)} %collective-permute-done.1), channel_id=1, source_target_pairs={{0,128},{16,400},{32,160},{48,432},{64,192},{80,464},{96,224},{112... | collective-permute-start | bytes 589832 | tf_op jit(solution)/shard_map/ppermute | solution.py:273
  43.8 16.6 %collective-permute-start.3 = (bf16[4,128,384]{2,1,0:T(8,128)(2,1)S(1)}, bf16[4,128,384]{2,1,0:T(8,128)(2,1)S(1)}, u32[]{:S(2)}, u32[]{:S(2)}) collective-permute-start(bf16[4,128,384]{2,1,0:T(8,128)(2,1)S(1)} %pad_maximum_fusion), channel_id=1, source_target_pairs={{0,64},{16,464},{32,96},{48,496},{64,128},{80,16},{96,160},{112,48... | collective-permute-start | bytes 1179656 | tf_op jit(solution)/shard_map/ppermute | solution.py:273
  60.5 23.2 %copy-start.1 = (bf16[8,128,384]{2,1,0:T(8,128)(2,1)}, bf16[8,128,384]{2,1,0:T(8,128)(2,1)S(1)}, u32[]{:S(2)}) copy-start(bf16[8,128,384]{2,1,0:T(8,128)(2,1)S(1)} %constant_dynamic-update-slice_fusion.refs_1_) | copy-start | bytes 2359300
  60.5 13.1 %collective-permute-start.4 = (bf16[8,128,384]{2,1,0:T(8,128)(2,1)S(1)}, bf16[8,128,384]{2,1,0:T(8,128)(2,1)S(1)}, u32[]{:S(2)}, u32[]{:S(2)}) collective-permute-start(bf16[8,128,384]{2,1,0:T(8,128)(2,1)S(1)} %constant_dynamic-update-slice_fusion.refs_1_), channel_id=1, source_target_pairs={{0,32},{16,496},{32,64},{48,16},{64,96},{80,48},{96,128},{112,80},... | collective-permute-start | bytes 2359304 | tf_op jit(solution)/shard_map/ppermute | solution.py:273
  62.5 19.4 %collective-permute-start.5 = (bf16[8,128,384]{2,1,0:T(8,128)(2,1)S(1)}, bf16[8,128,384]{2,1,0:T(8,128)(2,1)S(1)}, u32[]{:S(2)}, u32[]{:S(2)}) collective-permute-start(bf16[8,128,384]{2,1,0:T(8,128)(2,1)S(1)} %constant_dynamic-update-slice_fusion.refs_1_), channel_id=1, source_target_pairs={{0,16},{16,0},{32,48},{48,32},{64,80},{80,64},{96,112},{112,96},{1... | collective-permute-start | bytes 2359304 | tf_op jit(solution)/shard_map/ppermute | solution.py:277
  73.6 10.0 %copy-start.3 = (bf16[8,128,384]{2,1,0:T(8,128)(2,1)}, bf16[8,128,384]{2,1,0:T(8,128)(2,1)S(1)}, u32[]{:S(2)}) copy-start(bf16[8,128,384]{2,1,0:T(8,128)(2,1)S(1)} %collective-permute-done.4.refs_2_) | copy-start | bytes 2359300
  73.6 8.8 %collective-permute-start.6 = (bf16[8,128,384]{2,1,0:T(8,128)(2,1)S(1)}, bf16[8,128,384]{2,1,0:T(8,128)(2,1)S(1)}, u32[]{:S(2)}, u32[]{:S(2)}) collective-permute-start(bf16[8,128,384]{2,1,0:T(8,128)(2,1)S(1)} %collective-permute-done.4.refs_2_), channel_id=1, source_target_pairs={{0,16},{16,0},{32,48},{48,32},{64,80},{80,64},{96,112},{112,96},{1... | collective-permute-start | bytes 2359304 | tf_op jit(solution)/shard_map/ppermute | solution.py:277
  81.8 1.8 copy-start.4
  82.4 1.2 copy-start.5
  95.5 8.8 %collective-permute-start.8 = (bf16[7,384,128]{2,1,0:T(8,128)(2,1)}, bf16[7,384,128]{2,1,0:T(8,128)(2,1)S(1)}, u32[]{:S(2)}, u32[]{:S(2)}) collective-permute-start(bf16[7,384,128]{2,1,0:T(8,128)(2,1)} %get-tuple-element.16), channel_id=1, source_target_pairs={{0,16},{16,0},{32,48},{48,32},{64,80},{80,64},{96,112},{112,96},{1... | collective-permute-start | bytes 2064392 | tf_op jit(solution)/shard_map/ppermute | solution.py:277
  113.1 31.7 %copy-start.6 = (bf16[8,384,128]{2,1,0:T(8,128)(2,1)S(1)}, bf16[8,384,128]{2,1,0:T(8,128)(2,1)}, u32[]{:S(2)}) copy-start(bf16[8,384,128]{2,1,0:T(8,128)(2,1)} %get-tuple-element.13) | copy-start | bytes 2359300
  113.1 59.0 %all-to-all-start.1 = ((bf16[16,40,2048]{2,1,0:T(8,128)(2,1)}), bf16[16,40,2048]{2,1,0:T(8,128)(2,1)S(1)}, u32[]{:S(2)}, u32[]{:S(2)}) async-start(bf16[16,40,2048]{2,1,0:T(8,128)(2,1)} %bitcast.12), calls=%async_computation.1 | async-start | bytes 5242880 | tf_op jit(solution)/shard_map/all_to_all | solution.py:262
  117.7 19.0 %collective-permute-start.7 = (bf16[8,384,128]{2,1,0:T(8,128)(2,1)}, bf16[8,384,128]{2,1,0:T(8,128)(2,1)S(1)}, u32[]{:S(2)}, u32[]{:S(2)}) collective-permute-start(bf16[8,384,128]{2,1,0:T(8,128)(2,1)} %get-tuple-element.14), channel_id=1, source_target_pairs={{0,16},{16,0},{32,48},{48,32},{64,80},{80,64},{96,112},{112,96},{1... | collective-permute-start | bytes 2359304 | tf_op jit(solution)/shard_map/ppermute | solution.py:277
  120.2 24.6 %collective-permute-start.9 = (bf16[7,384,128]{2,1,0:T(8,128)(2,1)}, bf16[7,384,128]{2,1,0:T(8,128)(2,1)S(1)}, u32[]{:S(2)}, u32[]{:S(2)}) collective-permute-start(bf16[7,384,128]{2,1,0:T(8,128)(2,1)} %add_convert_fusion), channel_id=1, source_target_pairs={{0,32},{16,496},{32,64},{48,16},{64,96},{80,48},{96,128},{112,80},... | collective-permute-start | bytes 2064392 | tf_op jit(solution)/shard_map/ppermute | solution.py:273
  144.9 12.3 %collective-permute-start.10 = (bf16[4,384,128]{2,1,0:T(8,128)(2,1)S(1)}, bf16[4,384,128]{2,1,0:T(8,128)(2,1)S(1)}, u32[]{:S(2)}, u32[]{:S(2)}) collective-permute-start(bf16[4,384,128]{2,1,0:T(8,128)(2,1)S(1)} %add_convert_fusion.1), channel_id=1, source_target_pairs={{0,64},{16,464},{32,96},{48,496},{64,128},{80,16},{96,160},{112,48... | collective-permute-start | bytes 1179656 | tf_op jit(solution)/shard_map/ppermute | solution.py:273
  158.2 22.3 %copy-start.7 = (bf16[2,384,128]{2,1,0:T(8,128)(2,1)S(1)}, bf16[2,384,128]{2,1,0:T(8,128)(2,1)}, u32[]{:S(2)}) copy-start(bf16[2,384,128]{2,1,0:T(8,128)(2,1)} %get-tuple-element.21) | copy-start | bytes 589828
  158.2 20.2 %collective-permute-start.11 = (bf16[2,384,128]{2,1,0:T(8,128)(2,1)}, bf16[2,384,128]{2,1,0:T(8,128)(2,1)S(1)}, u32[]{:S(2)}, u32[]{:S(2)}) collective-permute-start(bf16[2,384,128]{2,1,0:T(8,128)(2,1)} %get-tuple-element.27), channel_id=1, source_target_pairs={{0,160},{16,368},{32,192},{48,400},{64,224},{80,432},{96,256},{112... | collective-permute-start | bytes 589832 | tf_op jit(solution)/shard_map/ppermute | solution.py:273
  168.5 12.1 %collective-permute-start.12 = (bf16[2,384,128]{2,1,0:T(8,128)(2,1)}, bf16[2,384,128]{2,1,0:T(8,128)(2,1)S(1)}, u32[]{:S(2)}, u32[]{:S(2)}) collective-permute-start(bf16[2,384,128]{2,1,0:T(8,128)(2,1)} %get-tuple-element.26), channel_id=1, source_target_pairs={{0,32},{16,496},{32,64},{48,16},{64,96},{80,48},{96,128},{112,80},... | collective-permute-start | bytes 589832 | tf_op jit(solution)/shard_map/ppermute | solution.py:273
  172.2 1.5 copy-start
  180.6 5.7 %collective-permute-start.13 = (bf16[1,384,128]{2,1,0:T(8,128)(2,1)S(1)}, bf16[1,384,128]{2,1,0:T(8,128)(2,1)S(1)}, u32[]{:S(2)}, u32[]{:S(2)}) collective-permute-start(bf16[1,384,128]{2,1,0:T(8,128)(2,1)S(1)} %slice.73), channel_id=1, source_target_pairs={{0,16},{16,0},{32,48},{48,32},{64,80},{80,64},{96,112},{112,96},{1... | collective-permute-start | bytes 294920 | tf_op jit(solution)/shard_map/ppermute | solution.py:277

commit v4 on v3

--- a/solution.py
+++ b/solution.py
@@ -15,6 +15,7 @@
 ROWS = 2 * EXPERTS * CAP
 STEPS = 1
 PARTS = 2
+GRAD_PARTS = 4
 COLS = HALF // STEPS
 BLOCKS = WIDTH // 128
 
@@ -101,9 +102,7 @@
     return own + other
 
 
-def stack_rows(table_ref, weights, step, h, start, stop):
-    count = COLS // 128
-    first = count * step + BLOCKS // 2 * h
+def stack_rows(table_ref, weights, first, count, start, stop):
     return jnp.concatenate(
         [weights[table_ref[first + j], :, start:stop] for j in range(count)], 0
     )
@@ -119,8 +118,8 @@
 
 
 def expert_kernel(table_ref, info_ref, recv_ref, *refs):
-    gathered, both_ref, pieces = refs[:5], refs[5], refs[6:11]
-    slots, weights, turned_ref, staged, sems, w_sems, out_sems = refs[11:]
+    gathered, slot_grad_ref, pieces = refs[:5], refs[5], refs[6:11]
+    slots, weights, turned_ref, staged, grads, sems, w_sems, out_sems, grad_sems = refs[11:]
     w_copies = piece_copies(gathered, weights, w_sems)
     for copy in w_copies:
         copy.start()
@@ -134,7 +133,11 @@
     halves[0].wait()
     x = slots[:, :HALF]
     gate_up = [
-        jnp.dot(x, stack_rows(table_ref, weights, 0, h, 0, 2 * HID), preferred_element_type=F32)
+        jnp.dot(
+            x,
+            stack_rows(table_ref, weights, BLOCKS // 2 * h, BLOCKS // 2, 0, 2 * HID),
+            preferred_element_type=F32,
+        )
         for h in range(2)
     ]
     joined = join_halves(*gate_up)
@@ -146,13 +149,18 @@
     hidden = silu_val * up_pre
     halves[1].wait()
     dy = slots[:, HALF:]
-    w_down = [stack_rows(table_ref, weights, 0, h, 2 * HID, 3 * HID) for h in range(2)]
+    w_down = [
+        stack_rows(table_ref, weights, BLOCKS // 2 * h, BLOCKS // 2, 2 * HID, 3 * HID)
+        for h in range(2)
+    ]
     down = jnp.dot(dy, jnp.concatenate(w_down, 1), preferred_element_type=F32)
     hid_grad = join_halves(down[:, :HID], down[:, HID:])
     gate_grad = hid_grad * up_pre * silu_slope
     up_grad = hid_grad * silu_val
-    both_ref[:, :HID] = gate_grad.astype(BF16)
-    both_ref[:, HID:] = up_grad.astype(BF16)
+    both = jnp.concatenate([gate_grad, up_grad], 1)
+    upper, _ = half_of_row(both.shape, 0)
+    both = jnp.concatenate([jnp.where(upper, 0.0, both), jnp.where(upper, both, 0.0)], 1)
+    both = both.astype(BF16)
     upper, _ = half_of_row((HID, ROWS), 1)
     for i, value in enumerate((gate_grad, up_grad, hidden)):
         turned = value.T
@@ -190,36 +198,28 @@
                     pl.when((place >= first) & (place < last))(
                         functools.partial(send, ref, first)
                     )
+    copies = []
+    for part in range(GRAD_PARTS):
+        count = BLOCKS // 2 // GRAD_PARTS
+        matching = [
+            stack_rows(table_ref, weights, count * part + BLOCKS // 2 * h, count, 0, 2 * HID)
+            for h in range(2)
+        ]
+        at = pl.ds(part * count * 128, count * 128)
+        grads[:, at] = lax.dot_general(
+            both,
+            jnp.concatenate(matching, 1),
+            (((1,), (1,)), ((), ())),
+            preferred_element_type=F32,
+        ).astype(BF16)
+        copies.append(
+            pltpu.make_async_copy(grads.at[:, at], slot_grad_ref.at[:, at], grad_sems.at[part])
+        )
+        copies[-1].start()
+    for copy in copies:
+        copy.wait()
     for block in range(BLOCKS):
         pltpu.make_async_copy(staged.at[block], pieces[0].at[0], out_sems.at[block]).wait()
-
-
-def slot_grad_kernel(table_ref, both_ref, *refs):
-    gathered, (out_ref, weights, w_sems) = refs[:5], refs[5:]
-    step = pl.program_id(0)
-
-    @pl.when(step == 0)
-    def _():
-        copies = piece_copies(gathered, weights, w_sems)
-        for copy in copies:
-            copy.start()
-        for copy in copies:
-            copy.wait()
-
-    both = both_ref[...]
-    upper, _ = half_of_row((ROWS, 2 * HID), 0)
-    zero = jnp.zeros_like(both)
-    total = None
-    for h in range(2):
-        own = jnp.where(upper, both, zero) if h else jnp.where(upper, zero, both)
-        part = lax.dot_general(
-            own,
-            stack_rows(table_ref, weights, step, h, 0, 2 * HID),
-            (((1,), (1,)), ((), ())),
-            preferred_element_type=F32,
-        )
-        total = part if total is None else total + part
-    out_ref[...] = total.astype(BF16)
 
 
 def combine_kernel(back_ref, slots_ref, out_ref):
@@ -370,39 +370,29 @@
     table = gathered_places(rep)
     info = jnp.concatenate([touched.reshape(-1), scattered_places(rep)])
     shares = [(n, 3 * HID, 128) for n in (7, 8, 2, 7, 8)]
-    both_grad, even, odd, here, give_even, give_odd = call(
+    slot_grad, even, odd, here, give_even, give_odd = call(
         expert_kernel,
         1,
         in_place * 6,
-        [whole((ROWS, 2 * HID))] + in_place * 5,
-        [sds((ROWS, 2 * HID), BF16)] + [sds(share, BF16) for share in shares],
-        2 * ROWS * HALF * 12 * HID,
+        in_place * 6,
+        [sds((ROWS, HALF), BF16)] + [sds(share, BF16) for share in shares],
+        2 * ROWS * HALF * 16 * HID,
         16 * mbytes,
         [
             pltpu.VMEM((ROWS, WIDTH), BF16),
             weights[0],
             pltpu.VMEM((6 * HID, ROWS), BF16),
             pltpu.VMEM((BLOCKS, 3 * HID, 128), BF16),
+            pltpu.VMEM((ROWS, HALF), BF16),
             pltpu.SemaphoreType.DMA((2,)),
             weights[1],
             pltpu.SemaphoreType.DMA((BLOCKS,)),
+            pltpu.SemaphoreType.DMA((GRAD_PARTS,)),
         ],
         2,
     )(table, info, received, *gathered)
     paired = (even.astype(F32) + swap(give_even).astype(F32)).astype(BF16)
-    paired, both_grad = lax.optimization_barrier((paired, both_grad))
     final = scatter_sum(paired, odd, give_odd)
-    slot_grad = call(
-        slot_grad_kernel,
-        STEPS,
-        [whole((ROWS, 2 * HID))] + in_place * 5,
-        columns(ROWS),
-        sds((ROWS, HALF), BF16),
-        2 * ROWS * HALF * 4 * HID,
-        6 * mbytes,
-        weights,
-        1,
-    )(table, both_grad, *gathered)
     returned = exchange(slot_grad)
     token_grad = call(
         combine_kernel,

time: 188 us -> 179 us (0.952)
  Pallas kernels: 29.6 us -> 24.1 us
  waiting for transfers between devices: 48.9 us -> 46.7 us
    pallas_call x2 -> x1, Pallas kernels: 18.6 us -> 13.1 us  [per_device(): call(expert_kernel, 1, in_place * 6, in_place * 6, [sds((ROWS, HALF), BF1...]
  transfers between devices with their start and end apart: 16 -> 16, of which waited for: 13 -> 12; matrix products, arithmetic and copies ran while one was open for 1% -> 2% of each run, Pallas kernels for 3% -> 3%
where the time goes in v4:
time: 179 us
  starting transfers between devices  100 us (56%)
  waiting for transfers between devices  46.7 us (26%)
  Pallas kernels  24.1 us (13%)
  other arithmetic  3.91 us (2%)
  local copies, waits for them, and re-layouts  2.5 us (1%)
    ppermute x8, starting transfers between devices, hop(): return lax.ppermute(value, 'rep', turn)  56.8 us
    ppermute x8, waiting for transfers between devices, hop(): return lax.ppermute(value, 'rep', turn)  42.9 us
    ppermute x6, starting transfers between devices, swap(): lax.ppermute(value, 'rep', [(i, i ^ 1) for i in range(lax.axis_size('rep'...  31.4 us
    pallas_call x1, Pallas kernels, per_device(): call(expert_kernel, 1, in_place * 6, in_place * 6, [sds((ROWS, HALF), BF1...  13.1 us
    all_to_all x2, starting transfers between devices, exchange(): lax.all_to_all(rows.reshape(EXPERTS, 2 * CAP, -1), 'exp', split_axis=0, c...  12.3 us
    pallas_call x1, Pallas kernels, per_device(): call(place_kernel, 2 * STEPS, [whole((2, TOK)), whole((2, TOK)), columns(...  5.5 us
    pallas_call x1, Pallas kernels, per_device(): call(combine_kernel, STEPS, [whole((2 * TOK, ROWS)), columns(ROWS)], whol...  3.81 us
  transfers between devices with their start and end apart: 16, of which 12 were waited for; matrix products, arithmetic and copies ran while one was open for 2% of the time, Pallas kernels for 3%

profile of v4, /device:TPU:1, one launch (start us, length us, event | category | flops | bytes accessed | tf_op | source)
XLA Modules:
  0.0 178.6 jit_solution(11026848567833526810)
XLA Ops:
  0.6 5.5 %shard_map.77 = bf16[640,4096]{1,0:T(8,128)(2,1)} custom-call(s32[2,128]{1,0:T(2,128)} %bitcast.16, f32[2,128]{1,0:T(2,128)} %bitcast.18, bf16[128,4096]{1,0:T(8,128)(2,1)} %x_high_ref.1, bf16[128,4096]{1,0:T(8,128)(2,1)} %x_high_ref.1, bf16[128,4096]{1,0:T(8,128)(2,1)} %dy_high_ref.1, bf16[128,4096]{1,0:T(8,128)(2,1)} %dy_high_ref.1), custom_call_target="tpu_custom_call" | custom-call | flops 1342177280 | bytes 8388608 | tf_op jit(solution)/shard_map/pallas_call | solution.py:337
  6.1 7.7 %all-to-all-start = ((bf16[16,40,4096]{2,1,0:T(8,128)(2,1)}), bf16[16,40,4096]{2,1,0:T(8,128)(2,1)}, u32[]{:S(2)}, u32[]{:S(2)}) async-start(bf16[16,40,4096]{2,1,0:T(8,128)(2,1)} %bitcast.11), calls=%async_computation | async-start | bytes 10485760 | tf_op jit(solution)/shard_map/all_to_all | solution.py:262
  13.9 0.0 copy-start.9
  13.9 5.7 %collective-permute-start = (bf16[128,384]{1,0:T(8,128)(2,1)S(1)}, bf16[128,384]{1,0:T(8,128)(2,1)S(1)}, u32[]{:S(2)}, u32[]{:S(2)}) collective-permute-start(bf16[128,384]{1,0:T(8,128)(2,1)S(1)} %bitcast.14), channel_id=1, source_target_pairs={{0,16},{16,0},{32,48},{48,32},{64,80},{80,64},{96,112},{112,96},{1... | collective-permute-start | bytes 294920 | tf_op jit(solution)/shard_map/ppermute | solution.py:277
  19.6 0.9 collective-permute-done
  20.6 0.0 copy-start.2
  20.6 8.3 %collective-permute-start.1 = (bf16[2,128,384]{2,1,0:T(8,128)(2,1)S(1)}, bf16[2,128,384]{2,1,0:T(8,128)(2,1)S(1)}, u32[]{:S(2)}, u32[]{:S(2)}) collective-permute-start(bf16[2,128,384]{2,1,0:T(8,128)(2,1)S(1)} %pad_maximum_fusion.1.refs_0_), channel_id=1, source_target_pairs={{0,32},{16,496},{32,64},{48,16},{64,96},{80,48},{96,128},{112,80},... | collective-permute-start | bytes 589832 | tf_op jit(solution)/shard_map/ppermute | solution.py:273
  28.9 2.6 %collective-permute-done.1 = bf16[2,128,384]{2,1,0:T(8,128)(2,1)S(1)} collective-permute-done((bf16[2,128,384]{2,1,0:T(8,128)(2,1)S(1)}, bf16[2,128,384]{2,1,0:T(8,128)(2,1)S(1)}, u32[]{:S(2)}, u32[]{:S(2)}) %collective-permute-start.1) | collective-permute-done | bytes 196640 | tf_op jit(solution)/shard_map/ppermute | solution.py:273
  31.5 5.5 %collective-permute-start.2 = (bf16[2,128,384]{2,1,0:T(8,128)(2,1)S(1)}, bf16[2,128,384]{2,1,0:T(8,128)(2,1)S(1)}, u32[]{:S(2)}, u32[]{:S(2)}) collective-permute-start(bf16[2,128,384]{2,1,0:T(8,128)(2,1)S(1)} %collective-permute-done.1), channel_id=1, source_target_pairs={{0,128},{16,400},{32,160},{48,432},{64,192},{80,464},{96,224},{112... | collective-permute-start | bytes 589832 | tf_op jit(solution)/shard_map/ppermute | solution.py:273
  37.0 6.8 %collective-permute-done.2 = bf16[2,128,384]{2,1,0:T(8,128)(2,1)S(1)} collective-permute-done((bf16[2,128,384]{2,1,0:T(8,128)(2,1)S(1)}, bf16[2,128,384]{2,1,0:T(8,128)(2,1)S(1)}, u32[]{:S(2)}, u32[]{:S(2)}) %collective-permute-start.2) | collective-permute-done | bytes 196640 | tf_op jit(solution)/shard_map/ppermute | solution.py:273
  43.8 7.8 %collective-permute-start.3 = (bf16[4,128,384]{2,1,0:T(8,128)(2,1)S(1)}, bf16[4,128,384]{2,1,0:T(8,128)(2,1)S(1)}, u32[]{:S(2)}, u32[]{:S(2)}) collective-permute-start(bf16[4,128,384]{2,1,0:T(8,128)(2,1)S(1)} %pad_maximum_fusion), channel_id=1, source_target_pairs={{0,64},{16,464},{32,96},{48,496},{64,128},{80,16},{96,160},{112,48... | collective-permute-start | bytes 1179656 | tf_op jit(solution)/shard_map/ppermute | solution.py:273
  51.7 8.7 %collective-permute-done.3 = bf16[4,128,384]{2,1,0:T(8,128)(2,1)S(1)} collective-permute-done((bf16[4,128,384]{2,1,0:T(8,128)(2,1)S(1)}, bf16[4,128,384]{2,1,0:T(8,128)(2,1)S(1)}, u32[]{:S(2)}, u32[]{:S(2)}) %collective-permute-start.3) | collective-permute-done | bytes 393248 | tf_op jit(solution)/shard_map/ppermute | solution.py:273
  60.4 0.1 constant_dynamic-update-slice_fusion.refs_1_
  60.5 0.0 copy-start.5
  60.5 2.0 %collective-permute-start.4 = (bf16[8,128,384]{2,1,0:T(8,128)(2,1)S(1)}, bf16[8,128,384]{2,1,0:T(8,128)(2,1)S(1)}, u32[]{:S(2)}, u32[]{:S(2)}) collective-permute-start(bf16[8,128,384]{2,1,0:T(8,128)(2,1)S(1)} %constant_dynamic-update-slice_fusion.refs_1_), channel_id=1, source_target_pairs={{0,32},{16,496},{32,64},{48,16},{64,96},{80,48},{96,128},{112,80},... | collective-permute-start | bytes 2359304 | tf_op jit(solution)/shard_map/ppermute | solution.py:273
  62.5 4.9 %collective-permute-start.5 = (bf16[8,128,384]{2,1,0:T(8,128)(2,1)S(1)}, bf16[8,128,384]{2,1,0:T(8,128)(2,1)S(1)}, u32[]{:S(2)}, u32[]{:S(2)}) collective-permute-start(bf16[8,128,384]{2,1,0:T(8,128)(2,1)S(1)} %constant_dynamic-update-slice_fusion.refs_1_), channel_id=1, source_target_pairs={{0,16},{16,0},{32,48},{48,32},{64,80},{80,64},{96,112},{112,96},{1... | collective-permute-start | bytes 2359304 | tf_op jit(solution)/shard_map/ppermute | solution.py:277
  67.4 6.2 %collective-permute-done.4.refs_2_ = bf16[8,128,384]{2,1,0:T(8,128)(2,1)S(1)} collective-permute-done((bf16[8,128,384]{2,1,0:T(8,128)(2,1)S(1)}, bf16[8,128,384]{2,1,0:T(8,128)(2,1)S(1)}, u32[]{:S(2)}, u32[]{:S(2)}) %collective-permute-start.4) | collective-permute-done | bytes 786464 | tf_op jit(solution)/shard_map/ppermute | solution.py:273
  73.6 6.9 %collective-permute-start.6 = (bf16[8,128,384]{2,1,0:T(8,128)(2,1)S(1)}, bf16[8,128,384]{2,1,0:T(8,128)(2,1)S(1)}, u32[]{:S(2)}, u32[]{:S(2)}) collective-permute-start(bf16[8,128,384]{2,1,0:T(8,128)(2,1)S(1)} %collective-permute-done.4.refs_2_), channel_id=1, source_target_pairs={{0,16},{16,0},{32,48},{48,32},{64,80},{80,64},{96,112},{112,96},{1... | collective-permute-start | bytes 2359304 | tf_op jit(solution)/shard_map/ppermute | solution.py:277
  80.6 0.6 compare_select_fusion.7.table_ref
  81.1 0.6 pad_add_fusion.info_ref
  81.7 0.0 collective-permute-done.5.refs_3_
  81.7 0.7 collective-permute-done.6.refs_4_
  82.4 1.2 all-to-all-done
  83.6 13.1 %shard_map.78 = (bf16[640,2048]{1,0:T(8,128)(2,1)}, bf16[7,384,128]{2,1,0:T(8,128)(2,1)}, bf16[8,384,128]{2,1,0:T(8,128)(2,1)}, bf16[2,384,128]{2,1,0:T(8,128)(2...) custom-call(s32[32]{0:T(128)} %compare_select_fusion.7.table_ref, s32[64]{0:T(128)} %pad_add_fusion.info_ref, ...), custom_call_target="tpu_custom_call" | custom-call | flops 5368709120 | bytes 16777216 | tf_op jit(solution)/shard_map/pallas_call | solution.py:373
  96.7 6.8 %collective-permute-start.8 = (bf16[7,384,128]{2,1,0:T(8,128)(2,1)}, bf16[7,384,128]{2,1,0:T(8,128)(2,1)}, u32[]{:S(2)}, u32[]{:S(2)}) collective-permute-start(bf16[7,384,128]{2,1,0:T(8,128)(2,1)} %get-tuple-element.14), channel_id=1, source_target_pairs={{0,16},{16,0},{32,48},{48,32},{64,80},{80,64},{96,112},{112,96},{1... | collective-permute-start | bytes 2064392 | tf_op jit(solution)/shard_map/ppermute | solution.py:277
  103.5 4.5 %all-to-all-start.1 = ((bf16[16,40,2048]{2,1,0:T(8,128)(2,1)}), bf16[16,40,2048]{2,1,0:T(8,128)(2,1)S(1)}, u32[]{:S(2)}, u32[]{:S(2)}) async-start(bf16[16,40,2048]{2,1,0:T(8,128)(2,1)} %bitcast.13), calls=%async_computation.1 | async-start | bytes 5242880 | tf_op jit(solution)/shard_map/all_to_all | solution.py:262
  108.0 2.2 %collective-permute-start.7 = (bf16[8,384,128]{2,1,0:T(8,128)(2,1)}, bf16[8,384,128]{2,1,0:T(8,128)(2,1)S(1)}, u32[]{:S(2)}, u32[]{:S(2)}) collective-permute-start(bf16[8,384,128]{2,1,0:T(8,128)(2,1)} %get-tuple-element.12), channel_id=1, source_target_pairs={{0,16},{16,0},{32,48},{48,32},{64,80},{80,64},{96,112},{112,96},{1... | collective-permute-start | bytes 2359304 | tf_op jit(solution)/shard_map/ppermute | solution.py:277
  110.2 0.0 collective-permute-done.8
  110.3 1.5 add_convert_fusion
  111.7 16.4 %collective-permute-start.9 = (bf16[7,384,128]{2,1,0:T(8,128)(2,1)S(1)}, bf16[7,384,128]{2,1,0:T(8,128)(2,1)S(1)}, u32[]{:S(2)}, u32[]{:S(2)}) collective-permute-start(bf16[7,384,128]{2,1,0:T(8,128)(2,1)S(1)} %add_convert_fusion), channel_id=1, source_target_pairs={{0,32},{16,496},{32,64},{48,16},{64,96},{80,48},{96,128},{112,80},... | collective-permute-start | bytes 2064392 | tf_op jit(solution)/shard_map/ppermute | solution.py:273
  128.2 0.0 collective-permute-done.7
  128.2 7.8 %collective-permute-done.9 = bf16[7,384,128]{2,1,0:T(8,128)(2,1)S(1)} collective-permute-done((bf16[7,384,128]{2,1,0:T(8,128)(2,1)S(1)}, bf16[7,384,128]{2,1,0:T(8,128)(2,1)S(1)}, u32[]{:S(2)}, u32[]{:S(2)}) %collective-permute-start.9) | collective-permute-done | bytes 688160 | tf_op jit(solution)/shard_map/ppermute | solution.py:273
  136.0 0.1 add_convert_fusion.1
  136.2 4.6 %collective-permute-start.10 = (bf16[4,384,128]{2,1,0:T(8,128)(2,1)S(1)}, bf16[4,384,128]{2,1,0:T(8,128)(2,1)S(1)}, u32[]{:S(2)}, u32[]{:S(2)}) collective-permute-start(bf16[4,384,128]{2,1,0:T(8,128)(2,1)S(1)} %add_convert_fusion.1), channel_id=1, source_target_pairs={{0,64},{16,464},{32,96},{48,496},{64,128},{80,16},{96,160},{112,48... | collective-permute-start | bytes 1179656 | tf_op jit(solution)/shard_map/ppermute | solution.py:273
  140.7 7.8 %collective-permute-done.10 = bf16[4,384,128]{2,1,0:T(8,128)(2,1)S(1)} collective-permute-done((bf16[4,384,128]{2,1,0:T(8,128)(2,1)S(1)}, bf16[4,384,128]{2,1,0:T(8,128)(2,1)S(1)}, u32[]{:S(2)}, u32[]{:S(2)}) %collective-permute-start.10) | collective-permute-done | bytes 393248 | tf_op jit(solution)/shard_map/ppermute | solution.py:273
  148.5 1.0 add_convert_fusion.2
  149.5 10.3 %collective-permute-start.11 = (bf16[2,384,128]{2,1,0:T(8,128)(2,1)}, bf16[2,384,128]{2,1,0:T(8,128)(2,1)S(1)}, u32[]{:S(2)}, u32[]{:S(2)}) collective-permute-start(bf16[2,384,128]{2,1,0:T(8,128)(2,1)} %get-tuple-element.23), channel_id=1, source_target_pairs={{0,160},{16,368},{32,192},{48,400},{64,224},{80,432},{96,256},{112... | collective-permute-start | bytes 589832 | tf_op jit(solution)/shard_map/ppermute | solution.py:273
  159.8 1.9 %collective-permute-start.12 = (bf16[2,384,128]{2,1,0:T(8,128)(2,1)}, bf16[2,384,128]{2,1,0:T(8,128)(2,1)S(1)}, u32[]{:S(2)}, u32[]{:S(2)}) collective-permute-start(bf16[2,384,128]{2,1,0:T(8,128)(2,1)} %get-tuple-element.22), channel_id=1, source_target_pairs={{0,32},{16,496},{32,64},{48,16},{64,96},{80,48},{96,128},{112,80},... | collective-permute-start | bytes 589832 | tf_op jit(solution)/shard_map/ppermute | solution.py:273
  161.7 1.8 shard_map.79.back_ref
  163.5 0.0 all-to-all-done.1
  163.5 1.5 copy-done
  165.0 3.8 %shard_map.80 = bf16[128,4096]{1,0:T(8,128)(2,1)} custom-call(bf16[256,640]{1,0:T(8,128)(2,1)} %shard_map.79.back_ref, bf16[640,2048]{1,0:T(8,128)(2,1)} %bitcast.12), custom_call_target="tpu_custom_call" | custom-call | flops 671088640 | bytes 4194304 | tf_op jit(solution)/shard_map/pallas_call | solution.py:397
  168.8 0.9 collective-permute-done.11
  169.8 2.1 %collective-permute-done.12 = bf16[2,384,128]{2,1,0:T(8,128)(2,1)S(1)} collective-permute-done((bf16[2,384,128]{2,1,0:T(8,128)(2,1)}, bf16[2,384,128]{2,1,0:T(8,128)(2,1)S(1)}, u32[]{:S(2)}, u32[]{:S(2)}) %collective-permute-start.12) | collective-permute-done | bytes 196640 | tf_op jit(solution)/shard_map/ppermute | solution.py:273
  171.9 0.1 convert_add_fusion
  171.9 4.9 %collective-permute-start.13 = (bf16[1,384,128]{2,1,0:T(8,128)(2,1)S(1)}, bf16[1,384,128]{2,1,0:T(8,128)(2,1)S(1)}, u32[]{:S(2)}, u32[]{:S(2)}) collective-permute-start(bf16[1,384,128]{2,1,0:T(8,128)(2,1)S(1)} %slice.73), channel_id=1, source_target_pairs={{0,16},{16,0},{32,48},{48,32},{64,80},{80,64},{96,112},{112,96},{1... | collective-permute-start | bytes 294920 | tf_op jit(solution)/shard_map/ppermute | solution.py:277
  176.8 0.9 collective-permute-done.13
  177.8 0.8 copy.8
  (23 shorter events, 0.2 us)
Async XLA Ops:
  6.1 7.8 %copy-start.4 = (bf16[1,128,384]{2,1,0:T(8,128)(2,1)S(1)}, bf16[1,128,384]{2,1,0:T(8,128)(2,1)}, u32[]{:S(2)}) copy-start(bf16[1,128,384]{2,1,0:T(8,128)(2,1)} %param.10) | copy-start | bytes 294916
  6.1 77.5 %all-to-all-start = ((bf16[16,40,4096]{2,1,0:T(8,128)(2,1)}), bf16[16,40,4096]{2,1,0:T(8,128)(2,1)}, u32[]{:S(2)}, u32[]{:S(2)}) async-start(bf16[16,40,4096]{2,1,0:T(8,128)(2,1)} %bitcast.11), calls=%async_computation | async-start | bytes 10485760 | tf_op jit(solution)/shard_map/all_to_all | solution.py:262
  13.9 67.2 %copy-start.9 = (s32[1,1,32]{2,1,0:T(1,128)S(1)}, s32[1,1,32]{2,1,0:T(1,128)}, u32[]{:S(2)}) copy-start(s32[1,1,32]{2,1,0:T(1,128)} %param.11) | copy-start | bytes 388
  13.9 6.6 %collective-permute-start = (bf16[128,384]{1,0:T(8,128)(2,1)S(1)}, bf16[128,384]{1,0:T(8,128)(2,1)S(1)}, u32[]{:S(2)}, u32[]{:S(2)}) collective-permute-start(bf16[128,384]{1,0:T(8,128)(2,1)S(1)} %bitcast.14), channel_id=1, source_target_pairs={{0,16},{16,0},{32,48},{48,32},{64,80},{80,64},{96,112},{112,96},{1... | collective-permute-start | bytes 294920 | tf_op jit(solution)/shard_map/ppermute | solution.py:277
  20.6 63.0 %copy-start.2 = (bf16[2,128,384]{2,1,0:T(8,128)(2,1)}, bf16[2,128,384]{2,1,0:T(8,128)(2,1)S(1)}, u32[]{:S(2)}) copy-start(bf16[2,128,384]{2,1,0:T(8,128)(2,1)S(1)} %pad_maximum_fusion.1.refs_0_) | copy-start | bytes 589828
  20.6 10.9 %collective-permute-start.1 = (bf16[2,128,384]{2,1,0:T(8,128)(2,1)S(1)}, bf16[2,128,384]{2,1,0:T(8,128)(2,1)S(1)}, u32[]{:S(2)}, u32[]{:S(2)}) collective-permute-start(bf16[2,128,384]{2,1,0:T(8,128)(2,1)S(1)} %pad_maximum_fusion.1.refs_0_), channel_id=1, source_target_pairs={{0,32},{16,496},{32,64},{48,16},{64,96},{80,48},{96,128},{112,80},... | collective-permute-start | bytes 589832 | tf_op jit(solution)/shard_map/ppermute | solution.py:273
  31.5 12.3 %collective-permute-start.2 = (bf16[2,128,384]{2,1,0:T(8,128)(2,1)S(1)}, bf16[2,128,384]{2,1,0:T(8,128)(2,1)S(1)}, u32[]{:S(2)}, u32[]{:S(2)}) collective-permute-start(bf16[2,128,384]{2,1,0:T(8,128)(2,1)S(1)} %collective-permute-done.1), channel_id=1, source_target_pairs={{0,128},{16,400},{32,160},{48,432},{64,192},{80,464},{96,224},{112... | collective-permute-start | bytes 589832 | tf_op jit(solution)/shard_map/ppermute | solution.py:273
  43.8 16.6 %collective-permute-start.3 = (bf16[4,128,384]{2,1,0:T(8,128)(2,1)S(1)}, bf16[4,128,384]{2,1,0:T(8,128)(2,1)S(1)}, u32[]{:S(2)}, u32[]{:S(2)}) collective-permute-start(bf16[4,128,384]{2,1,0:T(8,128)(2,1)S(1)} %pad_maximum_fusion), channel_id=1, source_target_pairs={{0,64},{16,464},{32,96},{48,496},{64,128},{80,16},{96,160},{112,48... | collective-permute-start | bytes 1179656 | tf_op jit(solution)/shard_map/ppermute | solution.py:273
  60.5 23.2 %copy-start.5 = (bf16[8,128,384]{2,1,0:T(8,128)(2,1)}, bf16[8,128,384]{2,1,0:T(8,128)(2,1)S(1)}, u32[]{:S(2)}) copy-start(bf16[8,128,384]{2,1,0:T(8,128)(2,1)S(1)} %constant_dynamic-update-slice_fusion.refs_1_) | copy-start | bytes 2359300
  60.5 13.1 %collective-permute-start.4 = (bf16[8,128,384]{2,1,0:T(8,128)(2,1)S(1)}, bf16[8,128,384]{2,1,0:T(8,128)(2,1)S(1)}, u32[]{:S(2)}, u32[]{:S(2)}) collective-permute-start(bf16[8,128,384]{2,1,0:T(8,128)(2,1)S(1)} %constant_dynamic-update-slice_fusion.refs_1_), channel_id=1, source_target_pairs={{0,32},{16,496},{32,64},{48,16},{64,96},{80,48},{96,128},{112,80},... | collective-permute-start | bytes 2359304 | tf_op jit(solution)/shard_map/ppermute | solution.py:273
  62.5 19.2 %collective-permute-start.5 = (bf16[8,128,384]{2,1,0:T(8,128)(2,1)S(1)}, bf16[8,128,384]{2,1,0:T(8,128)(2,1)S(1)}, u32[]{:S(2)}, u32[]{:S(2)}) collective-permute-start(bf16[8,128,384]{2,1,0:T(8,128)(2,1)S(1)} %constant_dynamic-update-slice_fusion.refs_1_), channel_id=1, source_target_pairs={{0,16},{16,0},{32,48},{48,32},{64,80},{80,64},{96,112},{112,96},{1... | collective-permute-start | bytes 2359304 | tf_op jit(solution)/shard_map/ppermute | solution.py:277
  73.6 10.0 %copy-start.6 = (bf16[8,128,384]{2,1,0:T(8,128)(2,1)}, bf16[8,128,384]{2,1,0:T(8,128)(2,1)S(1)}, u32[]{:S(2)}) copy-start(bf16[8,128,384]{2,1,0:T(8,128)(2,1)S(1)} %collective-permute-done.4.refs_2_) | copy-start | bytes 2359300
  73.6 8.8 %collective-permute-start.6 = (bf16[8,128,384]{2,1,0:T(8,128)(2,1)S(1)}, bf16[8,128,384]{2,1,0:T(8,128)(2,1)S(1)}, u32[]{:S(2)}, u32[]{:S(2)}) collective-permute-start(bf16[8,128,384]{2,1,0:T(8,128)(2,1)S(1)} %collective-permute-done.4.refs_2_), channel_id=1, source_target_pairs={{0,16},{16,0},{32,48},{48,32},{64,80},{80,64},{96,112},{112,96},{1... | collective-permute-start | bytes 2359304 | tf_op jit(solution)/shard_map/ppermute | solution.py:277
  81.7 1.9 %copy-start.7 = (bf16[8,128,384]{2,1,0:T(8,128)(2,1)}, bf16[8,128,384]{2,1,0:T(8,128)(2,1)S(1)}, u32[]{:S(2)}) copy-start(bf16[8,128,384]{2,1,0:T(8,128)(2,1)S(1)} %collective-permute-done.5.refs_3_) | copy-start | bytes 2359300
  82.4 1.2 copy-start.8
  96.7 13.5 %collective-permute-start.8 = (bf16[7,384,128]{2,1,0:T(8,128)(2,1)}, bf16[7,384,128]{2,1,0:T(8,128)(2,1)}, u32[]{:S(2)}, u32[]{:S(2)}) collective-permute-start(bf16[7,384,128]{2,1,0:T(8,128)(2,1)} %get-tuple-element.14), channel_id=1, source_target_pairs={{0,16},{16,0},{32,48},{48,32},{64,80},{80,64},{96,112},{112,96},{1... | collective-permute-start | bytes 2064392 | tf_op jit(solution)/shard_map/ppermute | solution.py:277
  103.5 32.5 %copy-start.1 = (bf16[8,384,128]{2,1,0:T(8,128)(2,1)S(1)}, bf16[8,384,128]{2,1,0:T(8,128)(2,1)}, u32[]{:S(2)}) copy-start(bf16[8,384,128]{2,1,0:T(8,128)(2,1)} %get-tuple-element.11) | copy-start | bytes 2359300
  103.5 60.0 %all-to-all-start.1 = ((bf16[16,40,2048]{2,1,0:T(8,128)(2,1)}), bf16[16,40,2048]{2,1,0:T(8,128)(2,1)S(1)}, u32[]{:S(2)}, u32[]{:S(2)}) async-start(bf16[16,40,2048]{2,1,0:T(8,128)(2,1)} %bitcast.13), calls=%async_computation.1 | async-start | bytes 5242880 | tf_op jit(solution)/shard_map/all_to_all | solution.py:262
  108.0 20.1 %collective-permute-start.7 = (bf16[8,384,128]{2,1,0:T(8,128)(2,1)}, bf16[8,384,128]{2,1,0:T(8,128)(2,1)S(1)}, u32[]{:S(2)}, u32[]{:S(2)}) collective-permute-start(bf16[8,384,128]{2,1,0:T(8,128)(2,1)} %get-tuple-element.12), channel_id=1, source_target_pairs={{0,16},{16,0},{32,48},{48,32},{64,80},{80,64},{96,112},{112,96},{1... | collective-permute-start | bytes 2359304 | tf_op jit(solution)/shard_map/ppermute | solution.py:277
  111.7 24.3 %collective-permute-start.9 = (bf16[7,384,128]{2,1,0:T(8,128)(2,1)S(1)}, bf16[7,384,128]{2,1,0:T(8,128)(2,1)S(1)}, u32[]{:S(2)}, u32[]{:S(2)}) collective-permute-start(bf16[7,384,128]{2,1,0:T(8,128)(2,1)S(1)} %add_convert_fusion), channel_id=1, source_target_pairs={{0,32},{16,496},{32,64},{48,16},{64,96},{80,48},{96,128},{112,80},... | collective-permute-start | bytes 2064392 | tf_op jit(solution)/shard_map/ppermute | solution.py:273
  136.2 12.4 %collective-permute-start.10 = (bf16[4,384,128]{2,1,0:T(8,128)(2,1)S(1)}, bf16[4,384,128]{2,1,0:T(8,128)(2,1)S(1)}, u32[]{:S(2)}, u32[]{:S(2)}) collective-permute-start(bf16[4,384,128]{2,1,0:T(8,128)(2,1)S(1)} %add_convert_fusion.1), channel_id=1, source_target_pairs={{0,64},{16,464},{32,96},{48,496},{64,128},{80,16},{96,160},{112,48... | collective-permute-start | bytes 1179656 | tf_op jit(solution)/shard_map/ppermute | solution.py:273
  149.5 22.4 %copy-start.3 = (bf16[2,384,128]{2,1,0:T(8,128)(2,1)S(1)}, bf16[2,384,128]{2,1,0:T(8,128)(2,1)}, u32[]{:S(2)}) copy-start(bf16[2,384,128]{2,1,0:T(8,128)(2,1)} %get-tuple-element.17) | copy-start | bytes 589828
  149.5 20.3 %collective-permute-start.11 = (bf16[2,384,128]{2,1,0:T(8,128)(2,1)}, bf16[2,384,128]{2,1,0:T(8,128)(2,1)S(1)}, u32[]{:S(2)}, u32[]{:S(2)}) collective-permute-start(bf16[2,384,128]{2,1,0:T(8,128)(2,1)} %get-tuple-element.23), channel_id=1, source_target_pairs={{0,160},{16,368},{32,192},{48,400},{64,224},{80,432},{96,256},{112... | collective-permute-start | bytes 589832 | tf_op jit(solution)/shard_map/ppermute | solution.py:273
  159.8 12.1 %collective-permute-start.12 = (bf16[2,384,128]{2,1,0:T(8,128)(2,1)}, bf16[2,384,128]{2,1,0:T(8,128)(2,1)S(1)}, u32[]{:S(2)}, u32[]{:S(2)}) collective-permute-start(bf16[2,384,128]{2,1,0:T(8,128)(2,1)} %get-tuple-element.22), channel_id=1, source_target_pairs={{0,32},{16,496},{32,64},{48,16},{64,96},{80,48},{96,128},{112,80},... | collective-permute-start | bytes 589832 | tf_op jit(solution)/shard_map/ppermute | solution.py:273
  163.5 1.5 copy-start
  171.9 5.8 %collective-permute-start.13 = (bf16[1,384,128]{2,1,0:T(8,128)(2,1)S(1)}, bf16[1,384,128]{2,1,0:T(8,128)(2,1)S(1)}, u32[]{:S(2)}, u32[]{:S(2)}) collective-permute-start(bf16[1,384,128]{2,1,0:T(8,128)(2,1)S(1)} %slice.73), channel_id=1, source_target_pairs={{0,16},{16,0},{32,48},{48,32},{64,80},{80,64},{96,112},{112,96},{1... | collective-permute-start | bytes 294920 | tf_op jit(solution)/shard_map/ppermute | solution.py:277

commit v5 on v4

--- a/solution.py
+++ b/solution.py
@@ -13,8 +13,9 @@
 TOK, WIDTH, EXPERTS, CAP, HID = 128, 4096, 16, 20, 128
 HALF = WIDTH // 2
 ROWS = 2 * EXPERTS * CAP
-STEPS = 1
+STEPS = 2
 PARTS = 2
+PLACE_PARTS = 4
 GRAD_PARTS = 4
 COLS = HALF // STEPS
 BLOCKS = WIDTH // 128
@@ -59,36 +60,48 @@
 
 
 def place_kernel(
-    ids_ref, gates_ref, x_low_ref, x_high_ref, dy_low_ref, dy_high_ref, out_ref, place, gate
+    ids_ref, gates_ref, x_ref, dy_ref, out_ref, x, dy, staged, in_sems, out_sems
 ):
-    step = pl.program_id(0)
-
-    @pl.when(step == 0)
-    def _():
-        place[...] = placement(*hits(ids_ref[...])).astype(BF16)
-
-    @pl.when(step < STEPS)
-    def _():
-        both = jnp.concatenate([x_low_ref[...], x_high_ref[...]], 0)
-        out_ref[...] = jnp.dot(place[...], both, preferred_element_type=F32).astype(BF16)
-
-    @pl.when(step == STEPS)
-    def _():
-        hit0, hit1, _ = hits(ids_ref[...])
-        gates = gates_ref[...]
-        weight = jnp.where(hit0, jnp.broadcast_to(gates[0:1, :], (ROWS, TOK)), 0.0) + jnp.where(
-            hit1, jnp.broadcast_to(gates[1:2, :], (ROWS, TOK)), 0.0
-        )
-        gate[...] = jnp.broadcast_to(jnp.sum(weight, 1, keepdims=True), (ROWS, 128))
-
-    @pl.when(step >= STEPS)
-    def _():
-        both = jnp.concatenate([dy_low_ref[...], dy_high_ref[...]], 0)
-        picked = jnp.dot(place[...], both, preferred_element_type=F32)
-        scale = gate[...]
-        for i in range(COLS // 128):
-            part = picked[:, i * 128 : i * 128 + 128] * scale
-            out_ref[:, i * 128 : i * 128 + 128] = part.astype(BF16)
+    arrivals = [
+        pltpu.make_async_copy(x_ref, x, in_sems.at[0]),
+        pltpu.make_async_copy(dy_ref, dy, in_sems.at[1]),
+    ]
+    for copy in arrivals:
+        copy.start()
+    hit0, hit1, upper = hits(ids_ref[...])
+    place = placement(hit0, hit1, upper).astype(BF16)
+    departures = []
+
+    def put(source, at, scale):
+        width = HALF // PLACE_PARTS
+        for part in range(PLACE_PARTS):
+            low = source[:, part * width : (part + 1) * width]
+            high = source[:, HALF + part * width : HALF + (part + 1) * width]
+            rows = jnp.dot(
+                place, jnp.concatenate([low, high], 0), preferred_element_type=F32
+            )
+            if scale is not None:
+                rows = rows * scale
+            lanes = pl.ds(at + part * width, width)
+            staged[:, lanes] = rows.astype(BF16)
+            departures.append(
+                pltpu.make_async_copy(
+                    staged.at[:, lanes], out_ref.at[:, lanes], out_sems.at[len(departures)]
+                )
+            )
+            departures[-1].start()
+
+    arrivals[0].wait()
+    put(x, 0, None)
+    gates = gates_ref[...]
+    weight = jnp.where(hit0, jnp.broadcast_to(gates[0:1, :], (ROWS, TOK)), 0.0) + jnp.where(
+        hit1, jnp.broadcast_to(gates[1:2, :], (ROWS, TOK)), 0.0
+    )
+    scale = jnp.sum(weight, 1, keepdims=True)
+    arrivals[1].wait()
+    put(dy, HALF, scale)
+    for copy in departures:
+        copy.wait()
 
 
 def back_kernel(ids_ref, back_ref):
@@ -332,25 +345,23 @@
     rep = lax.axis_index("rep")
     ids = expert_ids.T
     mbytes = 1 << 20
-    early = lambda i: jnp.minimum(i, STEPS - 1)
-    late = lambda i: jnp.maximum(i - STEPS, 0)
+    in_place = [pl.BlockSpec(memory_space=pl.ANY)]
     sent = call(
         place_kernel,
-        2 * STEPS,
-        [
-            whole((2, TOK)),
-            whole((2, TOK)),
-            columns(TOK, early),
-            columns(TOK, lambda i: early(i) + STEPS),
-            columns(TOK, late),
-            columns(TOK, lambda i: late(i) + STEPS),
-        ],
-        columns(ROWS),
+        1,
+        [whole((2, TOK)), whole((2, TOK))] + in_place * 2,
+        in_place[0],
         sds((ROWS, WIDTH), BF16),
         4 * ROWS * 256 * HALF,
         8 * mbytes,
-        [pltpu.VMEM((ROWS, 2 * TOK), BF16), pltpu.VMEM((ROWS, 128), F32)],
-    )(ids, gates.T, tokens, tokens, grad_out, grad_out)
+        [
+            pltpu.VMEM((TOK, WIDTH), BF16),
+            pltpu.VMEM((TOK, WIDTH), BF16),
+            pltpu.VMEM((ROWS, WIDTH), BF16),
+            pltpu.SemaphoreType.DMA((2,)),
+            pltpu.SemaphoreType.DMA((2 * PLACE_PARTS,)),
+        ],
+    )(ids, gates.T, tokens, grad_out)
     received = exchange(sent)
     back = call(
         back_kernel,
@@ -362,7 +373,6 @@
         mbytes,
     )(ids)
     gathered = gather_weights(w_all[0])
-    in_place = [pl.BlockSpec(memory_space=pl.ANY)]
     weights = [
         pltpu.VMEM((sum(piece.shape[0] for piece in gathered), 128, 3 * HID), BF16),
         pltpu.SemaphoreType.DMA((len(gathered),)),

time: 179 us -> 179 us (level)
  no operation moved by 1% of the time
where the time goes in v5:
time: 179 us; the launch traced here: 178 us
  starting transfers between devices  100 us (56%)
  waiting for transfers between devices  47 us (26%)
  Pallas kernels  23.1 us (13%)
  other arithmetic  3.91 us (2%)
  local copies, waits for them, and re-layouts  2.5 us (1%)
    ppermute x8, starting transfers between devices, hop(): return lax.ppermute(value, 'rep', turn)  56.8 us
    ppermute x8, waiting for transfers between devices, hop(): return lax.ppermute(value, 'rep', turn)  43.2 us
    ppermute x6, starting transfers between devices, swap(): lax.ppermute(value, 'rep', [(i, i ^ 1) for i in range(lax.axis_size('rep'...  31.4 us
    pallas_call x1, Pallas kernels, per_device(): call(expert_kernel, 1, in_place * 6, in_place * 6, [sds((ROWS, HALF), BF1...  13.1 us
    all_to_all x2, starting transfers between devices, exchange(): lax.all_to_all(rows.reshape(EXPERTS, 2 * CAP, -1), 'exp', split_axis=0, c...  12.3 us
    pallas_call x1, Pallas kernels, per_device(): call(place_kernel, 1, [whole((2, TOK)), whole((2, TOK))] + in_place * 2,...  4.76 us
  transfers between devices with their start and end apart: 16, of which 12 were waited for; matrix products, arithmetic and copies ran while one was open for 2% of the time, Pallas kernels for 3%

profile of v5, /device:TPU:1, one launch (start us, length us, event | category | flops | bytes accessed | tf_op | source)
XLA Modules:
  0.0 177.9 jit_solution(12790938153891182199)
XLA Ops:
  0.6 4.8 %shard_map.77 = bf16[640,4096]{1,0:T(8,128)(2,1)} custom-call(s32[2,128]{1,0:T(2,128)} %bitcast.16, f32[2,128]{1,0:T(2,128)} %bitcast.18, bf16[128,4096]{1,0:T(8,128)(2,1)} %x_ref.1, bf16[128,4096]{1,0:T(8,128)(2,1)} %dy_ref.1), custom_call_target="tpu_custom_call" | custom-call | flops 1342177280 | bytes 8388608 | tf_op jit(solution)/shard_map/pallas_call | solution.py:349
  5.4 0.0 copy-start.4
  5.4 7.8 %all-to-all-start = ((bf16[16,40,4096]{2,1,0:T(8,128)(2,1)}), bf16[16,40,4096]{2,1,0:T(8,128)(2,1)}, u32[]{:S(2)}, u32[]{:S(2)}) async-start(bf16[16,40,4096]{2,1,0:T(8,128)(2,1)} %bitcast.11), calls=%async_computation | async-start | bytes 10485760 | tf_op jit(solution)/shard_map/all_to_all | solution.py:275
  13.2 0.0 copy-start.9
  13.2 5.7 %collective-permute-start = (bf16[128,384]{1,0:T(8,128)(2,1)S(1)}, bf16[128,384]{1,0:T(8,128)(2,1)S(1)}, u32[]{:S(2)}, u32[]{:S(2)}) collective-permute-start(bf16[128,384]{1,0:T(8,128)(2,1)S(1)} %bitcast.14), channel_id=1, source_target_pairs={{0,16},{16,0},{32,48},{48,32},{64,80},{80,64},{96,112},{112,96},{1... | collective-permute-start | bytes 294920 | tf_op jit(solution)/shard_map/ppermute | solution.py:290
  18.9 0.9 collective-permute-done
  19.9 0.0 copy-start.2
  19.9 8.3 %collective-permute-start.1 = (bf16[2,128,384]{2,1,0:T(8,128)(2,1)S(1)}, bf16[2,128,384]{2,1,0:T(8,128)(2,1)S(1)}, u32[]{:S(2)}, u32[]{:S(2)}) collective-permute-start(bf16[2,128,384]{2,1,0:T(8,128)(2,1)S(1)} %pad_maximum_fusion.1.refs_0_), channel_id=1, source_target_pairs={{0,32},{16,496},{32,64},{48,16},{64,96},{80,48},{96,128},{112,80},... | collective-permute-start | bytes 589832 | tf_op jit(solution)/shard_map/ppermute | solution.py:286
  28.2 2.6 %collective-permute-done.1 = bf16[2,128,384]{2,1,0:T(8,128)(2,1)S(1)} collective-permute-done((bf16[2,128,384]{2,1,0:T(8,128)(2,1)S(1)}, bf16[2,128,384]{2,1,0:T(8,128)(2,1)S(1)}, u32[]{:S(2)}, u32[]{:S(2)}) %collective-permute-start.1) | collective-permute-done | bytes 196640 | tf_op jit(solution)/shard_map/ppermute | solution.py:286
  30.8 5.5 %collective-permute-start.2 = (bf16[2,128,384]{2,1,0:T(8,128)(2,1)S(1)}, bf16[2,128,384]{2,1,0:T(8,128)(2,1)S(1)}, u32[]{:S(2)}, u32[]{:S(2)}) collective-permute-start(bf16[2,128,384]{2,1,0:T(8,128)(2,1)S(1)} %collective-permute-done.1), channel_id=1, source_target_pairs={{0,128},{16,400},{32,160},{48,432},{64,192},{80,464},{96,224},{112... | collective-permute-start | bytes 589832 | tf_op jit(solution)/shard_map/ppermute | solution.py:286
  36.3 6.8 %collective-permute-done.2 = bf16[2,128,384]{2,1,0:T(8,128)(2,1)S(1)} collective-permute-done((bf16[2,128,384]{2,1,0:T(8,128)(2,1)S(1)}, bf16[2,128,384]{2,1,0:T(8,128)(2,1)S(1)}, u32[]{:S(2)}, u32[]{:S(2)}) %collective-permute-start.2) | collective-permute-done | bytes 196640 | tf_op jit(solution)/shard_map/ppermute | solution.py:286
  43.1 7.8 %collective-permute-start.3 = (bf16[4,128,384]{2,1,0:T(8,128)(2,1)S(1)}, bf16[4,128,384]{2,1,0:T(8,128)(2,1)S(1)}, u32[]{:S(2)}, u32[]{:S(2)}) collective-permute-start(bf16[4,128,384]{2,1,0:T(8,128)(2,1)S(1)} %pad_maximum_fusion), channel_id=1, source_target_pairs={{0,64},{16,464},{32,96},{48,496},{64,128},{80,16},{96,160},{112,48... | collective-permute-start | bytes 1179656 | tf_op jit(solution)/shard_map/ppermute | solution.py:286
  51.0 8.7 %collective-permute-done.3 = bf16[4,128,384]{2,1,0:T(8,128)(2,1)S(1)} collective-permute-done((bf16[4,128,384]{2,1,0:T(8,128)(2,1)S(1)}, bf16[4,128,384]{2,1,0:T(8,128)(2,1)S(1)}, u32[]{:S(2)}, u32[]{:S(2)}) %collective-permute-start.3) | collective-permute-done | bytes 393248 | tf_op jit(solution)/shard_map/ppermute | solution.py:286
  59.7 0.1 constant_dynamic-update-slice_fusion.refs_1_
  59.7 0.0 copy-start.5
  59.8 2.0 %collective-permute-start.4 = (bf16[8,128,384]{2,1,0:T(8,128)(2,1)S(1)}, bf16[8,128,384]{2,1,0:T(8,128)(2,1)S(1)}, u32[]{:S(2)}, u32[]{:S(2)}) collective-permute-start(bf16[8,128,384]{2,1,0:T(8,128)(2,1)S(1)} %constant_dynamic-update-slice_fusion.refs_1_), channel_id=1, source_target_pairs={{0,32},{16,496},{32,64},{48,16},{64,96},{80,48},{96,128},{112,80},... | collective-permute-start | bytes 2359304 | tf_op jit(solution)/shard_map/ppermute | solution.py:286
  61.8 4.9 %collective-permute-start.5 = (bf16[8,128,384]{2,1,0:T(8,128)(2,1)S(1)}, bf16[8,128,384]{2,1,0:T(8,128)(2,1)S(1)}, u32[]{:S(2)}, u32[]{:S(2)}) collective-permute-start(bf16[8,128,384]{2,1,0:T(8,128)(2,1)S(1)} %constant_dynamic-update-slice_fusion.refs_1_), channel_id=1, source_target_pairs={{0,16},{16,0},{32,48},{48,32},{64,80},{80,64},{96,112},{112,96},{1... | collective-permute-start | bytes 2359304 | tf_op jit(solution)/shard_map/ppermute | solution.py:290
  66.7 6.2 %collective-permute-done.4.refs_2_ = bf16[8,128,384]{2,1,0:T(8,128)(2,1)S(1)} collective-permute-done((bf16[8,128,384]{2,1,0:T(8,128)(2,1)S(1)}, bf16[8,128,384]{2,1,0:T(8,128)(2,1)S(1)}, u32[]{:S(2)}, u32[]{:S(2)}) %collective-permute-start.4) | collective-permute-done | bytes 786464 | tf_op jit(solution)/shard_map/ppermute | solution.py:286
  72.9 6.9 %collective-permute-start.6 = (bf16[8,128,384]{2,1,0:T(8,128)(2,1)S(1)}, bf16[8,128,384]{2,1,0:T(8,128)(2,1)S(1)}, u32[]{:S(2)}, u32[]{:S(2)}) collective-permute-start(bf16[8,128,384]{2,1,0:T(8,128)(2,1)S(1)} %collective-permute-done.4.refs_2_), channel_id=1, source_target_pairs={{0,16},{16,0},{32,48},{48,32},{64,80},{80,64},{96,112},{112,96},{1... | collective-permute-start | bytes 2359304 | tf_op jit(solution)/shard_map/ppermute | solution.py:290
  79.9 0.6 compare_select_fusion.7.table_ref
  80.4 0.6 pad_add_fusion.info_ref
  81.0 0.0 collective-permute-done.5.refs_3_
  81.0 0.7 collective-permute-done.6.refs_4_
  81.7 1.2 all-to-all-done
  82.9 13.1 %shard_map.78 = (bf16[640,2048]{1,0:T(8,128)(2,1)}, bf16[7,384,128]{2,1,0:T(8,128)(2,1)}, bf16[8,384,128]{2,1,0:T(8,128)(2,1)}, bf16[2,384,128]{2,1,0:T(8,128)(2...) custom-call(s32[32]{0:T(128)} %compare_select_fusion.7.table_ref, s32[64]{0:T(128)} %pad_add_fusion.info_ref, ...), custom_call_target="tpu_custom_call" | custom-call | flops 5368709120 | bytes 16777216 | tf_op jit(solution)/shard_map/pallas_call | solution.py:383
  96.0 6.8 %collective-permute-start.8 = (bf16[7,384,128]{2,1,0:T(8,128)(2,1)}, bf16[7,384,128]{2,1,0:T(8,128)(2,1)}, u32[]{:S(2)}, u32[]{:S(2)}) collective-permute-start(bf16[7,384,128]{2,1,0:T(8,128)(2,1)} %get-tuple-element.14), channel_id=1, source_target_pairs={{0,16},{16,0},{32,48},{48,32},{64,80},{80,64},{96,112},{112,96},{1... | collective-permute-start | bytes 2064392 | tf_op jit(solution)/shard_map/ppermute | solution.py:290
  102.8 4.5 %all-to-all-start.1 = ((bf16[16,40,2048]{2,1,0:T(8,128)(2,1)}), bf16[16,40,2048]{2,1,0:T(8,128)(2,1)S(1)}, u32[]{:S(2)}, u32[]{:S(2)}) async-start(bf16[16,40,2048]{2,1,0:T(8,128)(2,1)} %bitcast.13), calls=%async_computation.1 | async-start | bytes 5242880 | tf_op jit(solution)/shard_map/all_to_all | solution.py:275
  107.3 2.2 %collective-permute-start.7 = (bf16[8,384,128]{2,1,0:T(8,128)(2,1)}, bf16[8,384,128]{2,1,0:T(8,128)(2,1)S(1)}, u32[]{:S(2)}, u32[]{:S(2)}) collective-permute-start(bf16[8,384,128]{2,1,0:T(8,128)(2,1)} %get-tuple-element.12), channel_id=1, source_target_pairs={{0,16},{16,0},{32,48},{48,32},{64,80},{80,64},{96,112},{112,96},{1... | collective-permute-start | bytes 2359304 | tf_op jit(solution)/shard_map/ppermute | solution.py:290
  109.5 0.0 collective-permute-done.8
  109.5 1.5 add_convert_fusion
  111.0 16.4 %collective-permute-start.9 = (bf16[7,384,128]{2,1,0:T(8,128)(2,1)S(1)}, bf16[7,384,128]{2,1,0:T(8,128)(2,1)S(1)}, u32[]{:S(2)}, u32[]{:S(2)}) collective-permute-start(bf16[7,384,128]{2,1,0:T(8,128)(2,1)S(1)} %add_convert_fusion), channel_id=1, source_target_pairs={{0,32},{16,496},{32,64},{48,16},{64,96},{80,48},{96,128},{112,80},... | collective-permute-start | bytes 2064392 | tf_op jit(solution)/shard_map/ppermute | solution.py:286
  127.4 0.0 collective-permute-done.7
  127.5 7.8 %collective-permute-done.9 = bf16[7,384,128]{2,1,0:T(8,128)(2,1)S(1)} collective-permute-done((bf16[7,384,128]{2,1,0:T(8,128)(2,1)S(1)}, bf16[7,384,128]{2,1,0:T(8,128)(2,1)S(1)}, u32[]{:S(2)}, u32[]{:S(2)}) %collective-permute-start.9) | collective-permute-done | bytes 688160 | tf_op jit(solution)/shard_map/ppermute | solution.py:286
  135.3 0.1 add_convert_fusion.1
  135.5 4.6 %collective-permute-start.10 = (bf16[4,384,128]{2,1,0:T(8,128)(2,1)S(1)}, bf16[4,384,128]{2,1,0:T(8,128)(2,1)S(1)}, u32[]{:S(2)}, u32[]{:S(2)}) collective-permute-start(bf16[4,384,128]{2,1,0:T(8,128)(2,1)S(1)} %add_convert_fusion.1), channel_id=1, source_target_pairs={{0,64},{16,464},{32,96},{48,496},{64,128},{80,16},{96,160},{112,48... | collective-permute-start | bytes 1179656 | tf_op jit(solution)/shard_map/ppermute | solution.py:286
  140.0 7.8 %collective-permute-done.10 = bf16[4,384,128]{2,1,0:T(8,128)(2,1)S(1)} collective-permute-done((bf16[4,384,128]{2,1,0:T(8,128)(2,1)S(1)}, bf16[4,384,128]{2,1,0:T(8,128)(2,1)S(1)}, u32[]{:S(2)}, u32[]{:S(2)}) %collective-permute-start.10) | collective-permute-done | bytes 393248 | tf_op jit(solution)/shard_map/ppermute | solution.py:286
  147.8 1.0 add_convert_fusion.2
  148.8 10.3 %collective-permute-start.11 = (bf16[2,384,128]{2,1,0:T(8,128)(2,1)}, bf16[2,384,128]{2,1,0:T(8,128)(2,1)S(1)}, u32[]{:S(2)}, u32[]{:S(2)}) collective-permute-start(bf16[2,384,128]{2,1,0:T(8,128)(2,1)} %get-tuple-element.23), channel_id=1, source_target_pairs={{0,160},{16,368},{32,192},{48,400},{64,224},{80,432},{96,256},{112... | collective-permute-start | bytes 589832 | tf_op jit(solution)/shard_map/ppermute | solution.py:286
  159.1 1.9 %collective-permute-start.12 = (bf16[2,384,128]{2,1,0:T(8,128)(2,1)}, bf16[2,384,128]{2,1,0:T(8,128)(2,1)S(1)}, u32[]{:S(2)}, u32[]{:S(2)}) collective-permute-start(bf16[2,384,128]{2,1,0:T(8,128)(2,1)} %get-tuple-element.22), channel_id=1, source_target_pairs={{0,32},{16,496},{32,64},{48,16},{64,96},{80,48},{96,128},{112,80},... | collective-permute-start | bytes 589832 | tf_op jit(solution)/shard_map/ppermute | solution.py:286
  161.0 1.8 shard_map.79.back_ref
  162.8 1.5 copy-done
  164.3 3.5 %shard_map.80 = bf16[128,4096]{1,0:T(8,128)(2,1)} custom-call(bf16[256,640]{1,0:T(8,128)(2,1)} %shard_map.79.back_ref, bf16[640,2048]{1,0:T(8,128)(2,1)} %bitcast.12), custom_call_target="tpu_custom_call" | custom-call | flops 671088640 | bytes 4194304 | tf_op jit(solution)/shard_map/pallas_call | solution.py:407
  167.8 1.2 collective-permute-done.11
  169.0 2.1 %collective-permute-done.12 = bf16[2,384,128]{2,1,0:T(8,128)(2,1)S(1)} collective-permute-done((bf16[2,384,128]{2,1,0:T(8,128)(2,1)}, bf16[2,384,128]{2,1,0:T(8,128)(2,1)S(1)}, u32[]{:S(2)}, u32[]{:S(2)}) %collective-permute-start.12) | collective-permute-done | bytes 196640 | tf_op jit(solution)/shard_map/ppermute | solution.py:286
  171.1 0.1 convert_add_fusion
  171.2 4.9 %collective-permute-start.13 = (bf16[1,384,128]{2,1,0:T(8,128)(2,1)S(1)}, bf16[1,384,128]{2,1,0:T(8,128)(2,1)S(1)}, u32[]{:S(2)}, u32[]{:S(2)}) collective-permute-start(bf16[1,384,128]{2,1,0:T(8,128)(2,1)S(1)} %slice.73), channel_id=1, source_target_pairs={{0,16},{16,0},{32,48},{48,32},{64,80},{80,64},{96,112},{112,96},{1... | collective-permute-start | bytes 294920 | tf_op jit(solution)/shard_map/ppermute | solution.py:290
  176.1 0.9 collective-permute-done.13
  177.1 0.8 copy.8
  (23 shorter events, 0.2 us)
Async XLA Ops:
  5.4 7.8 %copy-start.4 = (bf16[1,128,384]{2,1,0:T(8,128)(2,1)S(1)}, bf16[1,128,384]{2,1,0:T(8,128)(2,1)}, u32[]{:S(2)}) copy-start(bf16[1,128,384]{2,1,0:T(8,128)(2,1)} %param.10) | copy-start | bytes 294916
  5.4 77.5 %all-to-all-start = ((bf16[16,40,4096]{2,1,0:T(8,128)(2,1)}), bf16[16,40,4096]{2,1,0:T(8,128)(2,1)}, u32[]{:S(2)}, u32[]{:S(2)}) async-start(bf16[16,40,4096]{2,1,0:T(8,128)(2,1)} %bitcast.11), calls=%async_computation | async-start | bytes 10485760 | tf_op jit(solution)/shard_map/all_to_all | solution.py:275
  13.2 67.2 %copy-start.9 = (s32[1,1,32]{2,1,0:T(1,128)S(1)}, s32[1,1,32]{2,1,0:T(1,128)}, u32[]{:S(2)}) copy-start(s32[1,1,32]{2,1,0:T(1,128)} %param.11) | copy-start | bytes 388
  13.2 6.6 %collective-permute-start = (bf16[128,384]{1,0:T(8,128)(2,1)S(1)}, bf16[128,384]{1,0:T(8,128)(2,1)S(1)}, u32[]{:S(2)}, u32[]{:S(2)}) collective-permute-start(bf16[128,384]{1,0:T(8,128)(2,1)S(1)} %bitcast.14), channel_id=1, source_target_pairs={{0,16},{16,0},{32,48},{48,32},{64,80},{80,64},{96,112},{112,96},{1... | collective-permute-start | bytes 294920 | tf_op jit(solution)/shard_map/ppermute | solution.py:290
  19.9 63.0 %copy-start.2 = (bf16[2,128,384]{2,1,0:T(8,128)(2,1)}, bf16[2,128,384]{2,1,0:T(8,128)(2,1)S(1)}, u32[]{:S(2)}) copy-start(bf16[2,128,384]{2,1,0:T(8,128)(2,1)S(1)} %pad_maximum_fusion.1.refs_0_) | copy-start | bytes 589828
  19.9 10.9 %collective-permute-start.1 = (bf16[2,128,384]{2,1,0:T(8,128)(2,1)S(1)}, bf16[2,128,384]{2,1,0:T(8,128)(2,1)S(1)}, u32[]{:S(2)}, u32[]{:S(2)}) collective-permute-start(bf16[2,128,384]{2,1,0:T(8,128)(2,1)S(1)} %pad_maximum_fusion.1.refs_0_), channel_id=1, source_target_pairs={{0,32},{16,496},{32,64},{48,16},{64,96},{80,48},{96,128},{112,80},... | collective-permute-start | bytes 589832 | tf_op jit(solution)/shard_map/ppermute | solution.py:286
  30.8 12.3 %collective-permute-start.2 = (bf16[2,128,384]{2,1,0:T(8,128)(2,1)S(1)}, bf16[2,128,384]{2,1,0:T(8,128)(2,1)S(1)}, u32[]{:S(2)}, u32[]{:S(2)}) collective-permute-start(bf16[2,128,384]{2,1,0:T(8,128)(2,1)S(1)} %collective-permute-done.1), channel_id=1, source_target_pairs={{0,128},{16,400},{32,160},{48,432},{64,192},{80,464},{96,224},{112... | collective-permute-start | bytes 589832 | tf_op jit(solution)/shard_map/ppermute | solution.py:286
  43.1 16.6 %collective-permute-start.3 = (bf16[4,128,384]{2,1,0:T(8,128)(2,1)S(1)}, bf16[4,128,384]{2,1,0:T(8,128)(2,1)S(1)}, u32[]{:S(2)}, u32[]{:S(2)}) collective-permute-start(bf16[4,128,384]{2,1,0:T(8,128)(2,1)S(1)} %pad_maximum_fusion), channel_id=1, source_target_pairs={{0,64},{16,464},{32,96},{48,496},{64,128},{80,16},{96,160},{112,48... | collective-permute-start | bytes 1179656 | tf_op jit(solution)/shard_map/ppermute | solution.py:286
  59.7 23.2 %copy-start.5 = (bf16[8,128,384]{2,1,0:T(8,128)(2,1)}, bf16[8,128,384]{2,1,0:T(8,128)(2,1)S(1)}, u32[]{:S(2)}) copy-start(bf16[8,128,384]{2,1,0:T(8,128)(2,1)S(1)} %constant_dynamic-update-slice_fusion.refs_1_) | copy-start | bytes 2359300
  59.8 13.1 %collective-permute-start.4 = (bf16[8,128,384]{2,1,0:T(8,128)(2,1)S(1)}, bf16[8,128,384]{2,1,0:T(8,128)(2,1)S(1)}, u32[]{:S(2)}, u32[]{:S(2)}) collective-permute-start(bf16[8,128,384]{2,1,0:T(8,128)(2,1)S(1)} %constant_dynamic-update-slice_fusion.refs_1_), channel_id=1, source_target_pairs={{0,32},{16,496},{32,64},{48,16},{64,96},{80,48},{96,128},{112,80},... | collective-permute-start | bytes 2359304 | tf_op jit(solution)/shard_map/ppermute | solution.py:286
  61.8 19.2 %collective-permute-start.5 = (bf16[8,128,384]{2,1,0:T(8,128)(2,1)S(1)}, bf16[8,128,384]{2,1,0:T(8,128)(2,1)S(1)}, u32[]{:S(2)}, u32[]{:S(2)}) collective-permute-start(bf16[8,128,384]{2,1,0:T(8,128)(2,1)S(1)} %constant_dynamic-update-slice_fusion.refs_1_), channel_id=1, source_target_pairs={{0,16},{16,0},{32,48},{48,32},{64,80},{80,64},{96,112},{112,96},{1... | collective-permute-start | bytes 2359304 | tf_op jit(solution)/shard_map/ppermute | solution.py:290
  72.9 10.0 %copy-start.6 = (bf16[8,128,384]{2,1,0:T(8,128)(2,1)}, bf16[8,128,384]{2,1,0:T(8,128)(2,1)S(1)}, u32[]{:S(2)}) copy-start(bf16[8,128,384]{2,1,0:T(8,128)(2,1)S(1)} %collective-permute-done.4.refs_2_) | copy-start | bytes 2359300
  72.9 8.8 %collective-permute-start.6 = (bf16[8,128,384]{2,1,0:T(8,128)(2,1)S(1)}, bf16[8,128,384]{2,1,0:T(8,128)(2,1)S(1)}, u32[]{:S(2)}, u32[]{:S(2)}) collective-permute-start(bf16[8,128,384]{2,1,0:T(8,128)(2,1)S(1)} %collective-permute-done.4.refs_2_), channel_id=1, source_target_pairs={{0,16},{16,0},{32,48},{48,32},{64,80},{80,64},{96,112},{112,96},{1... | collective-permute-start | bytes 2359304 | tf_op jit(solution)/shard_map/ppermute | solution.py:290
  81.0 1.9 %copy-start.7 = (bf16[8,128,384]{2,1,0:T(8,128)(2,1)}, bf16[8,128,384]{2,1,0:T(8,128)(2,1)S(1)}, u32[]{:S(2)}) copy-start(bf16[8,128,384]{2,1,0:T(8,128)(2,1)S(1)} %collective-permute-done.5.refs_3_) | copy-start | bytes 2359300
  81.7 1.2 copy-start.8
  96.0 13.5 %collective-permute-start.8 = (bf16[7,384,128]{2,1,0:T(8,128)(2,1)}, bf16[7,384,128]{2,1,0:T(8,128)(2,1)}, u32[]{:S(2)}, u32[]{:S(2)}) collective-permute-start(bf16[7,384,128]{2,1,0:T(8,128)(2,1)} %get-tuple-element.14), channel_id=1, source_target_pairs={{0,16},{16,0},{32,48},{48,32},{64,80},{80,64},{96,112},{112,96},{1... | collective-permute-start | bytes 2064392 | tf_op jit(solution)/shard_map/ppermute | solution.py:290
  102.8 32.5 %copy-start.1 = (bf16[8,384,128]{2,1,0:T(8,128)(2,1)S(1)}, bf16[8,384,128]{2,1,0:T(8,128)(2,1)}, u32[]{:S(2)}) copy-start(bf16[8,384,128]{2,1,0:T(8,128)(2,1)} %get-tuple-element.11) | copy-start | bytes 2359300
  102.8 60.0 %all-to-all-start.1 = ((bf16[16,40,2048]{2,1,0:T(8,128)(2,1)}), bf16[16,40,2048]{2,1,0:T(8,128)(2,1)S(1)}, u32[]{:S(2)}, u32[]{:S(2)}) async-start(bf16[16,40,2048]{2,1,0:T(8,128)(2,1)} %bitcast.13), calls=%async_computation.1 | async-start | bytes 5242880 | tf_op jit(solution)/shard_map/all_to_all | solution.py:275
  107.3 20.1 %collective-permute-start.7 = (bf16[8,384,128]{2,1,0:T(8,128)(2,1)}, bf16[8,384,128]{2,1,0:T(8,128)(2,1)S(1)}, u32[]{:S(2)}, u32[]{:S(2)}) collective-permute-start(bf16[8,384,128]{2,1,0:T(8,128)(2,1)} %get-tuple-element.12), channel_id=1, source_target_pairs={{0,16},{16,0},{32,48},{48,32},{64,80},{80,64},{96,112},{112,96},{1... | collective-permute-start | bytes 2359304 | tf_op jit(solution)/shard_map/ppermute | solution.py:290
  111.0 24.3 %collective-permute-start.9 = (bf16[7,384,128]{2,1,0:T(8,128)(2,1)S(1)}, bf16[7,384,128]{2,1,0:T(8,128)(2,1)S(1)}, u32[]{:S(2)}, u32[]{:S(2)}) collective-permute-start(bf16[7,384,128]{2,1,0:T(8,128)(2,1)S(1)} %add_convert_fusion), channel_id=1, source_target_pairs={{0,32},{16,496},{32,64},{48,16},{64,96},{80,48},{96,128},{112,80},... | collective-permute-start | bytes 2064392 | tf_op jit(solution)/shard_map/ppermute | solution.py:286
  135.5 12.4 %collective-permute-start.10 = (bf16[4,384,128]{2,1,0:T(8,128)(2,1)S(1)}, bf16[4,384,128]{2,1,0:T(8,128)(2,1)S(1)}, u32[]{:S(2)}, u32[]{:S(2)}) collective-permute-start(bf16[4,384,128]{2,1,0:T(8,128)(2,1)S(1)} %add_convert_fusion.1), channel_id=1, source_target_pairs={{0,64},{16,464},{32,96},{48,496},{64,128},{80,16},{96,160},{112,48... | collective-permute-start | bytes 1179656 | tf_op jit(solution)/shard_map/ppermute | solution.py:286
  148.8 22.4 %copy-start.3 = (bf16[2,384,128]{2,1,0:T(8,128)(2,1)S(1)}, bf16[2,384,128]{2,1,0:T(8,128)(2,1)}, u32[]{:S(2)}) copy-start(bf16[2,384,128]{2,1,0:T(8,128)(2,1)} %get-tuple-element.17) | copy-start | bytes 589828
  148.8 20.3 %collective-permute-start.11 = (bf16[2,384,128]{2,1,0:T(8,128)(2,1)}, bf16[2,384,128]{2,1,0:T(8,128)(2,1)S(1)}, u32[]{:S(2)}, u32[]{:S(2)}) collective-permute-start(bf16[2,384,128]{2,1,0:T(8,128)(2,1)} %get-tuple-element.23), channel_id=1, source_target_pairs={{0,160},{16,368},{32,192},{48,400},{64,224},{80,432},{96,256},{112... | collective-permute-start | bytes 589832 | tf_op jit(solution)/shard_map/ppermute | solution.py:286
  159.1 12.1 %collective-permute-start.12 = (bf16[2,384,128]{2,1,0:T(8,128)(2,1)}, bf16[2,384,128]{2,1,0:T(8,128)(2,1)S(1)}, u32[]{:S(2)}, u32[]{:S(2)}) collective-permute-start(bf16[2,384,128]{2,1,0:T(8,128)(2,1)} %get-tuple-element.22), channel_id=1, source_target_pairs={{0,32},{16,496},{32,64},{48,16},{64,96},{80,48},{96,128},{112,80},... | collective-permute-start | bytes 589832 | tf_op jit(solution)/shard_map/ppermute | solution.py:286
  162.8 1.5 copy-start
  171.2 5.8 %collective-permute-start.13 = (bf16[1,384,128]{2,1,0:T(8,128)(2,1)S(1)}, bf16[1,384,128]{2,1,0:T(8,128)(2,1)S(1)}, u32[]{:S(2)}, u32[]{:S(2)}) collective-permute-start(bf16[1,384,128]{2,1,0:T(8,128)(2,1)S(1)} %slice.73), channel_id=1, source_target_pairs={{0,16},{16,0},{32,48},{48,32},{64,80},{80,64},{96,112},{112,96},{1... | collective-permute-start | bytes 294920 | tf_op jit(solution)/shard_map/ppermute | solution.py:290
